TPU v7x, 32 devices: a whole 2x2x4 slice. The times are simulated.
32 devices in a mesh: grp: 4 (over y, x), gx: 2 (over core), gy: 4 (over z).
Axes of the slice: x: 2, y: 2, z: 4, core: 2. Of those that a mesh axis runs over, the one named last changes fastest.
Arguments:
- pressure: float32 [4, 8, 64, 128], P('grp', 'gx', 'gy'), may hold values from -6 to 6
- source: float32 [4, 8, 64, 128], P('grp', 'gx', 'gy'), may hold values from -6 to 6
- storage: float32 [4, 8, 64, 128], P('grp', 'gx', 'gy'), may hold values from 0.05 to 2
- well_mask: int32 [4, 8, 64, 128], P('grp', 'gx', 'gy'), may hold values 0 or 1
- block_id: int32 [4, 8, 64, 128], P('grp', 'gx', 'gy'), may hold values from 0 to 63
- basis_weight: float32 [4, 8, 8, 64, 128], P('grp', None, 'gx', 'gy'), may hold values from 0 to 1
- host_elem: int32 [4, 8, 64, 128], P('grp', 'gx', 'gy'), may hold values from 0 to 8191
- displacement: float32 [4, 3, 8, 64, 128], P('grp', None, 'gx', 'gy'), may hold values from -4 to 4
- body_force: float32 [4, 3, 8, 64, 128], P('grp', None, 'gx', 'gy'), may hold values from -6 to 6
- modulus: float32 [4, 8, 64, 128], P('grp', 'gx', 'gy'), may hold values from 0.5 to 4
- elem_mask: int32 [4, 8, 64, 128], P('grp', 'gx', 'gy'), may hold values 0 or 1
- stiffness: float32 [24, 24], replicated, as said below
Outputs:
- pressure_out: float32 [4, 8, 64, 128], P('grp', 'gx', 'gy')
- displacement_out: float32 [4, 3, 8, 64, 128], P('grp', None, 'gx', 'gy')
Inputs may be any that keep to these rules, and one draw needn't show every extreme that they name: stiffness is symmetric and each diagonal entry exceeds the sum of the magnitudes of the other entries in its row by one.
All inputs are finite; a program needn't handle non-finite values. No bound on the sum of `well_mask` or of `elem_mask` on one device may be relied on, other than what follows from the above.
Results may differ from a plain program's by a relative error of at most 0.0003.
Values sent between devices are 32-bit elements; how exact they have to be, the bound alone decides.
No kernel may reach another device: no remote copies, remote signals or barrier semaphores. Data moves between devices by JAX's collectives and lax.ppermute only.
A program may use at most 64 MiB of HBM per device.

v0:
```python
import jax
import jax.numpy as jnp
from jax import lax
from jax.sharding import PartitionSpec as P

NBLK = 64
SWEEPS = 2
ITERS = 2


biot_coef = 1.5
relaxation = 0.8
spring_coef = 0.5
well_index = 4.0
highest = lax.Precision.HIGHEST


def passed_along(value, axis, steps):
    count = lax.axis_size(axis)
    leading, last = (max(0, -steps), min(count, count - steps))
    return lax.ppermute(value, axis, [(source, source + steps) for source in range(leading, last)])


def broadcast(value, axis, source):
    kept = jnp.where(lax.axis_index(axis) == source, value, 0).astype(value.dtype)
    return lax.psum(kept, axis)


def extended_2(cells, sides, width):
    for axis, dim in sides:
        count = lax.axis_size(axis)
        ends = count - 1
        head = lax.slice_in_dim(cells, 0, width, axis=dim)
        tail = lax.slice_in_dim(cells, cells.shape[dim] - width, cells.shape[dim], axis=dim)
        cells = jnp.concatenate(
            [
                lax.ppermute(tail, axis, [(i, (i + 1) % count) for i in range(ends)]),
                cells,
                lax.ppermute(head, axis, [((i + 1) % count, i) for i in range(ends)]),
            ],
            axis=dim,
        )
    return cells


def coupling_vector():
    index = jnp.arange(24, dtype=jnp.int32)
    corner = index // 3
    component = index % 3
    bitval = corner >> 2 - component & 1
    return (bitval.astype(jnp.float32) * 2.0 - 1.0) * 0.25


def corner_list():
    return [(corner >> 2 & 1, corner >> 1 & 1, corner & 1) for corner in range(8)]


def spread(nodes):
    size_x, size_y, size_z = nodes.shape[1:]
    right = passed_along(nodes[:, :1], "gx", -1)
    extended = jnp.concatenate([nodes, right], 1)
    upper = passed_along(extended[:, :, :1], "gy", -1)
    extended = jnp.concatenate([extended, upper], 2)
    extended = jnp.pad(extended, ((0, 0), (0, 0), (0, 0), (0, 1)))
    pieces = [
        extended[
            :, shift_x : shift_x + size_x, shift_y : shift_y + size_y, shift_z : shift_z + size_z
        ]
        for shift_x, shift_y, shift_z in corner_list()
    ]
    return jnp.stack(pieces).reshape(24, size_x * size_y * size_z)


def assemble(values, shape):
    size_x, size_y, size_z = shape
    parts = values.reshape(8, 3, size_x, size_y, size_z)
    total = jnp.zeros((3, size_x + 1, size_y + 1, size_z + 1), jnp.float32)
    for corner, (shift_x, shift_y, shift_z) in enumerate(corner_list()):
        total = total + jnp.pad(
            parts[corner],
            ((0, 0), (shift_x, 1 - shift_x), (shift_y, 1 - shift_y), (shift_z, 1 - shift_z)),
        )
    total = total[:, :, :, :size_z]
    moved = passed_along(total[:, size_x:], "gx", 1)
    inner = total[:, :size_x]
    inner = jnp.concatenate([inner[:, :1] + moved, inner[:, 1:]], 1)
    moved = passed_along(inner[:, :, size_y:], "gy", 1)
    inner = inner[:, :, :size_y]
    return jnp.concatenate([inner[:, :, :1] + moved, inner[:, :, 1:]], 2)


def squares(remain):
    return lax.psum(jnp.sum(remain * remain), ("gx", "gy"))


def local(
    pressure,
    source,
    storage,
    well_mask,
    block_id,
    basis_weight,
    host_elem,
    displacement,
    body_force,
    modulus,
    elem_mask,
    stiffness,
):
    groups = lax.axis_size("grp")
    group_index = lax.axis_index("grp")
    is_mech = group_index == groups - 1
    is_top = group_index == groups - 2
    flow_keep = jnp.where(is_mech, 0.0, 1.0).astype(jnp.float32)
    top_keep = jnp.where(is_top, 0.0, 1.0).astype(jnp.float32)
    start = pressure[0]
    shape = start.shape
    elements = shape[0] * shape[1] * shape[2]
    coupling = coupling_vector()
    mech_mask = elem_mask[0].astype(jnp.float32).reshape(-1)
    weights = modulus[0].reshape(-1) * mech_mask

    def apply(vector):
        return (
            assemble(
                jnp.dot(stiffness, spread(vector), precision=highest) * weights[None, :], shape
            )
            + spring_coef * vector
        )

    initial = displacement[0]
    strain = mech_mask * jnp.dot(coupling, spread(initial), precision=highest)
    strain = broadcast(strain, "grp", groups - 1)
    hosts = host_elem[0].reshape(-1)
    strain_cells = jnp.take(strain, hosts).reshape(shape)
    diagonal = 6.0 + storage[0] + well_index * well_mask[0].astype(jnp.float32)
    forcing = source[0] - biot_coef * strain_cells

    def neighbours(field):
        padded = extended_2(field, (("grp", 2), ("gx", 0), ("gy", 1)), 1)
        padded = jnp.concatenate([padded[:, :, :-1], padded[:, :, -1:] * top_keep], 2)
        total = padded[2:, 1:-1, 1:-1] + padded[:-2, 1:-1, 1:-1]
        total = total + padded[1:-1, 2:, 1:-1] + padded[1:-1, :-2, 1:-1]
        return total + padded[1:-1, 1:-1, 2:] + padded[1:-1, 1:-1, :-2]

    def residual(field):
        return forcing - (diagonal * field - neighbours(field))

    current = start
    for sweep_index in range(SWEEPS):
        current = current + relaxation * residual(current) / diagonal
    remainder = residual(current).reshape(-1)
    onehot = (block_id[0].reshape(1, -1) == jnp.arange(NBLK, dtype=jnp.int32)[:, None]).astype(
        jnp.float32
    )
    weight_flat = basis_weight[0].reshape(8, -1)
    coarse = jnp.einsum("bc,jc->bj", onehot, weight_flat * remainder, precision=highest)
    scale = 1.0 + jnp.einsum(
        "bc,jc->bj", onehot, weight_flat * weight_flat * diagonal.reshape(1, -1), precision=highest
    )
    correction = coarse / scale
    spread_back = jnp.dot(correction.T, onehot, precision=highest)
    updated = current + jnp.sum(weight_flat * spread_back, axis=0).reshape(shape)
    change = ((updated - start) * flow_keep).reshape(-1)
    sums = jax.ops.segment_sum(change, hosts, num_segments=elements)
    counts = jax.ops.segment_sum(
        jnp.broadcast_to(flow_keep, change.shape), hosts, num_segments=elements
    )
    sums, counts = lax.psum((sums, counts), "grp")
    element_pressure = sums / jnp.maximum(counts, 1.0)
    force = body_force[0] + biot_coef * assemble(
        coupling[:, None] * (mech_mask * element_pressure)[None, :], shape
    )
    solution = initial
    remain = force - apply(solution)
    search = remain
    norm_now = squares(remain)
    for iteration in range(ITERS):
        image = apply(search)
        step_size = norm_now / lax.psum(jnp.sum(search * image), ("gx", "gy"))
        solution = solution + step_size * search
        remain = remain - step_size * image
        norm_next = squares(remain)
        search = remain + norm_next / norm_now * search
        norm_now = norm_next
    pressure_out = jnp.where(is_mech, 0.0, updated)[None]
    displacement_out = jnp.where(is_mech, solution, 0.0)[None]
    return (pressure_out, displacement_out)


def solution(mesh):
    placed = (
        P("grp", "gx", "gy", None),
        P("grp", "gx", "gy", None),
        P("grp", "gx", "gy", None),
        P("grp", "gx", "gy", None),
        P("grp", "gx", "gy", None),
        P("grp", None, "gx", "gy", None),
        P("grp", "gx", "gy", None),
        P("grp", None, "gx", "gy", None),
        P("grp", None, "gx", "gy", None),
        P("grp", "gx", "gy", None),
        P("grp", "gx", "gy", None),
        P(),
    )
    return jax.shard_map(
        local,
        mesh=mesh,
        in_specs=placed,
        out_specs=(P("grp", "gx", "gy", None), P("grp", None, "gx", "gy", None)),
        check_vma=False,
    )
```

profile of v0, /device:TPU:6, one launch (start us, length us, event | category | flops | bytes accessed | tf_op | source)
XLA Modules:
  0.0 389.6 jit_solution(8827465589989205)
XLA Ops:
  8.2 1.3 collective-permute-start.2
  9.5 4.5 %collective-permute-start.3 = (f32[4,16,1]{2,1,0:T(8,128)S(1)}, f32[4,16,1]{2,1,0:T(8,128)S(1)}, u32[]{:S(2)}, u32[]{:S(2)}) collective-permute-start(f32[4,16,1]{2,1,0:T(8,128)S(1)} %get-tuple-element.65), channel_id=1, source_target_pairs={{8,0},{16,8},{24,16},{9,1},{17,9},{25,17},{10,2},{18,10},{26,18},{... | collective-permute-start | bytes 776 | tf_op jit(solution)/shard_map/ppermute | solution.py:39
  17.7 1.3 collective-permute-start.4
  19.0 3.0 collective-permute-start.5
  23.7 1.3 collective-permute-start.6
  25.0 4.5 %collective-permute-start.7 = (f32[6,1,130]{2,1,0:T(1,128)S(1)}, f32[6,1,130]{2,1,0:T(1,128)S(1)}, u32[]{:S(2)}, u32[]{:S(2)}) collective-permute-start(f32[6,1,130]{2,1,0:T(1,128)S(1)} %get-tuple-element.49), channel_id=1, source_target_pairs={{0,1},{1,2},{2,3},{4,5},{5,6},{6,7},{8,9},{9,10},{10,11},{12,13},{... | collective-permute-start | bytes 9368 | tf_op jit(solution)/shard_map/ppermute | solution.py:37
  31.0 1.3 collective-permute-start.1
  32.4 4.4 %collective-permute-done.1 = f32[3,5,1,128]{3,2,1,0:T(1,128)S(1)} collective-permute-done((f32[3,5,1,128]{3,2,1,0:T(1,128)S(1)}, f32[3,5,1,128]{3,2,1,0:T(1,128)S(1)}, u32[]{:S(2)}, u32[]{:S(2)}) %collective-permute-start.1) | collective-permute-done | bytes 7712 | tf_op jit(solution)/shard_map/ppermute | solution.py:21
  38.0 15.2 %psum.49 = f32[8192]{0:T(1024)S(1)} all-reduce(f32[8192]{0:T(1024)S(1)} %multiply_select_fusion), channel_id=1, replica_groups=mesh['grp'=4,'gx'=2,'gy'=4] {'grp'}, use_global_device_ids=true, to_apply=%region_0.1 | all-reduce | flops 8192 | bytes 65536 | tf_op jit(solution)/shard_map/psum | solution.py:26
  53.2 45.5 %gather_fusion = f32[8192]{0:T(1024)S(1)} fusion(f32[8192]{0:T(1024)S(1)} %psum.49, s32[8192]{0:T(1024)S(1)} %broadcast_clamp_fusion), kind=kCustom, calls=%fused_computation | custom fusion | bytes 98304 | tf_op jit(solution)/shard_map/jit(_take)/gather | solution.py:135
  99.0 1.3 collective-permute-start.8
  100.3 4.6 %collective-permute-start.9 = (f32[4,16,1]{2,1,0:T(8,128)S(1)}, f32[4,16,1]{2,1,0:T(8,128)S(1)}, u32[]{:S(2)}, u32[]{:S(2)}) collective-permute-start(f32[4,16,1]{2,1,0:T(8,128)S(1)} %get-tuple-element.63), channel_id=1, source_target_pairs={{8,0},{16,8},{24,16},{9,1},{17,9},{25,17},{10,2},{18,10},{26,18},{... | collective-permute-start | bytes 776 | tf_op jit(solution)/shard_map/ppermute | solution.py:39
  104.9 1.6 collective-permute-done.9
  106.5 1.3 collective-permute-start.10
  107.8 3.0 collective-permute-start.11
  111.8 1.3 collective-permute-start.12
  113.1 4.5 %collective-permute-start.13 = (f32[6,1,130]{2,1,0:T(1,128)S(1)}, f32[6,1,130]{2,1,0:T(1,128)S(1)}, u32[]{:S(2)}, u32[]{:S(2)}) collective-permute-start(f32[6,1,130]{2,1,0:T(1,128)S(1)} %get-tuple-element.47), channel_id=1, source_target_pairs={{0,1},{1,2},{2,3},{4,5},{5,6},{6,7},{8,9},{9,10},{10,11},{12,13},{... | collective-permute-start | bytes 9368 | tf_op jit(solution)/shard_map/ppermute | solution.py:37
  117.7 1.3 collective-permute-done.13
  119.4 1.3 collective-permute-start.14
  120.7 5.4 %collective-permute-start.15 = (f32[4,16,1]{2,1,0:T(8,128)S(1)}, f32[4,16,1]{2,1,0:T(8,128)S(1)}, u32[]{:S(2)}, u32[]{:S(2)}) collective-permute-start(f32[4,16,1]{2,1,0:T(8,128)S(1)} %get-tuple-element.61), channel_id=1, source_target_pairs={{8,0},{16,8},{24,16},{9,1},{17,9},{25,17},{10,2},{18,10},{26,18},{... | collective-permute-start | bytes 776 | tf_op jit(solution)/shard_map/ppermute | solution.py:39
  126.2 1.6 collective-permute-done.15
  127.8 1.3 collective-permute-start.16
  129.1 3.0 collective-permute-start.17
  132.3 43.8 %scatter_custom_fusion.1 = f32[8192]{0:T(1024)} fusion(s32[8192]{0:T(1024)S(1)} %bitcast.346, f32[8192]{0:T(1024)S(1)} %broadcast.231, f32[]{:T(128)} %constant.22.clone.1), kind=kCustom, calls=%fused_computation.264 | custom fusion | flops 8192 | bytes 32772 | tf_op jit(solution)/shard_map/scatter-add | solution.py:166
  176.1 1.3 collective-permute-start.18
  177.4 4.8 %collective-permute-start.19 = (f32[6,1,130]{2,1,0:T(1,128)S(1)}, f32[6,1,130]{2,1,0:T(1,128)S(1)}, u32[]{:S(2)}, u32[]{:S(2)}) collective-permute-start(f32[6,1,130]{2,1,0:T(1,128)S(1)} %get-tuple-element.45), channel_id=1, source_target_pairs={{0,1},{1,2},{2,3},{4,5},{5,6},{6,7},{8,9},{9,10},{10,11},{12,13},{... | collective-permute-start | bytes 9368 | tf_op jit(solution)/shard_map/ppermute | solution.py:37
  186.4 43.8 %scatter_custom_fusion = f32[8192]{0:T(1024)} fusion(s32[8192]{0:T(1024)S(1)} %bitcast.347, f32[8192]{0:T(1024)S(1)} %bitcast.354, f32[]{:T(128)} %constant.22.clone.1), kind=kCustom, calls=%fused_computation.266 | custom fusion | flops 8192 | bytes 32772 | tf_op jit(solution)/shard_map/scatter-add | solution.py:165
  230.2 47.4 %all-reduce.39.cloned.1.call-done = (f32[8192]{0:T(1024)}, f32[8192]{0:T(1024)}) async-done(((f32[8192]{0:T(1024)}, f32[8192]{0:T(1024)}), (f32[8192]{0:T(1024)}, f32[8192]{0:T(1024)})) %all-reduce.39.cloned.1.call-update) | async-done | bytes 65552 | tf_op jit(solution)/shard_map/psum | solution.py:169
  279.9 1.3 collective-permute-start.22
  282.0 1.4 collective-permute-start.20
  283.5 3.4 collective-permute-start.23
  287.0 3.4 collective-permute-start.21
  290.4 1.3 collective-permute-done.21
  291.8 1.5 collective-permute-start.24
  293.3 1.6 collective-permute-done.24
  296.2 4.5 %collective-permute-done.25 = f32[3,5,1,128]{3,2,1,0:T(1,128)S(1)} collective-permute-done((f32[3,5,1,128]{3,2,1,0:T(1,128)S(1)}, f32[3,5,1,128]{3,2,1,0:T(1,128)S(1)}, u32[]{:S(2)}, u32[]{:S(2)}) %collective-permute-start.25) | collective-permute-done | bytes 7712 | tf_op jit(solution)/shard_map/ppermute | solution.py:21
  302.8 1.3 collective-permute-start.26
  304.9 3.9 %collective-permute-start.27 = (f32[3,4,1,128]{3,2,1,0:T(1,128)S(1)}, f32[3,4,1,128]{3,2,1,0:T(1,128)S(1)}, u32[]{:S(2)}, u32[]{:S(2)}) collective-permute-start(f32[3,4,1,128]{3,2,1,0:T(1,128)S(1)} %pad_maximum_fusion.79), channel_id=1, source_target_pairs={{0,1},{1,2},{2,3},{4,5},{5,6},{6,7},{8,9},{9,10},{10,11},{12,13},{... | collective-permute-start | bytes 18440 | tf_op jit(solution)/shard_map/ppermute | solution.py:21
  308.9 1.3 collective-permute-done.27
  310.8 16.7 %all-reduce.35 = (f32[]{:T(128)}, f32[]{:T(128)}) all-reduce(f32[]{:T(128)} %get-tuple-element.3, f32[]{:T(128)} %get-tuple-element.2), channel_id=1, replica_groups=mesh['grp'=4,'gx'=2,'gy'=4] {'gx','gy'}, use_global_device_ids=true, to_apply=%region_7.8 | all-reduce | flops 2 | bytes 16 | tf_op jit(solution)/shard_map/psum | solution.py:93
  329.5 15.1 %psum.54 = f32[]{:T(128)} all-reduce(f32[]{:T(128)} %multiply_reduce_fusion), channel_id=1, replica_groups=mesh['grp'=4,'gx'=2,'gy'=4] {'gx','gy'}, use_global_device_ids=true, to_apply=%region_11.12 | all-reduce | flops 1 | bytes 8 | tf_op jit(solution)/shard_map/psum | solution.py:93
  346.0 1.3 collective-permute-start.28
  347.3 1.8 collective-permute-done.28
  350.4 4.2 %collective-permute-done.29 = f32[3,5,1,128]{3,2,1,0:T(1,128)S(1)} collective-permute-done((f32[3,5,1,128]{3,2,1,0:T(1,128)S(1)}, f32[3,5,1,128]{3,2,1,0:T(1,128)S(1)}, u32[]{:S(2)}, u32[]{:S(2)}) %collective-permute-start.29) | collective-permute-done | bytes 7712 | tf_op jit(solution)/shard_map/ppermute | solution.py:21
  356.7 1.3 collective-permute-start.30
  358.9 3.4 collective-permute-start.31
  362.3 1.3 collective-permute-done.31
  364.2 16.6 %psum.55 = f32[]{:T(128)} all-reduce(f32[]{:T(128)} %fusion.43), channel_id=1, replica_groups=mesh['grp'=4,'gx'=2,'gy'=4] {'gx','gy'}, use_global_device_ids=true, to_apply=%region_13.14 | all-reduce | flops 1 | bytes 8 | tf_op jit(solution)/shard_map/psum | solution.py:180
  (193 shorter events, 28.7 us)
Async XLA Ops:
  7.2 271.2 %copy-start = (f32[24,24]{1,0:T(8,128)S(1)}, f32[24,24]{1,0:T(8,128)}, u32[]{:S(2)}) copy-start(f32[24,24]{1,0:T(8,128)} %param.23) | copy-start | bytes 6916
  7.2 23.7 %copy-start.2 = (f32[1,4,16,128]{3,2,1,0:T(8,128)S(1)}, f32[1,4,16,128]{3,2,1,0:T(8,128)}, u32[]{:S(2)}) copy-start(f32[1,4,16,128]{3,2,1,0:T(8,128)} %param.12) | copy-start | bytes 98308
  7.2 23.8 %copy-start.1 = (f32[1,3,4,16,128]{4,3,2,1,0:T(8,128)S(1)}, f32[1,3,4,16,128]{4,3,2,1,0:T(8,128)}, u32[]{:S(2)}) copy-start(f32[1,3,4,16,128]{4,3,2,1,0:T(8,128)} %param.19) | copy-start | bytes 294916
  7.2 23.2 %copy-start.9 = (s32[1,4,16,128]{3,2,1,0:T(8,128)S(1)}, s32[1,4,16,128]{3,2,1,0:T(8,128)}, u32[]{:S(2)}) copy-start(s32[1,4,16,128]{3,2,1,0:T(8,128)} %param.22) | copy-start | bytes 98308
  7.2 270.4 %all-reduce.39.cloned.1.call-start = ((), (), s32[]{:S(2)}) async-start(), calls=%async_computation | async-start | bytes 131072 | tf_op jit(solution)/shard_map/psum | solution.py:169
  8.2 8.7 %collective-permute-start.2 = (f32[4,16,1]{2,1,0:T(8,128)S(1)}, f32[4,16,1]{2,1,0:T(8,128)S(1)}, u32[]{:S(2)}, u32[]{:S(2)}) collective-permute-start(f32[4,16,1]{2,1,0:T(8,128)S(1)} %get-tuple-element.66), channel_id=1, source_target_pairs={{0,8},{8,16},{16,24},{1,9},{9,17},{17,25},{2,10},{10,18},{18,26},{... | collective-permute-start | bytes 776 | tf_op jit(solution)/shard_map/ppermute | solution.py:37
  9.5 7.4 %collective-permute-start.3 = (f32[4,16,1]{2,1,0:T(8,128)S(1)}, f32[4,16,1]{2,1,0:T(8,128)S(1)}, u32[]{:S(2)}, u32[]{:S(2)}) collective-permute-start(f32[4,16,1]{2,1,0:T(8,128)S(1)} %get-tuple-element.65), channel_id=1, source_target_pairs={{8,0},{16,8},{24,16},{9,1},{17,9},{25,17},{10,2},{18,10},{26,18},{... | collective-permute-start | bytes 776 | tf_op jit(solution)/shard_map/ppermute | solution.py:39
  14.8 16.2 %collective-permute-start = (f32[3,1,16,128]{3,2,1,0:T(8,128)S(1)}, f32[3,1,16,128]{3,2,1,0:T(8,128)S(1)}, u32[]{:S(2)}, u32[]{:S(2)}) collective-permute-start(f32[3,1,16,128]{3,2,1,0:T(8,128)S(1)} %slice.643), channel_id=1, source_target_pairs={{4,0},{5,1},{6,2},{7,3},{12,8},{13,9},{14,10},{15,11},{20,16},{21,... | collective-permute-start | bytes 73736 | tf_op jit(solution)/shard_map/ppermute | solution.py:21
  17.7 4.4 %collective-permute-start.4 = (f32[1,16,130]{2,1,0:T(8,128)S(1)}, f32[1,16,130]{2,1,0:T(8,128)S(1)}, u32[]{:S(2)}, u32[]{:S(2)}) collective-permute-start(f32[1,16,130]{2,1,0:T(8,128)S(1)} %get-tuple-element.56), channel_id=1, source_target_pairs={{4,0},{5,1},{6,2},{7,3},{12,8},{13,9},{14,10},{15,11},{20,16},{21,... | collective-permute-start | bytes 24968 | tf_op jit(solution)/shard_map/ppermute | solution.py:39
  19.0 3.9 collective-permute-start.5
  23.7 6.8 %collective-permute-start.6 = (f32[6,1,130]{2,1,0:T(1,128)S(1)}, f32[6,1,130]{2,1,0:T(1,128)S(1)}, u32[]{:S(2)}, u32[]{:S(2)}) collective-permute-start(f32[6,1,130]{2,1,0:T(1,128)S(1)} %get-tuple-element.50), channel_id=1, source_target_pairs={{1,0},{2,1},{3,2},{5,4},{6,5},{7,6},{9,8},{10,9},{11,10},{13,12},{... | collective-permute-start | bytes 9368 | tf_op jit(solution)/shard_map/ppermute | solution.py:39
  25.0 5.9 %collective-permute-start.7 = (f32[6,1,130]{2,1,0:T(1,128)S(1)}, f32[6,1,130]{2,1,0:T(1,128)S(1)}, u32[]{:S(2)}, u32[]{:S(2)}) collective-permute-start(f32[6,1,130]{2,1,0:T(1,128)S(1)} %get-tuple-element.49), channel_id=1, source_target_pairs={{0,1},{1,2},{2,3},{4,5},{5,6},{6,7},{8,9},{9,10},{10,11},{12,13},{... | collective-permute-start | bytes 9368 | tf_op jit(solution)/shard_map/ppermute | solution.py:37
  31.0 5.8 %collective-permute-start.1 = (f32[3,5,1,128]{3,2,1,0:T(1,128)S(1)}, f32[3,5,1,128]{3,2,1,0:T(1,128)S(1)}, u32[]{:S(2)}, u32[]{:S(2)}) collective-permute-start(f32[3,5,1,128]{3,2,1,0:T(1,128)S(1)} %pad_maximum_fusion.77), channel_id=1, source_target_pairs={{1,0},{2,1},{3,2},{5,4},{6,5},{7,6},{9,8},{10,9},{11,10},{13,12},{... | collective-permute-start | bytes 23048 | tf_op jit(solution)/shard_map/ppermute | solution.py:21
  53.1 45.6 %copy-start.5 = (s32[1,4,16,128]{3,2,1,0:T(8,128)S(1)}, s32[1,4,16,128]{3,2,1,0:T(8,128)}, u32[]{:S(2)}) copy-start(s32[1,4,16,128]{3,2,1,0:T(8,128)} %param.18) | copy-start | bytes 98308
  53.1 45.6 %copy-start.6 = (s32[1,4,16,128]{3,2,1,0:T(8,128)S(1)}, s32[1,4,16,128]{3,2,1,0:T(8,128)}, u32[]{:S(2)}) copy-start(s32[1,4,16,128]{3,2,1,0:T(8,128)} %param.15) | copy-start | bytes 98308
  53.1 45.6 %copy-start.7 = (f32[1,4,16,128]{3,2,1,0:T(8,128)S(1)}, f32[1,4,16,128]{3,2,1,0:T(8,128)}, u32[]{:S(2)}) copy-start(f32[1,4,16,128]{3,2,1,0:T(8,128)} %param.14) | copy-start | bytes 98308
  53.1 45.6 %copy-start.8 = (f32[1,4,16,128]{3,2,1,0:T(8,128)S(1)}, f32[1,4,16,128]{3,2,1,0:T(8,128)}, u32[]{:S(2)}) copy-start(f32[1,4,16,128]{3,2,1,0:T(8,128)} %param.13) | copy-start | bytes 98308
  98.9 33.3 %copy-start.4 = (f32[1,8,4,16,128]{4,3,2,1,0:T(8,128)S(1)}, f32[1,8,4,16,128]{4,3,2,1,0:T(8,128)}, u32[]{:S(2)}) copy-start(f32[1,8,4,16,128]{4,3,2,1,0:T(8,128)} %param.17) | copy-start | bytes 786436
  99.0 5.9 %collective-permute-start.8 = (f32[4,16,1]{2,1,0:T(8,128)S(1)}, f32[4,16,1]{2,1,0:T(8,128)S(1)}, u32[]{:S(2)}, u32[]{:S(2)}) collective-permute-start(f32[4,16,1]{2,1,0:T(8,128)S(1)} %get-tuple-element.64), channel_id=1, source_target_pairs={{0,8},{8,16},{16,24},{1,9},{9,17},{17,25},{2,10},{10,18},{18,26},{... | collective-permute-start | bytes 776 | tf_op jit(solution)/shard_map/ppermute | solution.py:37
  100.3 6.2 %collective-permute-start.9 = (f32[4,16,1]{2,1,0:T(8,128)S(1)}, f32[4,16,1]{2,1,0:T(8,128)S(1)}, u32[]{:S(2)}, u32[]{:S(2)}) collective-permute-start(f32[4,16,1]{2,1,0:T(8,128)S(1)} %get-tuple-element.63), channel_id=1, source_target_pairs={{8,0},{16,8},{24,16},{9,1},{17,9},{25,17},{10,2},{18,10},{26,18},{... | collective-permute-start | bytes 776 | tf_op jit(solution)/shard_map/ppermute | solution.py:39
  106.5 4.3 %collective-permute-start.10 = (f32[1,16,130]{2,1,0:T(8,128)S(1)}, f32[1,16,130]{2,1,0:T(8,128)S(1)}, u32[]{:S(2)}, u32[]{:S(2)}) collective-permute-start(f32[1,16,130]{2,1,0:T(8,128)S(1)} %get-tuple-element.54), channel_id=1, source_target_pairs={{4,0},{5,1},{6,2},{7,3},{12,8},{13,9},{14,10},{15,11},{20,16},{21,... | collective-permute-start | bytes 24968 | tf_op jit(solution)/shard_map/ppermute | solution.py:39
  107.8 3.9 collective-permute-start.11
  111.8 5.9 %collective-permute-start.12 = (f32[6,1,130]{2,1,0:T(1,128)S(1)}, f32[6,1,130]{2,1,0:T(1,128)S(1)}, u32[]{:S(2)}, u32[]{:S(2)}) collective-permute-start(f32[6,1,130]{2,1,0:T(1,128)S(1)} %get-tuple-element.48), channel_id=1, source_target_pairs={{1,0},{2,1},{3,2},{5,4},{6,5},{7,6},{9,8},{10,9},{11,10},{13,12},{... | collective-permute-start | bytes 9368 | tf_op jit(solution)/shard_map/ppermute | solution.py:39
  113.1 5.9 %collective-permute-start.13 = (f32[6,1,130]{2,1,0:T(1,128)S(1)}, f32[6,1,130]{2,1,0:T(1,128)S(1)}, u32[]{:S(2)}, u32[]{:S(2)}) collective-permute-start(f32[6,1,130]{2,1,0:T(1,128)S(1)} %get-tuple-element.47), channel_id=1, source_target_pairs={{0,1},{1,2},{2,3},{4,5},{5,6},{6,7},{8,9},{9,10},{10,11},{12,13},{... | collective-permute-start | bytes 9368 | tf_op jit(solution)/shard_map/ppermute | solution.py:37
  119.1 63.2 %copy-start.11 = (s32[1,4,16,128]{3,2,1,0:T(8,128)S(1)}, s32[1,4,16,128]{3,2,1,0:T(8,128)}, u32[]{:S(2)}) copy-start(s32[1,4,16,128]{3,2,1,0:T(8,128)} %param.16) | copy-start | bytes 98308
  119.4 6.8 %collective-permute-start.14 = (f32[4,16,1]{2,1,0:T(8,128)S(1)}, f32[4,16,1]{2,1,0:T(8,128)S(1)}, u32[]{:S(2)}, u32[]{:S(2)}) collective-permute-start(f32[4,16,1]{2,1,0:T(8,128)S(1)} %get-tuple-element.62), channel_id=1, source_target_pairs={{0,8},{8,16},{16,24},{1,9},{9,17},{17,25},{2,10},{10,18},{18,26},{... | collective-permute-start | bytes 776 | tf_op jit(solution)/shard_map/ppermute | solution.py:37
  120.7 7.0 %collective-permute-start.15 = (f32[4,16,1]{2,1,0:T(8,128)S(1)}, f32[4,16,1]{2,1,0:T(8,128)S(1)}, u32[]{:S(2)}, u32[]{:S(2)}) collective-permute-start(f32[4,16,1]{2,1,0:T(8,128)S(1)} %get-tuple-element.61), channel_id=1, source_target_pairs={{8,0},{16,8},{24,16},{9,1},{17,9},{25,17},{10,2},{18,10},{26,18},{... | collective-permute-start | bytes 776 | tf_op jit(solution)/shard_map/ppermute | solution.py:39
  127.8 48.2 %collective-permute-start.16 = (f32[1,16,130]{2,1,0:T(8,128)S(1)}, f32[1,16,130]{2,1,0:T(8,128)S(1)}, u32[]{:S(2)}, u32[]{:S(2)}) collective-permute-start(f32[1,16,130]{2,1,0:T(8,128)S(1)} %get-tuple-element.52), channel_id=1, source_target_pairs={{4,0},{5,1},{6,2},{7,3},{12,8},{13,9},{14,10},{15,11},{20,16},{21,... | collective-permute-start | bytes 24968 | tf_op jit(solution)/shard_map/ppermute | solution.py:39
  129.1 46.9 %collective-permute-start.17 = (f32[1,16,130]{2,1,0:T(8,128)S(1)}, f32[1,16,130]{2,1,0:T(8,128)S(1)}, u32[]{:S(2)}, u32[]{:S(2)}) collective-permute-start(f32[1,16,130]{2,1,0:T(8,128)S(1)} %get-tuple-element.51), channel_id=1, source_target_pairs={{0,4},{1,5},{2,6},{3,7},{8,12},{9,13},{10,14},{11,15},{16,20},{17,... | collective-permute-start | bytes 24968 | tf_op jit(solution)/shard_map/ppermute | solution.py:37
  176.1 7.3 %collective-permute-start.18 = (f32[6,1,130]{2,1,0:T(1,128)S(1)}, f32[6,1,130]{2,1,0:T(1,128)S(1)}, u32[]{:S(2)}, u32[]{:S(2)}) collective-permute-start(f32[6,1,130]{2,1,0:T(1,128)S(1)} %get-tuple-element.46), channel_id=1, source_target_pairs={{1,0},{2,1},{3,2},{5,4},{6,5},{7,6},{9,8},{10,9},{11,10},{13,12},{... | collective-permute-start | bytes 9368 | tf_op jit(solution)/shard_map/ppermute | solution.py:39
  177.4 6.2 %collective-permute-start.19 = (f32[6,1,130]{2,1,0:T(1,128)S(1)}, f32[6,1,130]{2,1,0:T(1,128)S(1)}, u32[]{:S(2)}, u32[]{:S(2)}) collective-permute-start(f32[6,1,130]{2,1,0:T(1,128)S(1)} %get-tuple-element.45), channel_id=1, source_target_pairs={{0,1},{1,2},{2,3},{4,5},{5,6},{6,7},{8,9},{9,10},{10,11},{12,13},{... | collective-permute-start | bytes 9368 | tf_op jit(solution)/shard_map/ppermute | solution.py:37
  183.9 93.7 %copy-start.10 = (f32[1,4,16,128]{3,2,1,0:T(8,128)S(1)}, f32[1,4,16,128]{3,2,1,0:T(8,128)}, u32[]{:S(2)}) copy-start(f32[1,4,16,128]{3,2,1,0:T(8,128)} %param.21) | copy-start | bytes 98308
  279.9 3.6 collective-permute-start.22
  282.0 9.7 %copy-start.3 = (f32[1,3,4,16,128]{4,3,2,1,0:T(8,128)S(1)}, f32[1,3,4,16,128]{4,3,2,1,0:T(8,128)}, u32[]{:S(2)}) copy-start(f32[1,3,4,16,128]{4,3,2,1,0:T(8,128)} %param.20) | copy-start | bytes 294916
  282.0 4.9 %collective-permute-start.20 = (f32[3,1,17,128]{3,2,1,0:T(8,128)S(1)}, f32[3,1,17,128]{3,2,1,0:T(8,128)S(1)}, u32[]{:S(2)}, u32[]{:S(2)}) collective-permute-start(f32[3,1,17,128]{3,2,1,0:T(8,128)S(1)} %slice.667), channel_id=1, source_target_pairs={{0,4},{1,5},{2,6},{3,7},{8,12},{9,13},{10,14},{11,15},{16,20},{17,... | collective-permute-start | bytes 78344 | tf_op jit(solution)/shard_map/ppermute | solution.py:21
  283.5 6.9 %collective-permute-start.23 = (f32[3,4,1,128]{3,2,1,0:T(1,128)S(1)}, f32[3,4,1,128]{3,2,1,0:T(1,128)S(1)}, u32[]{:S(2)}, u32[]{:S(2)}) collective-permute-start(f32[3,4,1,128]{3,2,1,0:T(1,128)S(1)} %pad_maximum_fusion.80), channel_id=1, source_target_pairs={{0,1},{1,2},{2,3},{4,5},{5,6},{6,7},{8,9},{9,10},{10,11},{12,13},{... | collective-permute-start | bytes 18440 | tf_op jit(solution)/shard_map/ppermute | solution.py:21
  287.0 4.7 %collective-permute-start.21 = (f32[3,4,1,128]{3,2,1,0:T(1,128)S(1)}, f32[3,4,1,128]{3,2,1,0:T(1,128)S(1)}, u32[]{:S(2)}, u32[]{:S(2)}) collective-permute-start(f32[3,4,1,128]{3,2,1,0:T(1,128)S(1)} %pad_maximum_fusion.81), channel_id=1, source_target_pairs={{0,1},{1,2},{2,3},{4,5},{5,6},{6,7},{8,9},{9,10},{10,11},{12,13},{... | collective-permute-start | bytes 18440 | tf_op jit(solution)/shard_map/ppermute | solution.py:21
  291.8 3.1 collective-permute-start.24
  294.9 5.8 %collective-permute-start.25 = (f32[3,5,1,128]{3,2,1,0:T(1,128)S(1)}, f32[3,5,1,128]{3,2,1,0:T(1,128)S(1)}, u32[]{:S(2)}, u32[]{:S(2)}) collective-permute-start(f32[3,5,1,128]{3,2,1,0:T(1,128)S(1)} %pad_maximum_fusion.76), channel_id=1, source_target_pairs={{1,0},{2,1},{3,2},{5,4},{6,5},{7,6},{9,8},{10,9},{11,10},{13,12},{... | collective-permute-start | bytes 23048 | tf_op jit(solution)/shard_map/ppermute | solution.py:21
  302.8 2.1 collective-permute-start.26
  304.9 5.3 %collective-permute-start.27 = (f32[3,4,1,128]{3,2,1,0:T(1,128)S(1)}, f32[3,4,1,128]{3,2,1,0:T(1,128)S(1)}, u32[]{:S(2)}, u32[]{:S(2)}) collective-permute-start(f32[3,4,1,128]{3,2,1,0:T(1,128)S(1)} %pad_maximum_fusion.79), channel_id=1, source_target_pairs={{0,1},{1,2},{2,3},{4,5},{5,6},{6,7},{8,9},{9,10},{10,11},{12,13},{... | collective-permute-start | bytes 18440 | tf_op jit(solution)/shard_map/ppermute | solution.py:21
  346.0 3.1 collective-permute-start.28
  349.1 5.5 %collective-permute-start.29 = (f32[3,5,1,128]{3,2,1,0:T(1,128)S(1)}, f32[3,5,1,128]{3,2,1,0:T(1,128)S(1)}, u32[]{:S(2)}, u32[]{:S(2)}) collective-permute-start(f32[3,5,1,128]{3,2,1,0:T(1,128)S(1)} %pad_maximum_fusion.75), channel_id=1, source_target_pairs={{1,0},{2,1},{3,2},{5,4},{6,5},{7,6},{9,8},{10,9},{11,10},{13,12},{... | collective-permute-start | bytes 23048 | tf_op jit(solution)/shard_map/ppermute | solution.py:21
  356.7 2.1 collective-permute-start.30
  358.9 4.7 %collective-permute-start.31 = (f32[3,4,1,128]{3,2,1,0:T(1,128)S(1)}, f32[3,4,1,128]{3,2,1,0:T(1,128)S(1)}, u32[]{:S(2)}, u32[]{:S(2)}) collective-permute-start(f32[3,4,1,128]{3,2,1,0:T(1,128)S(1)} %pad_maximum_fusion.78), channel_id=1, source_target_pairs={{0,1},{1,2},{2,3},{4,5},{5,6},{6,7},{8,9},{9,10},{10,11},{12,13},{... | collective-permute-start | bytes 18440 | tf_op jit(solution)/shard_map/ppermute | solution.py:21
Sparse Core Ops, SparseCore 0:
  230.3 47.2 all-reduce.38
where the time goes:
time: 393 us; the launch traced here: 390 us
  other arithmetic  97.2 us (25%)
  starting transfers between devices  76.5 us (19%)
  waiting for transfers between devices  76.1 us (19%)
  blocking collectives  63.6 us (16%)
  local copies, waits for them, and re-layouts  51 us (13%)
  between operations  19.4 us (5%)
  matrix products  5.83 us (1%)
    psum x1, waiting for transfers between devices, local(): sums, counts = lax.psum((sums, counts), 'grp')  47.4 us
    gather x1, local copies, waits for them, and re-layouts, local(): strain_cells = jnp.take(strain, hosts).reshape(shape)  45.5 us
    scatter-add x1, other arithmetic, local(): jax.ops.segment_sum(jnp.broadcast_to(flow_keep, change.shape), hosts, num...  43.8 us
    scatter-add x1, other arithmetic, local(): sums = jax.ops.segment_sum(change, hosts, num_segments=elements)  43.8 us
    psum x2, blocking collectives, squares(): return lax.psum(jnp.sum(remain * remain), ('gx', 'gy'))  31.8 us
    ppermute x14, starting transfers between devices, passed_along(): lax.ppermute(value, axis, [(source, source + steps) for source in range(l...  27.3 us
    ppermute x9, starting transfers between devices, extended_2(): lax.ppermute(tail, axis, [(i, (i + 1) % count) for i in range(ends)])  26.8 us
    ppermute x9, starting transfers between devices, extended_2(): lax.ppermute(head, axis, [((i + 1) % count, i) for i in range(ends)])  22.4 us
  transfers between devices with their start and end apart: 33, of which 18 were waited for; matrix products, arithmetic and copies ran while one was open for 13% of the time, Pallas kernels for 0%

commit v1 on v0

v1 whole, which is shorter than its diff:
```python
import functools
import jax
import jax.numpy as jnp
from jax import lax
from jax.experimental import pallas as pl
from jax.experimental.pallas import tpu as pltpu
from jax.sharding import PartitionSpec as P

NBLK = 64

biot_coef = 1.5
relaxation = 0.8
spring_coef = 0.5
well_index = 4.0

H = 3
TOP = 8
f32 = jnp.float32
bf16 = jnp.bfloat16


def pairs_a(n):
    return [(i, i ^ 1) for i in range(n)]


def pairs_b(n):
    return [(i, (i + 1) % n if i % 2 else (i - 1) % n) for i in range(n)]


def swap_a(value, axis):
    return lax.ppermute(value, axis, pairs_a(lax.axis_size(axis)))


def swap_b(value, axis):
    return lax.ppermute(value, axis, pairs_b(lax.axis_size(axis)))


def both(value_a, value_b, axis):
    got_a = swap_a(value_a, axis)
    if lax.axis_size(axis) == 2:
        return got_a, got_a
    return got_a, swap_b(value_b, axis)


def by_xor(value, axis):
    n = lax.axis_size(axis)
    return [lax.ppermute(value, axis, [(i, i ^ k) for i in range(n)]) for k in range(1, n)]


def call(body, name, outs, *args, scratch=()):
    vmem = pl.BlockSpec(memory_space=pltpu.VMEM)
    unique, spots = [], []
    for arg in args:
        found = [i for i, other in enumerate(unique) if other is arg]
        if not found:
            unique.append(arg)
        spots.append(found[0] if found else len(unique) - 1)

    def expanded(*refs):
        return body(*[refs[i] for i in spots], *refs[len(unique) :])

    return pl.pallas_call(
        expanded,
        name=name,
        out_shape=[jax.ShapeDtypeStruct(o, f32) for o in outs],
        in_specs=[vmem] * len(unique),
        out_specs=[vmem] * len(outs),
        scratch_shapes=list(scratch),
    )(*unique)


class Place:
    def __init__(self):
        self.groups = lax.axis_size("grp")
        self.g = lax.axis_index("grp")
        self.mech = self.g == self.groups - 1
        for name in ("x", "y"):
            n, i = lax.axis_size("g" + name), lax.axis_index("g" + name)
            setattr(self, name + "odd", lax.rem(i, 2) == 1)
            setattr(self, name + "prev", i > 0)
            setattr(self, name + "next", i < n - 1)


def lane(shape):
    return lax.broadcasted_iota(jnp.int32, shape, len(shape) - 1)


def sub(shape):
    return lax.broadcasted_iota(jnp.int32, shape, len(shape) - 2)


def roll(value, shift, axis):
    return pltpu.roll(value, shift % value.shape[axis], axis)


def z_up(value):
    n = value.shape[-1]
    return jnp.where(lane(value.shape) < n - 1, roll(value, -1, value.ndim - 1), 0.0)


def z_down(value):
    return jnp.where(lane(value.shape) > 0, roll(value, 1, value.ndim - 1), 0.0)


def y_up(value):
    return roll(value, -1, value.ndim - 2)


def y_down(value):
    return roll(value, 1, value.ndim - 2)


def pack_rows(at, tile, out_a, out_b, fields, size_x, size_y):
    for f in range(fields):
        for x in range(size_x):
            low = tile[f, x, 0:H, :]
            high = tile[f, x, size_y - H : size_y, :]
            r = (f * size_x + x) * H
            out_a[r : r + H, :] = jnp.where(at.yodd, low, high)
            out_b[r : r + H, :] = jnp.where(at.yodd, high, low)


def extend(at, ext, tile, xa, xb, ya, yb, xya, xyb, fields, size_x, size_y):
    rows = ext.shape[2]
    lanes = ext.shape[3]
    blank_low = jnp.zeros((TOP, lanes), f32)
    blank_high = jnp.zeros((rows - TOP - size_y, lanes), f32)

    def side(valid, odd_is, a, b, index):
        value = jnp.where(odd_is, a[index], b[index])
        return jnp.where(valid, value, 0.0)

    def fill(f, xe, xs, valid, own, msg_a, msg_b):
        ext[f, xe, 0:TOP, :] = blank_low
        ext[f, xe, TOP + size_y : rows, :] = blank_high
        ext[f, xe, TOP : TOP + size_y, :] = own
        r = (f * size_x + xs) * H
        index = (slice(r, r + H), slice(None))
        before = side(valid & at.yprev, at.yodd, msg_a, msg_b, index)
        after = side(valid & at.ynext, ~at.yodd, msg_a, msg_b, index)
        ext[f, xe, TOP - H : TOP, :] = before
        ext[f, xe, TOP + size_y : TOP + size_y + H, :] = after

    class Mixed:
        def __init__(self, pick_a, a, b):
            self.pick_a, self.a, self.b = pick_a, a, b

        def __getitem__(self, index):
            if self.a is self.b:
                return self.a[index]
            return jnp.where(self.pick_a, self.a[index], self.b[index])

    always = at.g >= 0
    for f in range(fields):
        for x in range(size_x):
            fill(f, H + x, x, always, tile[f, x], ya, yb)
        for k in range(H):
            xs = size_x - H + k
            tile_p = Mixed(at.xodd, xa, xb)
            own = jnp.where(at.xprev, tile_p[f, xs], 0.0)
            fill(f, k, xs, at.xprev, own, Mixed(at.xodd, xya[0], xyb[0]), Mixed(at.xodd, xya[1], xyb[1]))
            tile_n = Mixed(~at.xodd, xa, xb)
            own = jnp.where(at.xnext, tile_n[f, k], 0.0)
            fill(f, H + size_x + k, k, at.xnext, own, Mixed(~at.xodd, xya[0], xyb[0]), Mixed(~at.xodd, xya[1], xyb[1]))


def corners(nodes, x):
    out = [None] * 24
    for a in range(2):
        for m in range(3):
            here = nodes[m, x + a]
            up = z_up(here)
            for e, v in ((0, here), (1, up)):
                out[3 * (4 * a + e) + m] = v
                out[3 * (4 * a + 2 + e) + m] = y_up(v)
    return out


def stack_tiles(values, tiles):
    cols = [jnp.concatenate([v[8 * t : 8 * t + 8] for v in values], axis=0) for t in tiles]
    return jnp.concatenate(cols, axis=1)


def split(value):
    high = value.astype(bf16)
    return high, (value - high.astype(f32)).astype(bf16)


def stiff(k_high, k_low, stacked):
    high, low = split(stacked)
    dot = functools.partial(jnp.dot, preferred_element_type=f32)
    return dot(k_high[...], high) + dot(k_high[...], low) + dot(k_low[...], high)


def add_apply(nodes, weight, out, k_high, k_low, first, last):
    rows = nodes.shape[2]
    tiles = rows // 8
    for m in range(3):
        out[m, first] = jnp.zeros((rows, 128), f32)

    def plane(x, carry):
        v = stiff(k_high, k_low, stack_tiles(corners(nodes, x), range(tiles)))
        w = weight[x]

        def entry(j):
            return w * jnp.concatenate(
                [v[8 * j : 8 * j + 8, 128 * t : 128 * t + 128] for t in range(tiles)], axis=0
            )

        for a in range(2):
            for m in range(3):
                part = []
                for b in range(2):
                    c = 4 * a + 2 * b
                    part.append(entry(3 * c + m) + z_down(entry(3 * (c + 1) + m)))
                total = part[0] + y_down(part[1])
                if a == 0:
                    out[m, x] = out[m, x] + total
                else:
                    out[m, x + 1] = total
        return carry

    lax.fori_loop(first, last, plane, 0)


def total_of(value):
    return jnp.sum(jnp.sum(value, axis=0, keepdims=True), axis=1, keepdims=True)


def onehot_sum(rows_of, size_x, size_y, shape, row_fn):
    def plane(x, acc):
        lefts, rights = [], []
        for y in range(size_y):
            left, right = row_fn(x, y)
            lefts.append(left)
            rights.append(right)
        return acc + lax.dot_general(
            jnp.concatenate(lefts, axis=1),
            jnp.concatenate(rights, axis=1),
            (((1,), (1,)), ((), ())),
            preferred_element_type=f32,
        )

    return lax.fori_loop(0, size_x, plane, jnp.zeros(shape, f32))


def z_slot(field, x, size_x):
    return 8 * (field * size_x + x)


def pack_body(p, src, sto, well, host, u, body, mod, mask, tile, ya, yb, zmsg):
    at = Place()
    size_x, size_y = p.shape[0], p.shape[1]

    @pl.when(at.mech)
    def _():
        tile[0:3] = u[...]
        tile[3:6] = body[...]
        tile[6] = mod[...] * mask[...].astype(f32)
        pack_rows(at, tile, ya, yb, 7, size_x, size_y)

    @pl.when(~at.mech)
    def _():
        where = lane((size_y, 128))
        msg = jnp.zeros((size_y, 128), f32)
        for x in range(size_x):
            diag = 6.0 + sto[x] + well_index * well[x].astype(f32)
            for f, v in enumerate((p[x], relaxation / diag, src[x], host[x].astype(f32))):
                s = z_slot(f, x, size_x)
                msg = jnp.where((where >= s) & (where < s + 6), roll(v, s + 3, 1), msg)
        zmsg[...] = msg


def strain_body(tile, xa, xb, ya, yb, xyaa, xyab, xyba, xybb, mask, host, zmsg, out, ue):
    at = Place()
    size_x, size_y = mask.shape[0], mask.shape[1]
    rows = size_x * size_y

    @pl.when(at.mech)
    def _():
        for m in range(3):
            for x in range(size_x + 1):
                r = (m * size_x + (x if x < size_x else 0)) * H
                if x < size_x:
                    own = tile[m, x]
                    after = jnp.where(at.yodd, yb[r : r + 1, :], ya[r : r + 1, :])
                else:
                    own = jnp.where(at.xodd, xb[m, 0], xa[m, 0])
                    of_a = jnp.where(at.yodd, xyab[r : r + 1, :], xyaa[r : r + 1, :])
                    of_b = jnp.where(at.yodd, xybb[r : r + 1, :], xyba[r : r + 1, :])
                    after = jnp.where(at.xodd, of_b, of_a)
                    own = jnp.where(at.xnext, own, 0.0)
                    after = jnp.where(at.xnext, after, 0.0)
                ue[m, x, 0:size_y, :] = own
                ue[m, x, size_y : size_y + 8, :] = jnp.zeros((8, 128), f32)
                ue[m, x, size_y : size_y + 1, :] = jnp.where(at.ynext, after, 0.0)
        before = None
        for x in range(size_x + 1):
            v = ue[0, x]
            s = v + z_up(v)
            q0 = s + y_up(s)
            v = ue[1, x]
            s = v + z_up(v)
            q1 = y_up(s) - s
            v = ue[2, x]
            s = z_up(v) - v
            q2 = s + y_up(s)
            if x:
                value = (q0 - before[0]) + (q1 + before[1]) + (q2 + before[2])
                r = (x - 1) * size_y
                out[r : r + size_y, :] = 0.25 * mask[x - 1].astype(f32) * value[0:size_y]
            before = (q0, q1, q2)

    @pl.when(~at.mech)
    def _():
        high_id, low_id = sub((rows, 128)), sub((128, 128))

        def row(x, y):
            h = host[x, y : y + 1, :]
            left = jnp.where(high_id == (h >> 7), 1.0, 0.0).astype(bf16)
            right = jnp.where(low_id == (h & 127), 1.0, 0.0).astype(bf16)
            return left, right

        out[0:rows, :] = onehot_sum(None, size_x, size_y, (rows, 128), row)
        out[rows : rows + size_y, :] = zmsg[...]


def gather_body(*refs):
    at = Place()
    k = at.groups - 1
    got, refs = refs[:k], refs[k:]
    p, src, sto, well, host = refs[:5]
    tile, xa, xb, ya, yb, xyaa, xyab, xyba, xybb, k_high, k_low = refs[5:16]
    out, out_a, out_b, g0, we, ext, acc, table = refs[16:]
    size_x, size_y = p.shape[0], p.shape[1]
    rows = size_x * size_y

    def pick(partner, index):
        value = got[0][index]
        for i in range(1, k):
            value = jnp.where((at.g ^ partner) == i + 1, got[i][index], value)
        return value

    @pl.when(~at.mech)
    def _():
        table[...] = pick(at.groups - 1, (slice(0, rows), slice(None)))
        zrows = (slice(rows, rows + size_y), slice(None))
        before = jnp.where(at.g > 0, pick(at.g - 1, zrows), 0.0)
        after = jnp.where(at.g < at.groups - 2, pick(at.g + 1, zrows), 0.0)
        spot = lane((size_y, 128))
        zside = jnp.where((spot & 7) < 3, before, after)
        first_host = z_slot(3, 0, size_x)
        zhost = jnp.where(spot >= first_host, zside, 0.0).astype(jnp.int32)
        cells = [host[x] for x in range(size_x)] + [zhost]
        cells = [c[8 * t : 8 * t + 8] for c in cells for t in range(size_y // 8)]
        highs = [c >> 7 for c in cells]
        lows = [c & 127 for c in cells]

        def step(h, values):
            line = jnp.broadcast_to(table[pl.ds(h, 1), :], (8, 128))
            return tuple(
                jnp.where(hi == h, jnp.take_along_axis(line, lo, axis=1, mode="promise_in_bounds"), v)
                for hi, lo, v in zip(highs, lows, values)
            )

        values = lax.fori_loop(0, rows, step, tuple(jnp.zeros((8, 128), f32) for _ in cells), unroll=4)
        per = size_y // 8
        strain = [jnp.concatenate(values[per * i : per * i + per], axis=0) for i in range(size_x + 1)]

        def z_tile(field, x, depth, source):
            value = roll(source, -(z_slot(field, x, size_x) + 3), 1)
            return jnp.where((spot < depth) | (spot >= 128 - depth), value, 0.0)

        for x in range(size_x):
            diag = 6.0 + sto[x] + well_index * well[x].astype(f32)
            out[0, x, :, 0:128] = p[x]
            out[0, x, :, 128:256] = z_tile(0, x, 3, zside)
            out[1, x, :, 0:128] = relaxation / diag
            out[1, x, :, 128:256] = z_tile(1, x, 2, zside)
            out[2, x, :, 0:128] = src[x] - biot_coef * strain[x]
            out[2, x, :, 128:256] = z_tile(2, x, 2, zside) - biot_coef * z_tile(3, x, 2, strain[size_x])
        pack_rows(at, out, out_a, out_b, 3, size_x, size_y)

    @pl.when(at.mech)
    def _():
        extend(at, ext, tile, xa, xb, ya, yb, (xyaa, xyab), (xyba, xybb), 7, size_x, size_y)
        we[...] = ext[6]
        add_apply(ext, we, acc, k_high, k_low, 1, size_x + 5)
        for m in range(3):
            for x in range(2, size_x + 5):
                g0[m, x] = ext[3 + m, x] - acc[m, x] - spring_coef * ext[m, x]


def flow_body(tile, xa, xb, ya, yb, xyaa, xyab, xyba, xybb, sto, well, block, basis, host, pressure, sums, ext, work, corr):
    at = Place()
    size_x, size_y = sto.shape[0], sto.shape[1]
    rows = size_x * size_y
    nx = size_x + 2 * H

    @pl.when(at.mech)
    def _():
        pressure[...] = jnp.zeros_like(pressure)

    @pl.when(~at.mech)
    def _():
        extend(at, ext, tile, xa, xb, ya, yb, (xyaa, xyab), (xyba, xybb), 3, size_x, size_y)

        def around(field, x):
            v = field[x]
            total = field[x + 1] + field[x - 1]
            total = total + y_up(v) + y_down(v)
            return total + roll(v, 1, 1) + roll(v, -1, 1)

        p0 = [ext[0, x] for x in range(nx)]
        p1 = [None] * nx
        for x in range(1, nx - 1):
            p1[x] = (1.0 - relaxation) * p0[x] + ext[1, x] * (ext[2, x] + around(p0, x))
        p2 = [None] * nx
        for x in range(2, nx - 2):
            p2[x] = (1.0 - relaxation) * p1[x] + ext[1, x] * (ext[2, x] + around(p1, x))
        own = slice(TOP, TOP + size_y)
        for x in range(size_x):
            r = slice(x * size_y, (x + 1) * size_y)
            diag = 6.0 + sto[x] + well_index * well[x].astype(f32)
            here = p2[x + H]
            res = (ext[2, x + H] + around(p2, x + H))[own, 0:128] - diag * here[own, 0:128]
            work[0, r, :] = here[own, 0:128]
            work[1, r, :] = res
            work[2, r, :] = diag
        block_ids = sub((NBLK, 128))

        def coarse_row(x, y):
            r = x * size_y + y
            w = basis[pl.ds(r, 8, stride=rows), :]
            res = work[1, pl.ds(r, 1), :]
            diag = work[2, pl.ds(r, 1), :]
            high, low = split(jnp.concatenate([w * res, w * w * diag], axis=0))
            right = jnp.where(block_ids == block[x, y : y + 1, :], 1.0, 0.0).astype(bf16)
            return jnp.concatenate([high, low], axis=0), right

        acc = onehot_sum(None, size_x, size_y, (32, NBLK), coarse_row)
        corr[...] = jnp.zeros_like(corr)
        corr[:, 0:NBLK] = (acc[0:8] + acc[16:24]) / (1.0 + (acc[8:16] + acc[24:32]))
        lines = [jnp.broadcast_to(corr[j : j + 1, :], (8, 128)) for j in range(8)]
        for x in range(size_x):
            for t in range(size_y // 8):
                ids = block[x, 8 * t : 8 * t + 8, :]
                r = x * size_y + 8 * t
                delta = jnp.zeros((8, 128), f32)
                for j in range(8):
                    got = jnp.take_along_axis(lines[j], ids, axis=1, mode="promise_in_bounds")
                    delta = delta + basis[j * rows + r : j * rows + r + 8, :] * got
                updated = work[0, r : r + 8, :] + delta
                pressure[x, 8 * t : 8 * t + 8, :] = updated
                change = updated - tile[0, x, 8 * t : 8 * t + 8, 0:128]
                high = change.astype(bf16).astype(f32)
                work[0, r : r + 8, :] = high
                work[1, r : r + 8, :] = change - high
        high_id, low_id = sub((rows, 128)), sub((128, 128))

        def sum_row(x, y):
            r = x * size_y + y
            h = host[x, y : y + 1, :]
            hit = high_id == (h >> 7)
            left = [jnp.where(hit, work[i, pl.ds(r, 1), :], 0.0).astype(bf16) for i in range(2)]
            right = jnp.where(low_id == (h & 127), 1.0, 0.0).astype(bf16)
            return jnp.concatenate(left, axis=0), right

        acc = onehot_sum(None, size_x, size_y, (2 * rows, 128), sum_row)
        sums[...] = acc[0:rows] + acc[rows : 2 * rows]


def element_body(*refs):
    at = Place()
    k = at.groups - 1
    sums, counts, refs = refs[:k], refs[k : 2 * k], refs[2 * k :]
    mask, out, out_a, out_b = refs
    size_x, size_y = mask.shape[0], mask.shape[1]

    @pl.when(at.mech)
    def _():
        for x in range(size_x):
            r = slice(x * size_y, (x + 1) * size_y)
            total = sums[0][r, :]
            count = counts[0][r, :]
            for i in range(1, k):
                total = total + sums[i][r, :]
                count = count + counts[i][r, :]
            out[0, x] = mask[x].astype(f32) * (total / jnp.maximum(count, 1.0))
        pack_rows(at, out, out_a, out_b, 1, size_x, size_y)


def krylov_body(tile, xa, xb, ya, yb, xyaa, xyab, xyba, xybb, g0, we, k_high, k_low, r_out, q_out, scal, ext, res, acc):
    at = Place()
    size_x, size_y = tile.shape[1], tile.shape[2]
    rows = ext.shape[2]
    own = slice(TOP, TOP + size_y)

    @pl.when(at.mech)
    def _():
        extend(at, ext, tile, xa, xb, ya, yb, (xyaa, xyab), (xyba, xybb), 1, size_x, size_y)
        line = sub((rows, 128))
        inside = ((line >= TOP) | at.yprev) & ((line < TOP + size_y) | at.ynext)

        def inside_x(x):
            if x < H:
                return inside & at.xprev
            if x >= H + size_x:
                return inside & at.xnext
            return inside

        before = None
        for x in range(1, size_x + 5):
            e = ext[0, x]
            sz = e + z_down(e)
            ssz = sz + y_down(sz)
            dsz = y_down(sz) - sz
            dz = z_down(e) - e
            sdz = dz + y_down(dz)
            if before is not None:
                f = (before[0] - ssz, before[1] + dsz, before[2] + sdz)
                for m in range(3):
                    value = g0[m, x] + (0.25 * biot_coef) * f[m]
                    res[m, x] = jnp.where(inside_x(x), value, 0.0)
            before = (ssz, dsz, sdz)

        add_apply(res, we, acc, k_high, k_low, 2, size_x + 4)
        rr = jnp.zeros((8, 128), f32)
        rq = jnp.zeros((8, 128), f32)
        for m in range(3):
            for x in range(H, H + size_x + 1):
                q = jnp.where(inside_x(x), acc[m, x] + spring_coef * res[m, x], 0.0)
                acc[m, x] = q
                if x < H + size_x:
                    for t in range(TOP, TOP + size_y, 8):
                        v = res[m, x, t : t + 8, :]
                        rr = rr + v * v
                        rq = rq + v * q[t : t + 8]
        rr = total_of(rr)
        shift = total_of(rq) / jnp.maximum(rr, 1e-30)
        rq = jnp.zeros((8, 128), f32)
        qq = jnp.zeros((8, 128), f32)
        for m in range(3):
            for x in range(H, H + size_x + 1):
                q = acc[m, x] - shift * res[m, x]
                acc[m, x] = q
                if x < H + size_x:
                    q_out[m, x - H] = q[own]
                    r_out[m, x - H] = res[m, x, own, :]
                    for t in range(TOP, TOP + size_y, 8):
                        v = q[t : t + 8]
                        qq = qq + v * v
                        rq = rq + v * res[m, x, t : t + 8, :]
        rq, qq = total_of(rq), total_of(qq)
        tiles = range(TOP // 8, (TOP + size_y) // 8)

        def plane(x, sums):
            uq = stack_tiles(corners(acc, x), tiles)
            ur = stack_tiles(corners(res, x), tiles)
            vq = stiff(k_high, k_low, uq)
            vr = stiff(k_high, k_low, ur)
            w = jnp.concatenate([we[x, 8 * t : 8 * t + 8, :] for t in tiles], axis=1)
            out = []
            for s, u, v in zip(sums, (uq, ur, ur), (vq, vq, vr)):
                part = u * v
                t = part[0:8]
                for j in range(1, 24):
                    t = t + part[8 * j : 8 * j + 8]
                out.append(s + w * t)
            return tuple(out)

        zero = jnp.zeros((8, 128 * len(tiles)), f32)
        e11, e12, e22 = lax.fori_loop(H, H + size_x, plane, (zero, zero, zero))
        e11 = total_of(e11) + spring_coef * qq
        e12 = total_of(e12) + spring_coef * rq
        e22 = total_of(e22) + spring_coef * rr
        for i, v in enumerate((rr, shift, rq, qq, e11, e12, e22)):
            scal[i : i + 1, :] = jnp.broadcast_to(v, (1, 128))
        scal[7:8, :] = jnp.zeros((1, 128), f32)


def final_body(scals, own, r, q, u, out):
    at = Place()

    @pl.when(~at.mech)
    def _():
        out[...] = jnp.zeros_like(out)

    @pl.when(at.mech)
    def _():
        count = scals.shape[0]
        get = lambda d, i: scals[d, i : i + 1, :]
        total = lambda fn: functools.reduce(lambda a, b: a + b, [fn(d) for d in range(count)])
        rr = total(lambda d: get(d, 0))
        mean = total(lambda d: get(d, 2) + get(d, 1) * get(d, 0)) / rr

        def shifted(low, mid, high):
            def one(d):
                gap = get(d, 1) - mean
                return get(d, high) + gap * (2.0 * get(d, mid) + gap * get(d, low))

            return total(one)

        qq = shifted(0, 2, 3)
        energy = shifted(6, 5, 4)
        ratio = qq / (mean * mean * rr)
        curve = energy / (mean * mean) - ratio * ratio * mean * rr
        second = ratio * rr / curve
        gap = own[1:2, :] - mean
        by_r = 1.0 / mean + second * (ratio - gap / mean)
        by_q = -second / mean
        out[...] = u[...] + by_r[None, None] * r[...] + by_q[None, None] * q[...]


def neighbours(tile, msg_a, msg_b):
    xa, xb = both(tile, tile, "gx")
    ya, yb = both(msg_a, msg_b, "gy")
    xyaa, xyba = both(ya, ya, "gx")
    xyab, xybb = both(yb, yb, "gx")
    return (xa, xb, ya, yb, xyaa, xyab, xyba, xybb)


def local(
    pressure,
    source,
    storage,
    well_mask,
    block_id,
    basis_weight,
    host_elem,
    displacement,
    body_force,
    modulus,
    elem_mask,
    stiffness,
):
    p, src, sto, well = pressure[0], source[0], storage[0], well_mask[0]
    host, block, mask = host_elem[0], block_id[0], elem_mask[0]
    size_x, size_y, size_z = p.shape
    rows = size_x * size_y
    basis = basis_weight[0].reshape(8 * rows, size_z)
    u, body = displacement[0], body_force[0]
    nx, ny = size_x + 2 * H, size_y + 2 * TOP
    kron = (stiffness[:, None, :, None] * jnp.eye(8, dtype=f32)[None, :, None, :]).reshape(192, 192)
    k_high = lax.reduce_precision(kron, 8, 7)
    k_low = (kron - k_high).astype(bf16)
    k_high = k_high.astype(bf16)

    msg = (7 * size_x * H, size_z)
    tile, ya, yb, zmsg = call(
        pack_body,
        "pack",
        [(7, size_x, size_y, size_z), msg, msg, (size_y, size_z)],
        p, src, sto, well, host, u, body, modulus[0], mask,
    )
    near = neighbours(tile, ya, yb)
    (line,) = call(
        strain_body,
        "strain",
        [(rows + size_y, size_z)],
        tile, *near, mask, host, zmsg,
        scratch=[pltpu.VMEM((3, size_x + 1, size_y + 8, size_z), f32)],
    )
    got = by_xor(line, "grp")
    msg = (3 * size_x * H, 2 * size_z)
    cells, ya, yb, g0, we = call(
        gather_body,
        "gather",
        [(3, size_x, size_y, 2 * size_z), msg, msg, (3, nx, ny, size_z), (nx, ny, size_z)],
        *got, p, src, sto, well, host, tile, *near, k_high, k_low,
        scratch=[
            pltpu.VMEM((7, nx, ny, size_z), f32),
            pltpu.VMEM((3, nx, ny, size_z), f32),
            pltpu.VMEM((rows, size_z), f32),
        ],
    )
    near = neighbours(cells, ya, yb)
    updated, sums = call(
        flow_body,
        "flow",
        [(size_x, size_y, size_z), (rows, size_z)],
        cells, *near, sto, well, block, basis, host,
        scratch=[
            pltpu.VMEM((3, nx, ny, 2 * size_z), f32),
            pltpu.VMEM((3, rows, size_z), f32),
            pltpu.VMEM((8, size_z), f32),
        ],
    )
    summed = by_xor(sums, "grp")
    msg = (size_x * H, size_z)
    elem, ya, yb = call(
        element_body,
        "element",
        [(1, size_x, size_y, size_z), msg, msg],
        *summed, *got, mask,
    )
    near = neighbours(elem, ya, yb)
    own = (3, size_x, size_y, size_z)
    r, q, scal = call(
        krylov_body,
        "krylov",
        [own, own, (8, size_z)],
        elem, *near, g0, we, k_high, k_low,
        scratch=[
            pltpu.VMEM((1, nx, ny, size_z), f32),
            pltpu.VMEM((3, nx, ny, size_z), f32),
            pltpu.VMEM((3, nx, ny, size_z), f32),
        ],
    )
    if lax.axis_size("gx") == 2:
        duo = jnp.stack([scal, swap_a(scal, "gx")])
        scals = jnp.concatenate([duo] + by_xor(duo, "gy"))
    else:
        scals = lax.all_gather(scal, ("gx", "gy"))
    (moved,) = call(final_body, "final", [own], scals, scal, r, q, u)
    return (updated[None], moved[None])


def solution(mesh):
    cell = P("grp", "gx", "gy", None)
    deep = P("grp", None, "gx", "gy", None)
    placed = (cell, cell, cell, cell, cell, deep, cell, deep, deep, cell, cell, P())
    return jax.shard_map(
        local,
        mesh=mesh,
        in_specs=placed,
        out_specs=(cell, deep),
        check_vma=False,
    )
```

time: 393 us -> 75.6 us (0.19)
  other arithmetic: 97.2 us -> 2.32 us
  blocking collectives: 63.6 us -> 0 us
  starting transfers between devices: 76.5 us -> 22.2 us
  waiting for transfers between devices: 76.1 us -> 22.5 us
  local copies, waits for them, and re-layouts: 51 us -> 5.44 us
  Pallas kernels: 0 us -> 21.9 us
  between operations: 19.4 us -> 0.83 us
  matrix products: 5.83 us -> 0 us
    scatter-add x2 -> x0, other arithmetic: 87.6 us -> none  [the longest x1 43.8 us: local(): jax.ops.segment_sum(jnp.broadcast_to(flow_keep, change.shape), hosts, num...]
    psum x4 -> x0, blocking collectives: 63.6 us -> none  [the longest x2 31.8 us: squares(): return lax.psum(jnp.sum(remain * remain), ('gx', 'gy'))]
    ppermute x32 -> x25, starting transfers between devices: 76.5 us -> 22.2 us  [the longest x9 11.6 us: by_xor(): lax.ppermute(value, axis, [(i, i ^ k) for i in range(n)])]
    psum x1 -> x0, waiting for transfers between devices: 47.4 us -> none  [local(): sums, counts = lax.psum((sums, counts), 'grp')]
    gather x1 -> x0, local copies, waits for them, and re-layouts: 45.5 us -> none  [local(): strain_cells = jnp.take(strain, hosts).reshape(shape)]
    pallas_call x0 -> x7, Pallas kernels: none -> 21.9 us  [call(): pl.pallas_call(expanded, name=name, out_shape=[jax.ShapeDtypeStruct(o, f3...]
    ppermute x32 -> x25, waiting for transfers between devices: 28.7 us -> 22.5 us  [the longest x9 9.67 us: by_xor(): lax.ppermute(value, axis, [(i, i ^ k) for i in range(n)])]
    dot_general x7 -> x0, matrix products: 5.83 us -> none  [the longest x3 2.37 us: apply(): jnp.dot(stiffness, spread(vector), precision=highest) * weights[None, :]]
  transfers between devices with their start and end apart: 33 -> 25, of which waited for: 18 -> 17; matrix products, arithmetic and copies ran while one was open for 13% -> 4% of each run, Pallas kernels for 0% -> 0%
where the time goes in v1:
time: 75.6 us; the launch traced here: 75.1 us
  waiting for transfers between devices  22.5 us (30%)
  starting transfers between devices  22.2 us (29%)
  Pallas kernels  21.9 us (29%)
  local copies, waits for them, and re-layouts  5.44 us (7%)
  other arithmetic  2.32 us (3%)
  between operations  0.83 us (1%)
    pallas_call x7, Pallas kernels, call(): pl.pallas_call(expanded, name=name, out_shape=[jax.ShapeDtypeStruct(o, f3...  21.9 us
    ppermute x9, starting transfers between devices, by_xor(): lax.ppermute(value, axis, [(i, i ^ k) for i in range(n)])  11.6 us
    ppermute x9, waiting for transfers between devices, by_xor(): lax.ppermute(value, axis, [(i, i ^ k) for i in range(n)])  9.67 us
    ppermute x3, starting transfers between devices, swap_b(): return lax.ppermute(value, axis, pairs_b(lax.axis_size(axis)))  7.48 us
    ppermute x3, waiting for transfers between devices, swap_b(): return lax.ppermute(value, axis, pairs_b(lax.axis_size(axis)))  7.48 us
    ppermute x13, waiting for transfers between devices, swap_a(): return lax.ppermute(value, axis, pairs_a(lax.axis_size(axis)))  5.33 us
    unnamed x48, local copies, waits for them, and re-layouts  4.76 us
    ppermute x13, starting transfers between devices, swap_a(): return lax.ppermute(value, axis, pairs_a(lax.axis_size(axis)))  3.05 us
  transfers between devices with their start and end apart: 25, of which 17 were waited for; matrix products, arithmetic and copies ran while one was open for 4% of the time, Pallas kernels for 0%

profile of v1, /device:TPU:6, one launch (start us, length us, event | category | flops | bytes accessed | tf_op | source)
XLA Modules:
  0.0 75.1 jit_solution(17503426668493216632)
XLA Ops:
  0.6 1.8 %pack.1 = (f32[7,4,16,128]{3,2,1,0:T(8,128)}, f32[84,128]{1,0:T(8,128)}, f32[84,128]{1,0:T(8,128)}, f32[16,128]{1,0:T(8,128)}) custom-call(f32[4,16,128]{2,1,0:T(8,128)} %bitcast.35, f32[4,16,128]{2,1,0:T(8,128)} %bitcast.37, f32[4,16,128]{2,1,0:T(8,128)} %bitcast.28, s32[4,16,128]{2,1,0:T(8,128)} %bitcast.31, s32[4,16,128]{2,1,0:T(8,128)} %bitcast.19, ...), custom_call_target="tpu_custom_call" | custom-call | tf_op jit(solution)/shard_map/pack/pallas_call | solution.py:62
  2.5 1.6 %collective-permute-start.1 = (f32[84,128]{1,0:T(8,128)}, f32[84,128]{1,0:T(8,128)S(1)}, u32[]{:S(2)}, u32[]{:S(2)}) collective-permute-start(f32[84,128]{1,0:T(8,128)} %get-tuple-element.20), channel_id=1, source_target_pairs={{0,1},{1,0},{2,3},{3,2},{4,5},{5,4},{6,7},{7,6},{8,9},{9,8},{10,11... | collective-permute-start | bytes 129032 | tf_op jit(solution)/shard_map/ppermute | solution.py:31
  4.0 2.5 %collective-permute-start.2 = (f32[84,128]{1,0:T(8,128)}, f32[84,128]{1,0:T(8,128)S(1)}, u32[]{:S(2)}, u32[]{:S(2)}) collective-permute-start(f32[84,128]{1,0:T(8,128)} %get-tuple-element.21), channel_id=1, source_target_pairs={{0,3},{1,2},{2,1},{3,0},{4,7},{5,6},{6,5},{7,4},{8,11},{9,10},{10,... | collective-permute-start | bytes 129032 | tf_op jit(solution)/shard_map/ppermute | solution.py:35
  6.7 0.4 collective-permute-start.3
  7.1 3.0 %collective-permute-done.2.refs_3_.refs_11_ = f32[84,128]{1,0:T(8,128)S(1)} collective-permute-done((f32[84,128]{1,0:T(8,128)}, f32[84,128]{1,0:T(8,128)S(1)}, u32[]{:S(2)}, u32[]{:S(2)}) %collective-permute-start.2) | collective-permute-done | bytes 43040 | tf_op jit(solution)/shard_map/ppermute | solution.py:35
  10.1 0.9 %broadcast_multiply_fusion = f32[24,8,24,8]{3,2,1,0:T(8,128)S(1)} fusion(f32[8,8]{1,0:T(8,128)S(1)} %fusion.1, f32[24,24]{1,0:T(8,128)} %param.23), kind=kLoop, calls=%fused_computation | loop fusion | flops 36864 | bytes 150016 | tf_op jit(solution)/shard_map/mul | solution.py:644
  11.0 0.7 mul.20
  11.8 0.6 copy-done.4
  12.5 1.9 %strain.1 = f32[80,128]{1,0:T(8,128)} custom-call(f32[7,4,16,128]{3,2,1,0:T(8,128)} %get-tuple-element.19.refs_0_.refs_8_, f32[7,4,16,128]{3,2,1,0:T(8,128)} %copy-done, f32[84,128]{1,0:T(8,128)} %copy-done.2, f32[84,128]{1,0:T(8,128)} %copy-done.3, f32[84,128]{1,0:T(8,128)} %copy-done.4, f32[84,128]{1,0:T(8,128)} %copy-done.5, s32[4,16,128]{2,1,0:T(8,128)} %bitcast.26, ...), custom_call_target="tpu_custom_call" | custom-call | tf_op jit(solution)/shard_map/strain/pallas_call | solution.py:62
  14.3 1.6 %collective-permute-start.7 = (f32[80,128]{1,0:T(8,128)}, f32[80,128]{1,0:T(8,128)S(1)}, u32[]{:S(2)}, u32[]{:S(2)}) collective-permute-start(f32[80,128]{1,0:T(8,128)} %strain.1), channel_id=1, source_target_pairs={{0,24},{8,16},{16,8},{24,0},{1,25},{9,17},{17,9},{25,1},{2,26},{10... | collective-permute-start | bytes 122888 | tf_op jit(solution)/shard_map/ppermute | solution.py:47
  16.0 1.5 %collective-permute-start.6 = (f32[80,128]{1,0:T(8,128)}, f32[80,128]{1,0:T(8,128)S(1)}, u32[]{:S(2)}, u32[]{:S(2)}) collective-permute-start(f32[80,128]{1,0:T(8,128)} %strain.1), channel_id=1, source_target_pairs={{0,16},{8,24},{16,0},{24,8},{1,17},{9,25},{17,1},{25,9},{2,18},{10... | collective-permute-start | bytes 122888 | tf_op jit(solution)/shard_map/ppermute | solution.py:47
  17.5 0.3 collective-permute-start.5
  17.8 0.7 fusion
  18.5 1.0 %collective-permute-done.7.refs_2_.refs_5_ = f32[80,128]{1,0:T(8,128)S(1)} collective-permute-done((f32[80,128]{1,0:T(8,128)}, f32[80,128]{1,0:T(8,128)S(1)}, u32[]{:S(2)}, u32[]{:S(2)}) %collective-permute-start.7) | collective-permute-done | bytes 40992 | tf_op jit(solution)/shard_map/ppermute | solution.py:47
  19.6 0.8 %collective-permute-done.6.refs_1_.refs_4_ = f32[80,128]{1,0:T(8,128)S(1)} collective-permute-done((f32[80,128]{1,0:T(8,128)}, f32[80,128]{1,0:T(8,128)S(1)}, u32[]{:S(2)}, u32[]{:S(2)}) %collective-permute-start.6) | collective-permute-done | bytes 40992 | tf_op jit(solution)/shard_map/ppermute | solution.py:47
  20.3 1.4 %collective-permute-done.5.refs_0_.refs_3_ = f32[80,128]{1,0:T(8,128)S(1)} collective-permute-done((f32[80,128]{1,0:T(8,128)}, f32[80,128]{1,0:T(8,128)S(1)}, u32[]{:S(2)}, u32[]{:S(2)}) %collective-permute-start.5) | collective-permute-done | bytes 40992 | tf_op jit(solution)/shard_map/ppermute | solution.py:47
  21.7 0.6 copy-done.8
  22.3 6.2 %gather.1 = (f32[3,4,16,256]{3,2,1,0:T(8,128)}, f32[36,256]{1,0:T(8,128)}, f32[36,256]{1,0:T(8,128)}, f32[3,10,32,128]{3,2,1,0:T(8,128)}, f32[10,32,128]{2,1,0:T(8,128)}) custom-call(f32[80,128]{1,0:T(8,128)} %copy-done.8, f32[80,128]{1,0:T(8,128)} %copy-done.7, f32[80,128]{1,0:T(8,128)} %copy-done.6, f32[4,16,128]{2,1,0:T(8,128)} %bitcast.36, ...), custom_call_target="tpu_custom_call" | custom-call | tf_op jit(solution)/shard_map/gather/pallas_call | solution.py:62
  28.7 2.5 %collective-permute-start.10 = (f32[36,256]{1,0:T(8,128)}, f32[36,256]{1,0:T(8,128)S(1)}, u32[]{:S(2)}, u32[]{:S(2)}) collective-permute-start(f32[36,256]{1,0:T(8,128)} %get-tuple-element.25), channel_id=1, source_target_pairs={{0,3},{1,2},{2,1},{3,0},{4,7},{5,6},{6,5},{7,4},{8,11},{9,10},{10,... | collective-permute-start | bytes 110600 | tf_op jit(solution)/shard_map/ppermute | solution.py:35
  31.2 1.7 %collective-permute-done.9.refs_2_ = f32[36,256]{1,0:T(8,128)S(1)} collective-permute-done((f32[36,256]{1,0:T(8,128)}, f32[36,256]{1,0:T(8,128)S(1)}, u32[]{:S(2)}, u32[]{:S(2)}) %collective-permute-start.9) | collective-permute-done | bytes 36896 | tf_op jit(solution)/shard_map/ppermute | solution.py:31
  32.9 1.9 %collective-permute-done.10.refs_3_ = f32[36,256]{1,0:T(8,128)S(1)} collective-permute-done((f32[36,256]{1,0:T(8,128)}, f32[36,256]{1,0:T(8,128)S(1)}, u32[]{:S(2)}, u32[]{:S(2)}) %collective-permute-start.10) | collective-permute-done | bytes 36896 | tf_op jit(solution)/shard_map/ppermute | solution.py:35
  34.8 1.2 %collective-permute-done.12.refs_5_ = f32[36,256]{1,0:T(8,128)S(1)} collective-permute-done((f32[36,256]{1,0:T(8,128)S(1)}, f32[36,256]{1,0:T(8,128)S(1)}, u32[]{:S(2)}, u32[]{:S(2)}) %collective-permute-start.12) | collective-permute-done | bytes 36896 | tf_op jit(solution)/shard_map/ppermute | solution.py:31
  36.0 0.6 copy-done.13
  36.7 1.8 %flow.1 = (f32[4,16,128]{2,1,0:T(8,128)}, f32[64,128]{1,0:T(8,128)}) custom-call(f32[3,4,16,256]{3,2,1,0:T(8,128)} %get-tuple-element.23.refs_0_, f32[3,4,16,256]{3,2,1,0:T(8,128)} %copy-done.1, f32[36,256]{1,0:T(8,128)} %copy-done.10, f32[36,256]{1,0:T(8,128)} %copy-done.11, f32[36,256]{1,0:T(8,128)} %copy-done.12, f32[36,256]{1,0:T(8,128)} %copy-done.13, ...), custom_call_target="tpu_custom_call" | custom-call | tf_op jit(solution)/shard_map/flow/pallas_call | solution.py:62
  38.5 3.1 %collective-permute-start.15 = (f32[64,128]{1,0:T(8,128)}, f32[64,128]{1,0:T(8,128)S(1)}, u32[]{:S(2)}, u32[]{:S(2)}) collective-permute-start(f32[64,128]{1,0:T(8,128)} %get-tuple-element.27), channel_id=1, source_target_pairs={{0,24},{8,16},{16,8},{24,0},{1,25},{9,17},{17,9},{25,1},{2,26},{10... | collective-permute-start | bytes 98312 | tf_op jit(solution)/shard_map/ppermute | solution.py:47
  41.6 0.3 collective-permute-start.14
  41.9 0.3 collective-permute-start.13
  42.2 1.5 %collective-permute-done.15.refs_2_ = f32[64,128]{1,0:T(8,128)S(1)} collective-permute-done((f32[64,128]{1,0:T(8,128)}, f32[64,128]{1,0:T(8,128)S(1)}, u32[]{:S(2)}, u32[]{:S(2)}) %collective-permute-start.15) | collective-permute-done | bytes 32800 | tf_op jit(solution)/shard_map/ppermute | solution.py:47
  43.7 2.0 %collective-permute-done.14.refs_1_ = f32[64,128]{1,0:T(8,128)S(1)} collective-permute-done((f32[64,128]{1,0:T(8,128)}, f32[64,128]{1,0:T(8,128)S(1)}, u32[]{:S(2)}, u32[]{:S(2)}) %collective-permute-start.14) | collective-permute-done | bytes 32800 | tf_op jit(solution)/shard_map/ppermute | solution.py:47
  45.7 0.3 collective-permute-done.13.refs_0_
  46.3 0.6 copy-done.16
  46.9 1.5 %element.1 = (f32[1,4,16,128]{3,2,1,0:T(8,128)}, f32[12,128]{1,0:T(8,128)}, f32[12,128]{1,0:T(8,128)}) custom-call(f32[64,128]{1,0:T(8,128)} %copy-done.16, f32[64,128]{1,0:T(8,128)} %copy-done.15, f32[64,128]{1,0:T(8,128)} %copy-done.14, f32[80,128]{1,0:T(8,128)} %copy-done.8, f32[80,128]{1,0:T(8,128)} %copy-done.7, f32[80,128]{1,0:T(8,128)} %copy-done.6, ...), custom_call_target="tpu_custom_call" | custom-call | tf_op jit(solution)/shard_map/element/pallas_call | solution.py:62
  48.5 0.8 %collective-permute-start.17 = (f32[12,128]{1,0:T(8,128)}, f32[12,128]{1,0:T(8,128)S(1)}, u32[]{:S(2)}, u32[]{:S(2)}) collective-permute-start(f32[12,128]{1,0:T(8,128)} %get-tuple-element.29), channel_id=1, source_target_pairs={{0,1},{1,0},{2,3},{3,2},{4,5},{5,4},{6,7},{7,6},{8,9},{9,8},{10,11... | collective-permute-start | bytes 18440 | tf_op jit(solution)/shard_map/ppermute | solution.py:31
  49.3 2.5 %collective-permute-start.18 = (f32[12,128]{1,0:T(8,128)}, f32[12,128]{1,0:T(8,128)S(1)}, u32[]{:S(2)}, u32[]{:S(2)}) collective-permute-start(f32[12,128]{1,0:T(8,128)} %get-tuple-element.30), channel_id=1, source_target_pairs={{0,3},{1,2},{2,1},{3,0},{4,7},{5,6},{6,5},{7,4},{8,11},{9,10},{10,... | collective-permute-start | bytes 18440 | tf_op jit(solution)/shard_map/ppermute | solution.py:35
  51.8 0.6 collective-permute-done.17.refs_2_
  52.3 2.6 %collective-permute-done.18.refs_3_ = f32[12,128]{1,0:T(8,128)S(1)} collective-permute-done((f32[12,128]{1,0:T(8,128)}, f32[12,128]{1,0:T(8,128)S(1)}, u32[]{:S(2)}, u32[]{:S(2)}) %collective-permute-start.18) | collective-permute-done | bytes 6176 | tf_op jit(solution)/shard_map/ppermute | solution.py:35
  55.0 1.2 %collective-permute-done.20.refs_5_ = f32[12,128]{1,0:T(8,128)S(1)} collective-permute-done((f32[12,128]{1,0:T(8,128)S(1)}, f32[12,128]{1,0:T(8,128)S(1)}, u32[]{:S(2)}, u32[]{:S(2)}) %collective-permute-start.20) | collective-permute-done | bytes 6176 | tf_op jit(solution)/shard_map/ppermute | solution.py:31
  56.2 0.6 copy-done.21
  56.7 6.9 %krylov.1 = (f32[3,4,16,128]{3,2,1,0:T(8,128)}, f32[3,4,16,128]{3,2,1,0:T(8,128)}, f32[8,128]{1,0:T(8,128)}) custom-call(f32[1,4,16,128]{3,2,1,0:T(8,128)} %get-tuple-element.28.refs_0_, f32[1,4,16,128]{3,2,1,0:T(8,128)} %copy-done.17, f32[12,128]{1,0:T(8,128)} %copy-done.18, f32[12,128]{1,0:T(8,128)} %copy-done.19, f32[12,128]{1,0:T(8,128)} %copy-done.20, ...), custom_call_target="tpu_custom_call" | custom-call | tf_op jit(solution)/shard_map/krylov/pallas_call | solution.py:62
  63.8 0.7 constant_dynamic-update-slice_fusion.4
  64.5 0.5 collective-permute-done.21
  65.1 0.7 pad_maximum_fusion
  65.7 2.5 %collective-permute-start.24 = (f32[2,8,128]{2,1,0:T(8,128)S(1)}, f32[2,8,128]{2,1,0:T(8,128)S(1)}, u32[]{:S(2)}, u32[]{:S(2)}) collective-permute-start(f32[2,8,128]{2,1,0:T(8,128)S(1)} %pad_maximum_fusion), channel_id=1, source_target_pairs={{0,3},{1,2},{2,1},{3,0},{4,7},{5,6},{6,5},{7,4},{8,11},{9,10},{10,... | collective-permute-start | bytes 24584 | tf_op jit(solution)/shard_map/ppermute | solution.py:47
  68.2 1.9 %collective-permute-start.22 = (f32[2,8,128]{2,1,0:T(8,128)S(1)}, f32[2,8,128]{2,1,0:T(8,128)S(1)}, u32[]{:S(2)}, u32[]{:S(2)}) collective-permute-start(f32[2,8,128]{2,1,0:T(8,128)S(1)} %pad_maximum_fusion), channel_id=1, source_target_pairs={{0,1},{1,0},{2,3},{3,2},{4,5},{5,4},{6,7},{7,6},{8,9},{9,8},{10,11... | collective-permute-start | bytes 24584 | tf_op jit(solution)/shard_map/ppermute | solution.py:47
  70.1 1.7 %collective-permute-done.22 = f32[2,8,128]{2,1,0:T(8,128)S(1)} collective-permute-done((f32[2,8,128]{2,1,0:T(8,128)S(1)}, f32[2,8,128]{2,1,0:T(8,128)S(1)}, u32[]{:S(2)}, u32[]{:S(2)}) %collective-permute-start.22) | collective-permute-done | bytes 8224 | tf_op jit(solution)/shard_map/ppermute | solution.py:47
  71.9 0.9 %collective-permute-done.23 = f32[2,8,128]{2,1,0:T(8,128)S(1)} collective-permute-done((f32[2,8,128]{2,1,0:T(8,128)S(1)}, f32[2,8,128]{2,1,0:T(8,128)S(1)}, u32[]{:S(2)}, u32[]{:S(2)}) %collective-permute-start.23) | collective-permute-done | bytes 8224 | tf_op jit(solution)/shard_map/ppermute | solution.py:47
  72.8 0.6 copy-done.9
  73.4 1.7 %final.1 = f32[3,4,16,128]{3,2,1,0:T(8,128)} custom-call(f32[8,8,128]{2,1,0:T(8,128)} %copy-done.9, f32[8,128]{1,0:T(8,128)} %get-tuple-element.33.refs_1_, f32[3,4,16,128]{3,2,1,0:T(8,128)} %get-tuple-element.34.refs_2_, f32[3,4,16,128]{3,2,1,0:T(8,128)} %get-tuple-element.35.refs_3_, f32[3,4,16,128]{3,2,1,0:T(8,128)} %bitcast.24), custom_call_target="tpu_custom_call" | custom-call | tf_op jit(solution)/shard_map/final/pallas_call | solution.py:62
  (63 shorter events, 1.1 us)
Async XLA Ops:
  2.5 4.3 %collective-permute-start.1 = (f32[84,128]{1,0:T(8,128)}, f32[84,128]{1,0:T(8,128)S(1)}, u32[]{:S(2)}, u32[]{:S(2)}) collective-permute-start(f32[84,128]{1,0:T(8,128)} %get-tuple-element.20), channel_id=1, source_target_pairs={{0,1},{1,0},{2,3},{3,2},{4,5},{5,4},{6,7},{7,6},{8,9},{9,8},{10,11... | collective-permute-start | bytes 129032 | tf_op jit(solution)/shard_map/ppermute | solution.py:31
  4.0 6.1 %collective-permute-start.2 = (f32[84,128]{1,0:T(8,128)}, f32[84,128]{1,0:T(8,128)S(1)}, u32[]{:S(2)}, u32[]{:S(2)}) collective-permute-start(f32[84,128]{1,0:T(8,128)} %get-tuple-element.21), channel_id=1, source_target_pairs={{0,3},{1,2},{2,1},{3,0},{4,7},{5,6},{6,5},{7,4},{8,11},{9,10},{10,... | collective-permute-start | bytes 129032 | tf_op jit(solution)/shard_map/ppermute | solution.py:35
  6.5 5.3 %collective-permute-start = (f32[7,4,16,128]{3,2,1,0:T(8,128)}, f32[7,4,16,128]{3,2,1,0:T(8,128)S(1)}, u32[]{:S(2)}, u32[]{:S(2)}) collective-permute-start(f32[7,4,16,128]{3,2,1,0:T(8,128)} %get-tuple-element.19.refs_0_.refs_8_), channel_id=1, source_target_pairs={{0,4},{4,0},{1,5},{5,1},{2,6},{6,2},{3,7},{7,3},{8,12},{12,8},{9,1... | collective-permute-start | bytes 688136 | tf_op jit(solution)/shard_map/ppermute | solution.py:31
  6.7 5.0 %copy-start.2 = (f32[84,128]{1,0:T(8,128)}, f32[84,128]{1,0:T(8,128)S(1)}, u32[]{:S(2)}) copy-start(f32[84,128]{1,0:T(8,128)S(1)} %collective-permute-done.1.refs_2_.refs_10_) | copy-start | bytes 129028
  6.7 5.0 %collective-permute-start.3 = (f32[84,128]{1,0:T(8,128)S(1)}, f32[84,128]{1,0:T(8,128)S(1)}, u32[]{:S(2)}, u32[]{:S(2)}) collective-permute-start(f32[84,128]{1,0:T(8,128)S(1)} %collective-permute-done.1.refs_2_.refs_10_), channel_id=1, source_target_pairs={{0,4},{4,0},{1,5},{5,1},{2,6},{6,2},{3,7},{7,3},{8,12},{12,8},{9,1... | collective-permute-start | bytes 129032 | tf_op jit(solution)/shard_map/ppermute | solution.py:31
  10.1 1.6 %copy-start.3 = (f32[84,128]{1,0:T(8,128)}, f32[84,128]{1,0:T(8,128)S(1)}, u32[]{:S(2)}) copy-start(f32[84,128]{1,0:T(8,128)S(1)} %collective-permute-done.2.refs_3_.refs_11_) | copy-start | bytes 129028
  10.1 1.7 %collective-permute-start.4 = (f32[84,128]{1,0:T(8,128)S(1)}, f32[84,128]{1,0:T(8,128)S(1)}, u32[]{:S(2)}, u32[]{:S(2)}) collective-permute-start(f32[84,128]{1,0:T(8,128)S(1)} %collective-permute-done.2.refs_3_.refs_11_), channel_id=1, source_target_pairs={{0,4},{4,0},{1,5},{5,1},{2,6},{6,2},{3,7},{7,3},{8,12},{12,8},{9,1... | collective-permute-start | bytes 129032 | tf_op jit(solution)/shard_map/ppermute | solution.py:31
  11.7 0.6 copy-start.4
  11.8 0.6 copy-start.5
  11.8 0.7 copy-start
  14.3 5.2 %collective-permute-start.7 = (f32[80,128]{1,0:T(8,128)}, f32[80,128]{1,0:T(8,128)S(1)}, u32[]{:S(2)}, u32[]{:S(2)}) collective-permute-start(f32[80,128]{1,0:T(8,128)} %strain.1), channel_id=1, source_target_pairs={{0,24},{8,16},{16,8},{24,0},{1,25},{9,17},{17,9},{25,1},{2,26},{10... | collective-permute-start | bytes 122888 | tf_op jit(solution)/shard_map/ppermute | solution.py:47
  16.0 4.3 %collective-permute-start.6 = (f32[80,128]{1,0:T(8,128)}, f32[80,128]{1,0:T(8,128)S(1)}, u32[]{:S(2)}, u32[]{:S(2)}) collective-permute-start(f32[80,128]{1,0:T(8,128)} %strain.1), channel_id=1, source_target_pairs={{0,16},{8,24},{16,0},{24,8},{1,17},{9,25},{17,1},{25,9},{2,18},{10... | collective-permute-start | bytes 122888 | tf_op jit(solution)/shard_map/ppermute | solution.py:47
  17.5 4.2 %collective-permute-start.5 = (f32[80,128]{1,0:T(8,128)}, f32[80,128]{1,0:T(8,128)S(1)}, u32[]{:S(2)}, u32[]{:S(2)}) collective-permute-start(f32[80,128]{1,0:T(8,128)} %strain.1), channel_id=1, source_target_pairs={{0,8},{8,0},{16,24},{24,16},{1,9},{9,1},{17,25},{25,17},{2,10},{10... | collective-permute-start | bytes 122888 | tf_op jit(solution)/shard_map/ppermute | solution.py:47
  19.6 2.2 %copy-start.6 = (f32[80,128]{1,0:T(8,128)}, f32[80,128]{1,0:T(8,128)S(1)}, u32[]{:S(2)}) copy-start(f32[80,128]{1,0:T(8,128)S(1)} %collective-permute-done.7.refs_2_.refs_5_) | copy-start | bytes 122884
  20.3 1.4 %copy-start.7 = (f32[80,128]{1,0:T(8,128)}, f32[80,128]{1,0:T(8,128)S(1)}, u32[]{:S(2)}) copy-start(f32[80,128]{1,0:T(8,128)S(1)} %collective-permute-done.6.refs_1_.refs_4_) | copy-start | bytes 122884
  21.7 0.6 copy-start.8
  28.6 7.4 %collective-permute-start.8 = (f32[3,4,16,256]{3,2,1,0:T(8,128)}, f32[3,4,16,256]{3,2,1,0:T(8,128)S(1)}, u32[]{:S(2)}, u32[]{:S(2)}) collective-permute-start(f32[3,4,16,256]{3,2,1,0:T(8,128)} %get-tuple-element.23.refs_0_), channel_id=1, source_target_pairs={{0,4},{4,0},{1,5},{5,1},{2,6},{6,2},{3,7},{7,3},{8,12},{12,8},{9,1... | collective-permute-start | bytes 589832 | tf_op jit(solution)/shard_map/ppermute | solution.py:31
  28.6 4.3 %collective-permute-start.9 = (f32[36,256]{1,0:T(8,128)}, f32[36,256]{1,0:T(8,128)S(1)}, u32[]{:S(2)}, u32[]{:S(2)}) collective-permute-start(f32[36,256]{1,0:T(8,128)} %get-tuple-element.24), channel_id=1, source_target_pairs={{0,1},{1,0},{2,3},{3,2},{4,5},{5,4},{6,7},{7,6},{8,9},{9,8},{10,11... | collective-permute-start | bytes 110600 | tf_op jit(solution)/shard_map/ppermute | solution.py:31
  28.7 6.1 %collective-permute-start.10 = (f32[36,256]{1,0:T(8,128)}, f32[36,256]{1,0:T(8,128)S(1)}, u32[]{:S(2)}, u32[]{:S(2)}) collective-permute-start(f32[36,256]{1,0:T(8,128)} %get-tuple-element.25), channel_id=1, source_target_pairs={{0,3},{1,2},{2,1},{3,0},{4,7},{5,6},{6,5},{7,4},{8,11},{9,10},{10,... | collective-permute-start | bytes 110600 | tf_op jit(solution)/shard_map/ppermute | solution.py:35
  32.9 3.1 %copy-start.10 = (f32[36,256]{1,0:T(8,128)}, f32[36,256]{1,0:T(8,128)S(1)}, u32[]{:S(2)}) copy-start(f32[36,256]{1,0:T(8,128)S(1)} %collective-permute-done.9.refs_2_) | copy-start | bytes 110596
  32.9 1.9 %collective-permute-start.11 = (f32[36,256]{1,0:T(8,128)S(1)}, f32[36,256]{1,0:T(8,128)S(1)}, u32[]{:S(2)}, u32[]{:S(2)}) collective-permute-start(f32[36,256]{1,0:T(8,128)S(1)} %collective-permute-done.9.refs_2_), channel_id=1, source_target_pairs={{0,4},{4,0},{1,5},{5,1},{2,6},{6,2},{3,7},{7,3},{8,12},{12,8},{9,1... | collective-permute-start | bytes 110600 | tf_op jit(solution)/shard_map/ppermute | solution.py:31
  34.7 1.2 %copy-start.11 = (f32[36,256]{1,0:T(8,128)}, f32[36,256]{1,0:T(8,128)S(1)}, u32[]{:S(2)}) copy-start(f32[36,256]{1,0:T(8,128)S(1)} %collective-permute-done.10.refs_3_) | copy-start | bytes 110596
  34.8 1.2 %collective-permute-start.12 = (f32[36,256]{1,0:T(8,128)S(1)}, f32[36,256]{1,0:T(8,128)S(1)}, u32[]{:S(2)}, u32[]{:S(2)}) collective-permute-start(f32[36,256]{1,0:T(8,128)S(1)} %collective-permute-done.10.refs_3_), channel_id=1, source_target_pairs={{0,4},{4,0},{1,5},{5,1},{2,6},{6,2},{3,7},{7,3},{8,12},{12,8},{9,1... | collective-permute-start | bytes 110600 | tf_op jit(solution)/shard_map/ppermute | solution.py:31
  34.8 1.2 %copy-start.12 = (f32[36,256]{1,0:T(8,128)}, f32[36,256]{1,0:T(8,128)S(1)}, u32[]{:S(2)}) copy-start(f32[36,256]{1,0:T(8,128)S(1)} %collective-permute-done.11.refs_4_) | copy-start | bytes 110596
  36.0 0.6 copy-start.13
  36.0 0.7 copy-start.1
  38.5 5.2 %collective-permute-start.15 = (f32[64,128]{1,0:T(8,128)}, f32[64,128]{1,0:T(8,128)S(1)}, u32[]{:S(2)}, u32[]{:S(2)}) collective-permute-start(f32[64,128]{1,0:T(8,128)} %get-tuple-element.27), channel_id=1, source_target_pairs={{0,24},{8,16},{16,8},{24,0},{1,25},{9,17},{17,9},{25,1},{2,26},{10... | collective-permute-start | bytes 98312 | tf_op jit(solution)/shard_map/ppermute | solution.py:47
  41.6 4.1 %collective-permute-start.14 = (f32[64,128]{1,0:T(8,128)}, f32[64,128]{1,0:T(8,128)S(1)}, u32[]{:S(2)}, u32[]{:S(2)}) collective-permute-start(f32[64,128]{1,0:T(8,128)} %get-tuple-element.27), channel_id=1, source_target_pairs={{0,16},{8,24},{16,0},{24,8},{1,17},{9,25},{17,1},{25,9},{2,18},{10... | collective-permute-start | bytes 98312 | tf_op jit(solution)/shard_map/ppermute | solution.py:47
  41.9 4.1 %collective-permute-start.13 = (f32[64,128]{1,0:T(8,128)}, f32[64,128]{1,0:T(8,128)S(1)}, u32[]{:S(2)}, u32[]{:S(2)}) collective-permute-start(f32[64,128]{1,0:T(8,128)} %get-tuple-element.27), channel_id=1, source_target_pairs={{0,8},{8,0},{16,24},{24,16},{1,9},{9,1},{17,25},{25,17},{2,10},{10... | collective-permute-start | bytes 98312 | tf_op jit(solution)/shard_map/ppermute | solution.py:47
  43.7 2.4 %copy-start.14 = (f32[64,128]{1,0:T(8,128)}, f32[64,128]{1,0:T(8,128)S(1)}, u32[]{:S(2)}) copy-start(f32[64,128]{1,0:T(8,128)S(1)} %collective-permute-done.15.refs_2_) | copy-start | bytes 98308
  45.7 0.6 copy-start.15
  46.3 0.6 copy-start.16
  48.5 7.7 %collective-permute-start.16 = (f32[1,4,16,128]{3,2,1,0:T(8,128)}, f32[1,4,16,128]{3,2,1,0:T(8,128)S(1)}, u32[]{:S(2)}, u32[]{:S(2)}) collective-permute-start(f32[1,4,16,128]{3,2,1,0:T(8,128)} %get-tuple-element.28.refs_0_), channel_id=1, source_target_pairs={{0,4},{4,0},{1,5},{5,1},{2,6},{6,2},{3,7},{7,3},{8,12},{12,8},{9,1... | collective-permute-start | bytes 98312 | tf_op jit(solution)/shard_map/ppermute | solution.py:31
  48.5 3.9 %collective-permute-start.17 = (f32[12,128]{1,0:T(8,128)}, f32[12,128]{1,0:T(8,128)S(1)}, u32[]{:S(2)}, u32[]{:S(2)}) collective-permute-start(f32[12,128]{1,0:T(8,128)} %get-tuple-element.29), channel_id=1, source_target_pairs={{0,1},{1,0},{2,3},{3,2},{4,5},{5,4},{6,7},{7,6},{8,9},{9,8},{10,11... | collective-permute-start | bytes 18440 | tf_op jit(solution)/shard_map/ppermute | solution.py:31
  49.3 5.7 %collective-permute-start.18 = (f32[12,128]{1,0:T(8,128)}, f32[12,128]{1,0:T(8,128)S(1)}, u32[]{:S(2)}, u32[]{:S(2)}) collective-permute-start(f32[12,128]{1,0:T(8,128)} %get-tuple-element.30), channel_id=1, source_target_pairs={{0,3},{1,2},{2,1},{3,0},{4,7},{5,6},{6,5},{7,4},{8,11},{9,10},{10,... | collective-permute-start | bytes 18440 | tf_op jit(solution)/shard_map/ppermute | solution.py:35
  52.3 3.8 %copy-start.18 = (f32[12,128]{1,0:T(8,128)}, f32[12,128]{1,0:T(8,128)S(1)}, u32[]{:S(2)}) copy-start(f32[12,128]{1,0:T(8,128)S(1)} %collective-permute-done.17.refs_2_) | copy-start | bytes 18436
  52.3 2.6 %collective-permute-start.19 = (f32[12,128]{1,0:T(8,128)S(1)}, f32[12,128]{1,0:T(8,128)S(1)}, u32[]{:S(2)}, u32[]{:S(2)}) collective-permute-start(f32[12,128]{1,0:T(8,128)S(1)} %collective-permute-done.17.refs_2_), channel_id=1, source_target_pairs={{0,4},{4,0},{1,5},{5,1},{2,6},{6,2},{3,7},{7,3},{8,12},{12,8},{9,1... | collective-permute-start | bytes 18440 | tf_op jit(solution)/shard_map/ppermute | solution.py:31
  54.9 1.2 %copy-start.19 = (f32[12,128]{1,0:T(8,128)}, f32[12,128]{1,0:T(8,128)S(1)}, u32[]{:S(2)}) copy-start(f32[12,128]{1,0:T(8,128)S(1)} %collective-permute-done.18.refs_3_) | copy-start | bytes 18436
  55.0 1.2 %collective-permute-start.20 = (f32[12,128]{1,0:T(8,128)S(1)}, f32[12,128]{1,0:T(8,128)S(1)}, u32[]{:S(2)}, u32[]{:S(2)}) collective-permute-start(f32[12,128]{1,0:T(8,128)S(1)} %collective-permute-done.18.refs_3_), channel_id=1, source_target_pairs={{0,4},{4,0},{1,5},{5,1},{2,6},{6,2},{3,7},{7,3},{8,12},{12,8},{9,1... | collective-permute-start | bytes 18440 | tf_op jit(solution)/shard_map/ppermute | solution.py:31
  55.0 1.2 %copy-start.20 = (f32[12,128]{1,0:T(8,128)}, f32[12,128]{1,0:T(8,128)S(1)}, u32[]{:S(2)}) copy-start(f32[12,128]{1,0:T(8,128)S(1)} %collective-permute-done.19.refs_4_) | copy-start | bytes 18436
  56.1 0.6 copy-start.21
  56.1 0.6 copy-start.17
  63.7 1.4 %collective-permute-start.21 = (f32[8,128]{1,0:T(8,128)}, f32[8,128]{1,0:T(8,128)S(1)}, u32[]{:S(2)}, u32[]{:S(2)}) collective-permute-start(f32[8,128]{1,0:T(8,128)} %get-tuple-element.33.refs_1_), channel_id=1, source_target_pairs={{0,4},{4,0},{1,5},{5,1},{2,6},{6,2},{3,7},{7,3},{8,12},{12,8},{9,1... | collective-permute-start | bytes 12296 | tf_op jit(solution)/shard_map/ppermute | solution.py:31
  65.7 7.0 %collective-permute-start.24 = (f32[2,8,128]{2,1,0:T(8,128)S(1)}, f32[2,8,128]{2,1,0:T(8,128)S(1)}, u32[]{:S(2)}, u32[]{:S(2)}) collective-permute-start(f32[2,8,128]{2,1,0:T(8,128)S(1)} %pad_maximum_fusion), channel_id=1, source_target_pairs={{0,3},{1,2},{2,1},{3,0},{4,7},{5,6},{6,5},{7,4},{8,11},{9,10},{10,... | collective-permute-start | bytes 24584 | tf_op jit(solution)/shard_map/ppermute | solution.py:47
  68.2 4.5 %collective-permute-start.23 = (f32[2,8,128]{2,1,0:T(8,128)S(1)}, f32[2,8,128]{2,1,0:T(8,128)S(1)}, u32[]{:S(2)}, u32[]{:S(2)}) collective-permute-start(f32[2,8,128]{2,1,0:T(8,128)S(1)} %pad_maximum_fusion), channel_id=1, source_target_pairs={{0,2},{1,3},{2,0},{3,1},{4,6},{5,7},{6,4},{7,5},{8,10},{9,11},{10,... | collective-permute-start | bytes 24584 | tf_op jit(solution)/shard_map/ppermute | solution.py:47
  68.2 3.7 %collective-permute-start.22 = (f32[2,8,128]{2,1,0:T(8,128)S(1)}, f32[2,8,128]{2,1,0:T(8,128)S(1)}, u32[]{:S(2)}, u32[]{:S(2)}) collective-permute-start(f32[2,8,128]{2,1,0:T(8,128)S(1)} %pad_maximum_fusion), channel_id=1, source_target_pairs={{0,1},{1,0},{2,3},{3,2},{4,5},{5,4},{6,7},{7,6},{8,9},{9,8},{10,11... | collective-permute-start | bytes 24584 | tf_op jit(solution)/shard_map/ppermute | solution.py:47
  72.8 0.6 copy-start.9

commit v2 on v1

--- a/solution.py
+++ b/solution.py
@@ -15,6 +15,7 @@
 
 H = 3
 TOP = 8
+GRANT = 16 * 1024 * 1024
 f32 = jnp.float32
 bf16 = jnp.bfloat16
 
@@ -62,10 +63,11 @@
     return pl.pallas_call(
         expanded,
         name=name,
-        out_shape=[jax.ShapeDtypeStruct(o, f32) for o in outs],
+        out_shape=[o if hasattr(o, "dtype") else jax.ShapeDtypeStruct(o, f32) for o in outs],
         in_specs=[vmem] * len(unique),
         out_specs=[vmem] * len(outs),
         scratch_shapes=list(scratch),
+        compiler_params=pltpu.CompilerParams(vmem_limit_bytes=GRANT),
     )(*unique)
 
 
@@ -190,6 +192,16 @@
     high, low = split(stacked)
     dot = functools.partial(jnp.dot, preferred_element_type=f32)
     return dot(k_high[...], high) + dot(k_high[...], low) + dot(k_low[...], high)
+
+
+def spread_stiffness(stiffness, k_high, k_low):
+    n = 8 * stiffness.shape[0]
+    pick = jnp.where(sub((n, n // 8)) // 8 == lane((n, n // 8)), 1.0, 0.0).astype(bf16)
+    keep = (sub((n, n)) & 7) == (lane((n, n)) & 7)
+    for term, out in zip(split(stiffness[...]), (k_high, k_low)):
+        tall = jnp.dot(pick, term, preferred_element_type=f32).astype(bf16)
+        wide = lax.dot_general(tall, pick, (((1,), (1,)), ((), ())), preferred_element_type=f32)
+        out[...] = jnp.where(keep, wide, 0.0).astype(bf16)
 
 
 def add_apply(nodes, weight, out, k_high, k_low, first, last):
@@ -330,8 +342,8 @@
     k = at.groups - 1
     got, refs = refs[:k], refs[k:]
     p, src, sto, well, host = refs[:5]
-    tile, xa, xb, ya, yb, xyaa, xyab, xyba, xybb, k_high, k_low = refs[5:16]
-    out, out_a, out_b, g0, we, ext, acc, table = refs[16:]
+    tile, xa, xb, ya, yb, xyaa, xyab, xyba, xybb, stiffness = refs[5:15]
+    out, out_a, out_b, g0, we, k_high, k_low, ext, acc, table = refs[15:]
     size_x, size_y = p.shape[0], p.shape[1]
     rows = size_x * size_y
 
@@ -385,6 +397,7 @@
     def _():
         extend(at, ext, tile, xa, xb, ya, yb, (xyaa, xyab), (xyba, xybb), 7, size_x, size_y)
         we[...] = ext[6]
+        spread_stiffness(stiffness, k_high, k_low)
         add_apply(ext, we, acc, k_high, k_low, 1, size_x + 5)
         for m in range(3):
             for x in range(2, size_x + 5):
@@ -574,13 +587,20 @@
         e11 = total_of(e11) + spring_coef * qq
         e12 = total_of(e12) + spring_coef * rq
         e22 = total_of(e22) + spring_coef * rr
+        line = sub((8, 128))
+        value = jnp.zeros((8, 128), f32)
         for i, v in enumerate((rr, shift, rq, qq, e11, e12, e22)):
-            scal[i : i + 1, :] = jnp.broadcast_to(v, (1, 128))
-        scal[7:8, :] = jnp.zeros((1, 128), f32)
-
-
-def final_body(scals, own, r, q, u, out):
+            value = jnp.where(line == i, v, value)
+        if scal.shape[0] == 8:
+            scal[...] = value
+        else:
+            scal[0:8] = jnp.where(at.xodd, 0.0, value)
+            scal[8:16] = jnp.where(at.xodd, value, 0.0)
+
+
+def final_body(*refs):
     at = Place()
+    scals, own, r, q, u, out = refs[:-5], *refs[-5:]
 
     @pl.when(~at.mech)
     def _():
@@ -588,16 +608,16 @@
 
     @pl.when(at.mech)
     def _():
-        count = scals.shape[0]
-        get = lambda d, i: scals[d, i : i + 1, :]
-        total = lambda fn: functools.reduce(lambda a, b: a + b, [fn(d) for d in range(count)])
-        rr = total(lambda d: get(d, 0))
-        mean = total(lambda d: get(d, 2) + get(d, 1) * get(d, 0)) / rr
+        parts = [s[8 * i : 8 * i + 8] for s in scals for i in range(s.shape[0] // 8)]
+        get = lambda part, i: part[i : i + 1]
+        total = lambda fn: functools.reduce(lambda a, b: a + b, [fn(p) for p in parts])
+        rr = total(lambda p: get(p, 0))
+        mean = total(lambda p: get(p, 2) + get(p, 1) * get(p, 0)) / rr
 
         def shifted(low, mid, high):
-            def one(d):
-                gap = get(d, 1) - mean
-                return get(d, high) + gap * (2.0 * get(d, mid) + gap * get(d, low))
+            def one(p):
+                gap = get(p, 1) - mean
+                return get(p, high) + gap * (2.0 * get(p, mid) + gap * get(p, low))
 
             return total(one)
 
@@ -606,8 +626,10 @@
         ratio = qq / (mean * mean * rr)
         curve = energy / (mean * mean) - ratio * ratio * mean * rr
         second = ratio * rr / curve
-        gap = own[1:2, :] - mean
-        by_r = 1.0 / mean + second * (ratio - gap / mean)
+        shift = own[1:2]
+        if own.shape[0] == 16:
+            shift = jnp.where(at.xodd, own[9:10], shift)
+        by_r = 1.0 / mean + second * (ratio - (shift - mean) / mean)
         by_q = -second / mean
         out[...] = u[...] + by_r[None, None] * r[...] + by_q[None, None] * q[...]
 
@@ -641,10 +663,7 @@
     basis = basis_weight[0].reshape(8 * rows, size_z)
     u, body = displacement[0], body_force[0]
     nx, ny = size_x + 2 * H, size_y + 2 * TOP
-    kron = (stiffness[:, None, :, None] * jnp.eye(8, dtype=f32)[None, :, None, :]).reshape(192, 192)
-    k_high = lax.reduce_precision(kron, 8, 7)
-    k_low = (kron - k_high).astype(bf16)
-    k_high = k_high.astype(bf16)
+    kron = jax.ShapeDtypeStruct((8 * stiffness.shape[0],) * 2, bf16)
 
     msg = (7 * size_x * H, size_z)
     tile, ya, yb, zmsg = call(
@@ -663,11 +682,11 @@
     )
     got = by_xor(line, "grp")
     msg = (3 * size_x * H, 2 * size_z)
-    cells, ya, yb, g0, we = call(
+    cells, ya, yb, g0, we, k_high, k_low = call(
         gather_body,
         "gather",
-        [(3, size_x, size_y, 2 * size_z), msg, msg, (3, nx, ny, size_z), (nx, ny, size_z)],
-        *got, p, src, sto, well, host, tile, *near, k_high, k_low,
+        [(3, size_x, size_y, 2 * size_z), msg, msg, (3, nx, ny, size_z), (nx, ny, size_z), kron, kron],
+        *got, p, src, sto, well, host, tile, *near, stiffness,
         scratch=[
             pltpu.VMEM((7, nx, ny, size_z), f32),
             pltpu.VMEM((3, nx, ny, size_z), f32),
@@ -696,10 +715,11 @@
     )
     near = neighbours(elem, ya, yb)
     own = (3, size_x, size_y, size_z)
+    duo = lax.axis_size("gx") == 2
     r, q, scal = call(
         krylov_body,
         "krylov",
-        [own, own, (8, size_z)],
+        [own, own, (16 if duo else 8, size_z)],
         elem, *near, g0, we, k_high, k_low,
         scratch=[
             pltpu.VMEM((1, nx, ny, size_z), f32),
@@ -707,12 +727,12 @@
             pltpu.VMEM((3, nx, ny, size_z), f32),
         ],
     )
-    if lax.axis_size("gx") == 2:
-        duo = jnp.stack([scal, swap_a(scal, "gx")])
-        scals = jnp.concatenate([duo] + by_xor(duo, "gy"))
+    if duo:
+        pair = scal + swap_a(scal, "gx")
+        scals = [pair] + by_xor(pair, "gy")
     else:
-        scals = lax.all_gather(scal, ("gx", "gy"))
-    (moved,) = call(final_body, "final", [own], scals, scal, r, q, u)
+        scals = [lax.all_gather(scal, ("gx", "gy"), tiled=True)]
+    (moved,) = call(final_body, "final", [own], *scals, scal, r, q, u)
     return (updated[None], moved[None])
 
 

time: 75.6 us -> 65.4 us (0.87)
  Pallas kernels: 21.9 us -> 10.9 us
  other arithmetic: 2.32 us -> 0.01 us
  local copies, waits for them, and re-layouts: 5.44 us -> 7.12 us
  waiting for transfers between devices: 22.5 us -> 23.8 us
    pallas_call x7, Pallas kernels: 21.9 us -> 10.9 us  [call(): pl.pallas_call(expanded, name=name, out_shape=[o if hasattr(o, 'dtype') e...]
    unnamed x48 -> x32, local copies, waits for them, and re-layouts: 4.76 us -> 7.12 us
    mul x1 -> x0, other arithmetic: 0.94 us -> none  [local(): stiffness[:, None, :, None] * jnp.eye(8, dtype=f32)[None, :, None, :]]
    ppermute x13, waiting for transfers between devices: 5.33 us -> 6.16 us  [swap_a(): return lax.ppermute(value, axis, pairs_a(lax.axis_size(axis)))]
  transfers between devices with their start and end apart: 25 -> 25, of which waited for: 17 -> 17; matrix products, arithmetic and copies ran while one was open for 4% -> 0% of each run, Pallas kernels for 0% -> 0%
where the time goes in v2:
time: 65.4 us; the launch traced here: 64.8 us
  waiting for transfers between devices  23.8 us (36%)
  starting transfers between devices  22.2 us (34%)
  Pallas kernels  10.9 us (17%)
  local copies, waits for them, and re-layouts  7.12 us (11%)
  between operations  0.79 us (1%)
    ppermute x9, starting transfers between devices, by_xor(): lax.ppermute(value, axis, [(i, i ^ k) for i in range(n)])  11.4 us
    pallas_call x7, Pallas kernels, call(): pl.pallas_call(expanded, name=name, out_shape=[o if hasattr(o, 'dtype') e...  10.9 us
    ppermute x9, waiting for transfers between devices, by_xor(): lax.ppermute(value, axis, [(i, i ^ k) for i in range(n)])  9.67 us
    ppermute x3, waiting for transfers between devices, swap_b(): return lax.ppermute(value, axis, pairs_b(lax.axis_size(axis)))  7.96 us
    ppermute x3, starting transfers between devices, swap_b(): return lax.ppermute(value, axis, pairs_b(lax.axis_size(axis)))  7.91 us
    unnamed x32, local copies, waits for them, and re-layouts  7.12 us
    ppermute x13, waiting for transfers between devices, swap_a(): return lax.ppermute(value, axis, pairs_a(lax.axis_size(axis)))  6.16 us
    ppermute x13, starting transfers between devices, swap_a(): return lax.ppermute(value, axis, pairs_a(lax.axis_size(axis)))  2.84 us
  transfers between devices with their start and end apart: 25, of which 17 were waited for; matrix products, arithmetic and copies ran while one was open for 0% of the time, Pallas kernels for 0%

profile of v2, /device:TPU:6, one launch (start us, length us, event | category | flops | bytes accessed | tf_op | source)
XLA Modules:
  0.0 64.8 jit_solution(7007949240054751328)
XLA Ops:
  0.6 0.7 %copy-done = s32[1,4,16,128]{3,2,1,0:T(8,128)S(1)} copy-done((s32[1,4,16,128]{3,2,1,0:T(8,128)S(1)}, s32[1,4,16,128]{3,2,1,0:T(8,128)}, u32[]{:S(2)}) %copy-start) | copy-done | bytes 32792
  1.4 0.9 %copy-done.2 = f32[1,3,4,16,128]{4,3,2,1,0:T(8,128)S(1)} copy-done((f32[1,3,4,16,128]{4,3,2,1,0:T(8,128)S(1)}, f32[1,3,4,16,128]{4,3,2,1,0:T(8,128)}, u32[]{:S(2)}) %copy-start.2) | copy-done | bytes 98328
  2.3 0.8 %copy-done.4 = s32[1,4,16,128]{3,2,1,0:T(8,128)S(1)} copy-done((s32[1,4,16,128]{3,2,1,0:T(8,128)S(1)}, s32[1,4,16,128]{3,2,1,0:T(8,128)}, u32[]{:S(2)}) %copy-start.4) | copy-done | bytes 32792
  3.0 0.8 %copy-done.6 = f32[1,4,16,128]{3,2,1,0:T(8,128)S(1)} copy-done((f32[1,4,16,128]{3,2,1,0:T(8,128)S(1)}, f32[1,4,16,128]{3,2,1,0:T(8,128)}, u32[]{:S(2)}) %copy-start.6) | copy-done | bytes 32792
  3.8 0.8 %copy-done.7 = s32[1,4,16,128]{3,2,1,0:T(8,128)S(1)} copy-done((s32[1,4,16,128]{3,2,1,0:T(8,128)S(1)}, s32[1,4,16,128]{3,2,1,0:T(8,128)}, u32[]{:S(2)}) %copy-start.7) | copy-done | bytes 32792
  4.6 0.8 %copy-done.10 = f32[1,4,16,128]{3,2,1,0:T(8,128)S(1)} copy-done((f32[1,4,16,128]{3,2,1,0:T(8,128)S(1)}, f32[1,4,16,128]{3,2,1,0:T(8,128)}, u32[]{:S(2)}) %copy-start.10) | copy-done | bytes 32792
  5.3 0.8 %copy-done.11 = f32[1,4,16,128]{3,2,1,0:T(8,128)S(1)} copy-done((f32[1,4,16,128]{3,2,1,0:T(8,128)S(1)}, f32[1,4,16,128]{3,2,1,0:T(8,128)}, u32[]{:S(2)}) %copy-start.11) | copy-done | bytes 32792
  6.1 0.9 %copy-done.12 = f32[1,3,4,16,128]{4,3,2,1,0:T(8,128)S(1)} copy-done((f32[1,3,4,16,128]{4,3,2,1,0:T(8,128)S(1)}, f32[1,3,4,16,128]{4,3,2,1,0:T(8,128)}, u32[]{:S(2)}) %copy-start.12) | copy-done | bytes 98328
  7.0 0.8 %copy-done.13 = f32[1,4,16,128]{3,2,1,0:T(8,128)S(1)} copy-done((f32[1,4,16,128]{3,2,1,0:T(8,128)S(1)}, f32[1,4,16,128]{3,2,1,0:T(8,128)}, u32[]{:S(2)}) %copy-start.13) | copy-done | bytes 32792
  7.8 0.1 collective-permute-start
  7.9 1.6 %collective-permute-start.1 = (f32[84,128]{1,0:T(8,128)S(1)}, f32[84,128]{1,0:T(8,128)S(1)}, u32[]{:S(2)}, u32[]{:S(2)}) collective-permute-start(f32[84,128]{1,0:T(8,128)S(1)} %get-tuple-element.22), channel_id=1, source_target_pairs={{0,1},{1,0},{2,3},{3,2},{4,5},{5,4},{6,7},{7,6},{8,9},{9,8},{10,11... | collective-permute-start | bytes 129032 | tf_op jit(solution)/shard_map/ppermute | solution.py:32
  9.5 2.5 %collective-permute-start.2 = (f32[84,128]{1,0:T(8,128)S(1)}, f32[84,128]{1,0:T(8,128)S(1)}, u32[]{:S(2)}, u32[]{:S(2)}) collective-permute-start(f32[84,128]{1,0:T(8,128)S(1)} %get-tuple-element.23), channel_id=1, source_target_pairs={{0,3},{1,2},{2,1},{3,0},{4,7},{5,6},{6,5},{7,4},{8,11},{9,10},{10,... | collective-permute-start | bytes 129032 | tf_op jit(solution)/shard_map/ppermute | solution.py:36
  12.0 3.4 %collective-permute-done.2.refs_3_.refs_11_ = f32[84,128]{1,0:T(8,128)S(1)} collective-permute-done((f32[84,128]{1,0:T(8,128)S(1)}, f32[84,128]{1,0:T(8,128)S(1)}, u32[]{:S(2)}, u32[]{:S(2)}) %collective-permute-start.2) | collective-permute-done | bytes 43040 | tf_op jit(solution)/shard_map/ppermute | solution.py:36
  15.3 1.2 %collective-permute-done.4.refs_5_.refs_13_ = f32[84,128]{1,0:T(8,128)S(1)} collective-permute-done((f32[84,128]{1,0:T(8,128)S(1)}, f32[84,128]{1,0:T(8,128)S(1)}, u32[]{:S(2)}, u32[]{:S(2)}) %collective-permute-start.4) | collective-permute-done | bytes 43040 | tf_op jit(solution)/shard_map/ppermute | solution.py:32
  16.6 0.1 strain.1
  16.8 1.7 %collective-permute-start.7 = (f32[80,128]{1,0:T(8,128)S(1)}, f32[80,128]{1,0:T(8,128)S(1)}, u32[]{:S(2)}, u32[]{:S(2)}) collective-permute-start(f32[80,128]{1,0:T(8,128)S(1)} %strain.1), channel_id=1, source_target_pairs={{0,24},{8,16},{16,8},{24,0},{1,25},{9,17},{17,9},{25,1},{2,26},{10... | collective-permute-start | bytes 122888 | tf_op jit(solution)/shard_map/ppermute | solution.py:48
  18.5 1.5 %collective-permute-start.6 = (f32[80,128]{1,0:T(8,128)S(1)}, f32[80,128]{1,0:T(8,128)S(1)}, u32[]{:S(2)}, u32[]{:S(2)}) collective-permute-start(f32[80,128]{1,0:T(8,128)S(1)} %strain.1), channel_id=1, source_target_pairs={{0,16},{8,24},{16,0},{24,8},{1,17},{9,25},{17,1},{25,9},{2,18},{10... | collective-permute-start | bytes 122888 | tf_op jit(solution)/shard_map/ppermute | solution.py:48
  20.0 0.3 collective-permute-start.5
  20.3 1.5 %collective-permute-done.7.refs_2_.refs_5_ = f32[80,128]{1,0:T(8,128)S(1)} collective-permute-done((f32[80,128]{1,0:T(8,128)S(1)}, f32[80,128]{1,0:T(8,128)S(1)}, u32[]{:S(2)}, u32[]{:S(2)}) %collective-permute-start.7) | collective-permute-done | bytes 40992 | tf_op jit(solution)/shard_map/ppermute | solution.py:48
  21.8 0.6 %collective-permute-done.6.refs_1_.refs_4_ = f32[80,128]{1,0:T(8,128)S(1)} collective-permute-done((f32[80,128]{1,0:T(8,128)S(1)}, f32[80,128]{1,0:T(8,128)S(1)}, u32[]{:S(2)}, u32[]{:S(2)}) %collective-permute-start.6) | collective-permute-done | bytes 40992 | tf_op jit(solution)/shard_map/ppermute | solution.py:48
  22.5 1.5 %collective-permute-done.5.refs_0_.refs_3_ = f32[80,128]{1,0:T(8,128)S(1)} collective-permute-done((f32[80,128]{1,0:T(8,128)S(1)}, f32[80,128]{1,0:T(8,128)S(1)}, u32[]{:S(2)}, u32[]{:S(2)}) %collective-permute-start.5) | collective-permute-done | bytes 40992 | tf_op jit(solution)/shard_map/ppermute | solution.py:48
  24.0 4.3 %gather.1 = (f32[3,4,16,256]{3,2,1,0:T(8,128)S(1)}, f32[36,256]{1,0:T(8,128)S(1)}, f32[36,256]{1,0:T(8,128)S(1)}, f32[3,10,32,128]{3,2,1,0:T(8,128)S(1)}, f32[10...) custom-call(f32[80,128]{1,0:T(8,128)S(1)} %collective-permute-done.5.refs_0_.refs_3_, ...), custom_call_target="tpu_custom_call" | custom-call | tf_op jit(solution)/shard_map/gather/pallas_call | solution.py:63
  28.3 0.1 collective-permute-start.8
  28.4 0.1 collective-permute-start.9
  28.5 3.2 %collective-permute-start.10 = (f32[36,256]{1,0:T(8,128)S(1)}, f32[36,256]{1,0:T(8,128)S(1)}, u32[]{:S(2)}, u32[]{:S(2)}) collective-permute-start(f32[36,256]{1,0:T(8,128)S(1)} %get-tuple-element.27), channel_id=1, source_target_pairs={{0,3},{1,2},{2,1},{3,0},{4,7},{5,6},{6,5},{7,4},{8,11},{9,10},{10,... | collective-permute-start | bytes 110600 | tf_op jit(solution)/shard_map/ppermute | solution.py:36
  31.6 0.8 %collective-permute-done.9.refs_2_ = f32[36,256]{1,0:T(8,128)S(1)} collective-permute-done((f32[36,256]{1,0:T(8,128)S(1)}, f32[36,256]{1,0:T(8,128)S(1)}, u32[]{:S(2)}, u32[]{:S(2)}) %collective-permute-start.9) | collective-permute-done | bytes 36896 | tf_op jit(solution)/shard_map/ppermute | solution.py:32
  32.5 2.1 %collective-permute-done.10.refs_3_ = f32[36,256]{1,0:T(8,128)S(1)} collective-permute-done((f32[36,256]{1,0:T(8,128)S(1)}, f32[36,256]{1,0:T(8,128)S(1)}, u32[]{:S(2)}, u32[]{:S(2)}) %collective-permute-start.10) | collective-permute-done | bytes 36896 | tf_op jit(solution)/shard_map/ppermute | solution.py:36
  34.6 1.2 %collective-permute-done.12.refs_5_ = f32[36,256]{1,0:T(8,128)S(1)} collective-permute-done((f32[36,256]{1,0:T(8,128)S(1)}, f32[36,256]{1,0:T(8,128)S(1)}, u32[]{:S(2)}, u32[]{:S(2)}) %collective-permute-start.12) | collective-permute-done | bytes 36896 | tf_op jit(solution)/shard_map/ppermute | solution.py:32
  35.9 0.6 flow.1
  36.5 2.8 %collective-permute-start.15 = (f32[64,128]{1,0:T(8,128)S(1)}, f32[64,128]{1,0:T(8,128)S(1)}, u32[]{:S(2)}, u32[]{:S(2)}) collective-permute-start(f32[64,128]{1,0:T(8,128)S(1)} %get-tuple-element.29), channel_id=1, source_target_pairs={{0,24},{8,16},{16,8},{24,0},{1,25},{9,17},{17,9},{25,1},{2,26},{10... | collective-permute-start | bytes 98312 | tf_op jit(solution)/shard_map/ppermute | solution.py:48
  39.3 0.4 collective-permute-start.14
  39.7 0.3 collective-permute-start.13
  40.0 1.3 %collective-permute-done.15.refs_2_ = f32[64,128]{1,0:T(8,128)S(1)} collective-permute-done((f32[64,128]{1,0:T(8,128)S(1)}, f32[64,128]{1,0:T(8,128)S(1)}, u32[]{:S(2)}, u32[]{:S(2)}) %collective-permute-start.15) | collective-permute-done | bytes 32800 | tf_op jit(solution)/shard_map/ppermute | solution.py:48
  41.3 1.9 %collective-permute-done.14.refs_1_ = f32[64,128]{1,0:T(8,128)S(1)} collective-permute-done((f32[64,128]{1,0:T(8,128)S(1)}, f32[64,128]{1,0:T(8,128)S(1)}, u32[]{:S(2)}, u32[]{:S(2)}) %collective-permute-start.14) | collective-permute-done | bytes 32800 | tf_op jit(solution)/shard_map/ppermute | solution.py:48
  43.2 0.4 collective-permute-done.13.refs_0_
  43.7 0.7 %collective-permute-start.17 = (f32[12,128]{1,0:T(8,128)S(1)}, f32[12,128]{1,0:T(8,128)S(1)}, u32[]{:S(2)}, u32[]{:S(2)}) collective-permute-start(f32[12,128]{1,0:T(8,128)S(1)} %get-tuple-element.31), channel_id=1, source_target_pairs={{0,1},{1,0},{2,3},{3,2},{4,5},{5,4},{6,7},{7,6},{8,9},{9,8},{10,11... | collective-permute-start | bytes 18440 | tf_op jit(solution)/shard_map/ppermute | solution.py:32
  44.4 2.3 %collective-permute-start.18 = (f32[12,128]{1,0:T(8,128)S(1)}, f32[12,128]{1,0:T(8,128)S(1)}, u32[]{:S(2)}, u32[]{:S(2)}) collective-permute-start(f32[12,128]{1,0:T(8,128)S(1)} %get-tuple-element.32), channel_id=1, source_target_pairs={{0,3},{1,2},{2,1},{3,0},{4,7},{5,6},{6,5},{7,4},{8,11},{9,10},{10,... | collective-permute-start | bytes 18440 | tf_op jit(solution)/shard_map/ppermute | solution.py:36
  46.7 0.7 %collective-permute-done.17.refs_2_ = f32[12,128]{1,0:T(8,128)S(1)} collective-permute-done((f32[12,128]{1,0:T(8,128)S(1)}, f32[12,128]{1,0:T(8,128)S(1)}, u32[]{:S(2)}, u32[]{:S(2)}) %collective-permute-start.17) | collective-permute-done | bytes 6176 | tf_op jit(solution)/shard_map/ppermute | solution.py:32
  47.4 2.5 %collective-permute-done.18.refs_3_ = f32[12,128]{1,0:T(8,128)S(1)} collective-permute-done((f32[12,128]{1,0:T(8,128)S(1)}, f32[12,128]{1,0:T(8,128)S(1)}, u32[]{:S(2)}, u32[]{:S(2)}) %collective-permute-start.18) | collective-permute-done | bytes 6176 | tf_op jit(solution)/shard_map/ppermute | solution.py:36
  49.9 1.2 %collective-permute-done.20.refs_5_ = f32[12,128]{1,0:T(8,128)S(1)} collective-permute-done((f32[12,128]{1,0:T(8,128)S(1)}, f32[12,128]{1,0:T(8,128)S(1)}, u32[]{:S(2)}, u32[]{:S(2)}) %collective-permute-start.20) | collective-permute-done | bytes 6176 | tf_op jit(solution)/shard_map/ppermute | solution.py:32
  51.0 5.0 %krylov.1 = (f32[3,4,16,128]{3,2,1,0:T(8,128)S(1)}, f32[3,4,16,128]{3,2,1,0:T(8,128)S(1)}, f32[16,128]{1,0:T(8,128)S(1)}) custom-call(f32[1,4,16,128]{3,2,1,0:T(8,128)S(1)} %get-tuple-element.30.refs_0_, f32[1,4,16,128]{3,2,1,0:T(8,128)S(1)} %collective-permute-done.16.refs_1_, f32[12,128]{1,0:T(8,128)S(1)} %collective-permute-done.17.refs_2_, ...), custom_call_target="tpu_custom_call" | custom-call | tf_op jit(solution)/shard_map/krylov/pallas_call | solution.py:63
  56.1 0.2 collective-permute-start.21
  56.2 1.0 %collective-permute-done.21 = f32[16,128]{1,0:T(8,128)S(1)} collective-permute-done((f32[16,128]{1,0:T(8,128)S(1)}, f32[16,128]{1,0:T(8,128)S(1)}, u32[]{:S(2)}, u32[]{:S(2)}) %collective-permute-start.21) | collective-permute-done | bytes 8224 | tf_op jit(solution)/shard_map/ppermute | solution.py:32
  57.2 2.3 %collective-permute-start.24 = (f32[16,128]{1,0:T(8,128)S(1)}, f32[16,128]{1,0:T(8,128)S(1)}, u32[]{:S(2)}, u32[]{:S(2)}) collective-permute-start(f32[16,128]{1,0:T(8,128)S(1)} %add.3.refs_0_), channel_id=1, source_target_pairs={{0,3},{1,2},{2,1},{3,0},{4,7},{5,6},{6,5},{7,4},{8,11},{9,10},{10,... | collective-permute-start | bytes 24584 | tf_op jit(solution)/shard_map/ppermute | solution.py:48
  59.5 2.1 %collective-permute-start.22 = (f32[16,128]{1,0:T(8,128)S(1)}, f32[16,128]{1,0:T(8,128)S(1)}, u32[]{:S(2)}, u32[]{:S(2)}) collective-permute-start(f32[16,128]{1,0:T(8,128)S(1)} %add.3.refs_0_), channel_id=1, source_target_pairs={{0,1},{1,0},{2,3},{3,2},{4,5},{5,4},{6,7},{7,6},{8,9},{9,8},{10,11... | collective-permute-start | bytes 24584 | tf_op jit(solution)/shard_map/ppermute | solution.py:48
  61.6 1.1 %collective-permute-done.24.refs_3_ = f32[16,128]{1,0:T(8,128)S(1)} collective-permute-done((f32[16,128]{1,0:T(8,128)S(1)}, f32[16,128]{1,0:T(8,128)S(1)}, u32[]{:S(2)}, u32[]{:S(2)}) %collective-permute-start.24) | collective-permute-done | bytes 8224 | tf_op jit(solution)/shard_map/ppermute | solution.py:48
  62.7 1.4 %collective-permute-done.23.refs_2_ = f32[16,128]{1,0:T(8,128)S(1)} collective-permute-done((f32[16,128]{1,0:T(8,128)S(1)}, f32[16,128]{1,0:T(8,128)S(1)}, u32[]{:S(2)}, u32[]{:S(2)}) %collective-permute-start.23) | collective-permute-done | bytes 8224 | tf_op jit(solution)/shard_map/ppermute | solution.py:48
  64.1 0.7 %final.1 = f32[3,4,16,128]{3,2,1,0:T(8,128)} custom-call(f32[16,128]{1,0:T(8,128)S(1)} %add.3.refs_0_, f32[16,128]{1,0:T(8,128)S(1)} %collective-permute-done.22.refs_1_, f32[16,128]{1,0:T(8,128)S(1)} %collective-permute-done.23.refs_2_, f32[16,128]{1,0:T(8,128)S(1)} %collective-permute-done.24.refs_3_, f32[16,128]{1,0:T(8,128)S(1)} %get-tuple-element.37.refs_4_, ...), custom_call_target="tpu_custom_call" | custom-call | tf_op jit(solution)/shard_map/final/pallas_call | solution.py:63
  (42 shorter events, 0.2 us)
Async XLA Ops:
  0.6 0.8 %copy-start = (s32[1,4,16,128]{3,2,1,0:T(8,128)S(1)}, s32[1,4,16,128]{3,2,1,0:T(8,128)}, u32[]{:S(2)}) copy-start(s32[1,4,16,128]{3,2,1,0:T(8,128)} %param.18) | copy-start | bytes 98308
  1.4 0.9 %copy-start.2 = (f32[1,3,4,16,128]{4,3,2,1,0:T(8,128)S(1)}, f32[1,3,4,16,128]{4,3,2,1,0:T(8,128)}, u32[]{:S(2)}) copy-start(f32[1,3,4,16,128]{4,3,2,1,0:T(8,128)} %param.19) | copy-start | bytes 294916
  2.3 0.8 %copy-start.4 = (s32[1,4,16,128]{3,2,1,0:T(8,128)S(1)}, s32[1,4,16,128]{3,2,1,0:T(8,128)}, u32[]{:S(2)}) copy-start(s32[1,4,16,128]{3,2,1,0:T(8,128)} %param.22) | copy-start | bytes 98308
  3.0 0.8 %copy-start.6 = (f32[1,4,16,128]{3,2,1,0:T(8,128)S(1)}, f32[1,4,16,128]{3,2,1,0:T(8,128)}, u32[]{:S(2)}) copy-start(f32[1,4,16,128]{3,2,1,0:T(8,128)} %param.14) | copy-start | bytes 98308
  3.8 0.8 %copy-start.7 = (s32[1,4,16,128]{3,2,1,0:T(8,128)S(1)}, s32[1,4,16,128]{3,2,1,0:T(8,128)}, u32[]{:S(2)}) copy-start(s32[1,4,16,128]{3,2,1,0:T(8,128)} %param.15) | copy-start | bytes 98308
  4.6 0.8 %copy-start.10 = (f32[1,4,16,128]{3,2,1,0:T(8,128)S(1)}, f32[1,4,16,128]{3,2,1,0:T(8,128)}, u32[]{:S(2)}) copy-start(f32[1,4,16,128]{3,2,1,0:T(8,128)} %param.12) | copy-start | bytes 98308
  5.3 0.8 %copy-start.11 = (f32[1,4,16,128]{3,2,1,0:T(8,128)S(1)}, f32[1,4,16,128]{3,2,1,0:T(8,128)}, u32[]{:S(2)}) copy-start(f32[1,4,16,128]{3,2,1,0:T(8,128)} %param.13) | copy-start | bytes 98308
  6.1 0.9 %copy-start.12 = (f32[1,3,4,16,128]{4,3,2,1,0:T(8,128)S(1)}, f32[1,3,4,16,128]{4,3,2,1,0:T(8,128)}, u32[]{:S(2)}) copy-start(f32[1,3,4,16,128]{4,3,2,1,0:T(8,128)} %param.20) | copy-start | bytes 294916
  7.0 0.8 %copy-start.13 = (f32[1,4,16,128]{3,2,1,0:T(8,128)S(1)}, f32[1,4,16,128]{3,2,1,0:T(8,128)}, u32[]{:S(2)}) copy-start(f32[1,4,16,128]{3,2,1,0:T(8,128)} %param.21) | copy-start | bytes 98308
  7.8 8.8 %collective-permute-start = (f32[7,4,16,128]{3,2,1,0:T(8,128)S(1)}, f32[7,4,16,128]{3,2,1,0:T(8,128)S(1)}, u32[]{:S(2)}, u32[]{:S(2)}) collective-permute-start(f32[7,4,16,128]{3,2,1,0:T(8,128)S(1)} %get-tuple-element.21.refs_0_.refs_8_), channel_id=1, source_target_pairs={{0,4},{4,0},{1,5},{5,1},{2,6},{6,2},{3,7},{7,3},{8,12},{12,8},{9,1... | collective-permute-start | bytes 688136 | tf_op jit(solution)/shard_map/ppermute | solution.py:32
  7.9 4.1 %collective-permute-start.1 = (f32[84,128]{1,0:T(8,128)S(1)}, f32[84,128]{1,0:T(8,128)S(1)}, u32[]{:S(2)}, u32[]{:S(2)}) collective-permute-start(f32[84,128]{1,0:T(8,128)S(1)} %get-tuple-element.22), channel_id=1, source_target_pairs={{0,1},{1,0},{2,3},{3,2},{4,5},{5,4},{6,7},{7,6},{8,9},{9,8},{10,11... | collective-permute-start | bytes 129032 | tf_op jit(solution)/shard_map/ppermute | solution.py:32
  9.5 5.8 %collective-permute-start.2 = (f32[84,128]{1,0:T(8,128)S(1)}, f32[84,128]{1,0:T(8,128)S(1)}, u32[]{:S(2)}, u32[]{:S(2)}) collective-permute-start(f32[84,128]{1,0:T(8,128)S(1)} %get-tuple-element.23), channel_id=1, source_target_pairs={{0,3},{1,2},{2,1},{3,0},{4,7},{5,6},{6,5},{7,4},{8,11},{9,10},{10,... | collective-permute-start | bytes 129032 | tf_op jit(solution)/shard_map/ppermute | solution.py:36
  12.0 3.4 %collective-permute-start.3 = (f32[84,128]{1,0:T(8,128)S(1)}, f32[84,128]{1,0:T(8,128)S(1)}, u32[]{:S(2)}, u32[]{:S(2)}) collective-permute-start(f32[84,128]{1,0:T(8,128)S(1)} %collective-permute-done.1.refs_2_.refs_10_), channel_id=1, source_target_pairs={{0,4},{4,0},{1,5},{5,1},{2,6},{6,2},{3,7},{7,3},{8,12},{12,8},{9,1... | collective-permute-start | bytes 129032 | tf_op jit(solution)/shard_map/ppermute | solution.py:32
  15.3 1.2 %collective-permute-start.4 = (f32[84,128]{1,0:T(8,128)S(1)}, f32[84,128]{1,0:T(8,128)S(1)}, u32[]{:S(2)}, u32[]{:S(2)}) collective-permute-start(f32[84,128]{1,0:T(8,128)S(1)} %collective-permute-done.2.refs_3_.refs_11_), channel_id=1, source_target_pairs={{0,4},{4,0},{1,5},{5,1},{2,6},{6,2},{3,7},{7,3},{8,12},{12,8},{9,1... | collective-permute-start | bytes 129032 | tf_op jit(solution)/shard_map/ppermute | solution.py:32
  16.6 7.4 %copy-start.15 = (f32[24,24]{1,0:T(8,128)S(1)}, f32[24,24]{1,0:T(8,128)}, u32[]{:S(2)}) copy-start(f32[24,24]{1,0:T(8,128)} %refs_14_.1) | copy-start | bytes 6916
  16.7 19.1 %copy-start.1 = (s32[1,4,16,128]{3,2,1,0:T(8,128)S(1)}, s32[1,4,16,128]{3,2,1,0:T(8,128)}, u32[]{:S(2)}) copy-start(s32[1,4,16,128]{3,2,1,0:T(8,128)} %param.18) | copy-start | bytes 98308
  16.7 19.1 %copy-start.8 = (s32[1,4,16,128]{3,2,1,0:T(8,128)S(1)}, s32[1,4,16,128]{3,2,1,0:T(8,128)}, u32[]{:S(2)}) copy-start(s32[1,4,16,128]{3,2,1,0:T(8,128)} %param.15) | copy-start | bytes 98308
  16.7 19.1 %copy-start.9 = (f32[1,8,4,16,128]{4,3,2,1,0:T(8,128)S(1)}, f32[1,8,4,16,128]{4,3,2,1,0:T(8,128)}, u32[]{:S(2)}) copy-start(f32[1,8,4,16,128]{4,3,2,1,0:T(8,128)} %param.17) | copy-start | bytes 786436
  16.7 19.1 %copy-start.14 = (s32[1,4,16,128]{3,2,1,0:T(8,128)S(1)}, s32[1,4,16,128]{3,2,1,0:T(8,128)}, u32[]{:S(2)}) copy-start(s32[1,4,16,128]{3,2,1,0:T(8,128)} %param.16) | copy-start | bytes 98308
  16.8 5.1 %collective-permute-start.7 = (f32[80,128]{1,0:T(8,128)S(1)}, f32[80,128]{1,0:T(8,128)S(1)}, u32[]{:S(2)}, u32[]{:S(2)}) collective-permute-start(f32[80,128]{1,0:T(8,128)S(1)} %strain.1), channel_id=1, source_target_pairs={{0,24},{8,16},{16,8},{24,0},{1,25},{9,17},{17,9},{25,1},{2,26},{10... | collective-permute-start | bytes 122888 | tf_op jit(solution)/shard_map/ppermute | solution.py:48
  18.5 4.0 %collective-permute-start.6 = (f32[80,128]{1,0:T(8,128)S(1)}, f32[80,128]{1,0:T(8,128)S(1)}, u32[]{:S(2)}, u32[]{:S(2)}) collective-permute-start(f32[80,128]{1,0:T(8,128)S(1)} %strain.1), channel_id=1, source_target_pairs={{0,16},{8,24},{16,0},{24,8},{1,17},{9,25},{17,1},{25,9},{2,18},{10... | collective-permute-start | bytes 122888 | tf_op jit(solution)/shard_map/ppermute | solution.py:48
  20.0 4.0 %collective-permute-start.5 = (f32[80,128]{1,0:T(8,128)S(1)}, f32[80,128]{1,0:T(8,128)S(1)}, u32[]{:S(2)}, u32[]{:S(2)}) collective-permute-start(f32[80,128]{1,0:T(8,128)S(1)} %strain.1), channel_id=1, source_target_pairs={{0,8},{8,0},{16,24},{24,16},{1,9},{9,1},{17,25},{25,17},{2,10},{10... | collective-permute-start | bytes 122888 | tf_op jit(solution)/shard_map/ppermute | solution.py:48
  28.3 7.5 %collective-permute-start.8 = (f32[3,4,16,256]{3,2,1,0:T(8,128)S(1)}, f32[3,4,16,256]{3,2,1,0:T(8,128)S(1)}, u32[]{:S(2)}, u32[]{:S(2)}) collective-permute-start(f32[3,4,16,256]{3,2,1,0:T(8,128)S(1)} %get-tuple-element.25.refs_0_), channel_id=1, source_target_pairs={{0,4},{4,0},{1,5},{5,1},{2,6},{6,2},{3,7},{7,3},{8,12},{12,8},{9,1... | collective-permute-start | bytes 589832 | tf_op jit(solution)/shard_map/ppermute | solution.py:32
  28.4 4.1 %collective-permute-start.9 = (f32[36,256]{1,0:T(8,128)S(1)}, f32[36,256]{1,0:T(8,128)S(1)}, u32[]{:S(2)}, u32[]{:S(2)}) collective-permute-start(f32[36,256]{1,0:T(8,128)S(1)} %get-tuple-element.26), channel_id=1, source_target_pairs={{0,1},{1,0},{2,3},{3,2},{4,5},{5,4},{6,7},{7,6},{8,9},{9,8},{10,11... | collective-permute-start | bytes 110600 | tf_op jit(solution)/shard_map/ppermute | solution.py:32
  28.5 6.1 %collective-permute-start.10 = (f32[36,256]{1,0:T(8,128)S(1)}, f32[36,256]{1,0:T(8,128)S(1)}, u32[]{:S(2)}, u32[]{:S(2)}) collective-permute-start(f32[36,256]{1,0:T(8,128)S(1)} %get-tuple-element.27), channel_id=1, source_target_pairs={{0,3},{1,2},{2,1},{3,0},{4,7},{5,6},{6,5},{7,4},{8,11},{9,10},{10,... | collective-permute-start | bytes 110600 | tf_op jit(solution)/shard_map/ppermute | solution.py:36
  32.5 2.1 %collective-permute-start.11 = (f32[36,256]{1,0:T(8,128)S(1)}, f32[36,256]{1,0:T(8,128)S(1)}, u32[]{:S(2)}, u32[]{:S(2)}) collective-permute-start(f32[36,256]{1,0:T(8,128)S(1)} %collective-permute-done.9.refs_2_), channel_id=1, source_target_pairs={{0,4},{4,0},{1,5},{5,1},{2,6},{6,2},{3,7},{7,3},{8,12},{12,8},{9,1... | collective-permute-start | bytes 110600 | tf_op jit(solution)/shard_map/ppermute | solution.py:32
  34.6 1.2 %collective-permute-start.12 = (f32[36,256]{1,0:T(8,128)S(1)}, f32[36,256]{1,0:T(8,128)S(1)}, u32[]{:S(2)}, u32[]{:S(2)}) collective-permute-start(f32[36,256]{1,0:T(8,128)S(1)} %collective-permute-done.10.refs_3_), channel_id=1, source_target_pairs={{0,4},{4,0},{1,5},{5,1},{2,6},{6,2},{3,7},{7,3},{8,12},{12,8},{9,1... | collective-permute-start | bytes 110600 | tf_op jit(solution)/shard_map/ppermute | solution.py:32
  35.8 7.7 %copy-start.5 = (s32[1,4,16,128]{3,2,1,0:T(8,128)S(1)}, s32[1,4,16,128]{3,2,1,0:T(8,128)}, u32[]{:S(2)}) copy-start(s32[1,4,16,128]{3,2,1,0:T(8,128)} %param.22) | copy-start | bytes 98308
  36.5 4.8 %collective-permute-start.15 = (f32[64,128]{1,0:T(8,128)S(1)}, f32[64,128]{1,0:T(8,128)S(1)}, u32[]{:S(2)}, u32[]{:S(2)}) collective-permute-start(f32[64,128]{1,0:T(8,128)S(1)} %get-tuple-element.29), channel_id=1, source_target_pairs={{0,24},{8,16},{16,8},{24,0},{1,25},{9,17},{17,9},{25,1},{2,26},{10... | collective-permute-start | bytes 98312 | tf_op jit(solution)/shard_map/ppermute | solution.py:48
  39.3 3.9 %collective-permute-start.14 = (f32[64,128]{1,0:T(8,128)S(1)}, f32[64,128]{1,0:T(8,128)S(1)}, u32[]{:S(2)}, u32[]{:S(2)}) collective-permute-start(f32[64,128]{1,0:T(8,128)S(1)} %get-tuple-element.29), channel_id=1, source_target_pairs={{0,16},{8,24},{16,0},{24,8},{1,17},{9,25},{17,1},{25,9},{2,18},{10... | collective-permute-start | bytes 98312 | tf_op jit(solution)/shard_map/ppermute | solution.py:48
  39.7 3.9 %collective-permute-start.13 = (f32[64,128]{1,0:T(8,128)S(1)}, f32[64,128]{1,0:T(8,128)S(1)}, u32[]{:S(2)}, u32[]{:S(2)}) collective-permute-start(f32[64,128]{1,0:T(8,128)S(1)} %get-tuple-element.29), channel_id=1, source_target_pairs={{0,8},{8,0},{16,24},{24,16},{1,9},{9,1},{17,25},{25,17},{2,10},{10... | collective-permute-start | bytes 98312 | tf_op jit(solution)/shard_map/ppermute | solution.py:48
  43.6 7.4 %collective-permute-start.16 = (f32[1,4,16,128]{3,2,1,0:T(8,128)S(1)}, f32[1,4,16,128]{3,2,1,0:T(8,128)S(1)}, u32[]{:S(2)}, u32[]{:S(2)}) collective-permute-start(f32[1,4,16,128]{3,2,1,0:T(8,128)S(1)} %get-tuple-element.30.refs_0_), channel_id=1, source_target_pairs={{0,4},{4,0},{1,5},{5,1},{2,6},{6,2},{3,7},{7,3},{8,12},{12,8},{9,1... | collective-permute-start | bytes 98312 | tf_op jit(solution)/shard_map/ppermute | solution.py:32
  43.7 3.7 %collective-permute-start.17 = (f32[12,128]{1,0:T(8,128)S(1)}, f32[12,128]{1,0:T(8,128)S(1)}, u32[]{:S(2)}, u32[]{:S(2)}) collective-permute-start(f32[12,128]{1,0:T(8,128)S(1)} %get-tuple-element.31), channel_id=1, source_target_pairs={{0,1},{1,0},{2,3},{3,2},{4,5},{5,4},{6,7},{7,6},{8,9},{9,8},{10,11... | collective-permute-start | bytes 18440 | tf_op jit(solution)/shard_map/ppermute | solution.py:32
  44.4 5.4 %collective-permute-start.18 = (f32[12,128]{1,0:T(8,128)S(1)}, f32[12,128]{1,0:T(8,128)S(1)}, u32[]{:S(2)}, u32[]{:S(2)}) collective-permute-start(f32[12,128]{1,0:T(8,128)S(1)} %get-tuple-element.32), channel_id=1, source_target_pairs={{0,3},{1,2},{2,1},{3,0},{4,7},{5,6},{6,5},{7,4},{8,11},{9,10},{10,... | collective-permute-start | bytes 18440 | tf_op jit(solution)/shard_map/ppermute | solution.py:36
  47.4 2.5 %collective-permute-start.19 = (f32[12,128]{1,0:T(8,128)S(1)}, f32[12,128]{1,0:T(8,128)S(1)}, u32[]{:S(2)}, u32[]{:S(2)}) collective-permute-start(f32[12,128]{1,0:T(8,128)S(1)} %collective-permute-done.17.refs_2_), channel_id=1, source_target_pairs={{0,4},{4,0},{1,5},{5,1},{2,6},{6,2},{3,7},{7,3},{8,12},{12,8},{9,1... | collective-permute-start | bytes 18440 | tf_op jit(solution)/shard_map/ppermute | solution.py:32
  49.9 1.2 %collective-permute-start.20 = (f32[12,128]{1,0:T(8,128)S(1)}, f32[12,128]{1,0:T(8,128)S(1)}, u32[]{:S(2)}, u32[]{:S(2)}) collective-permute-start(f32[12,128]{1,0:T(8,128)S(1)} %collective-permute-done.18.refs_3_), channel_id=1, source_target_pairs={{0,4},{4,0},{1,5},{5,1},{2,6},{6,2},{3,7},{7,3},{8,12},{12,8},{9,1... | collective-permute-start | bytes 18440 | tf_op jit(solution)/shard_map/ppermute | solution.py:32
  51.0 13.0 %copy-start.3 = (f32[1,3,4,16,128]{4,3,2,1,0:T(8,128)S(1)}, f32[1,3,4,16,128]{4,3,2,1,0:T(8,128)}, u32[]{:S(2)}) copy-start(f32[1,3,4,16,128]{4,3,2,1,0:T(8,128)} %param.19) | copy-start | bytes 294916
  56.1 1.2 %collective-permute-start.21 = (f32[16,128]{1,0:T(8,128)S(1)}, f32[16,128]{1,0:T(8,128)S(1)}, u32[]{:S(2)}, u32[]{:S(2)}) collective-permute-start(f32[16,128]{1,0:T(8,128)S(1)} %get-tuple-element.37.refs_4_), channel_id=1, source_target_pairs={{0,4},{4,0},{1,5},{5,1},{2,6},{6,2},{3,7},{7,3},{8,12},{12,8},{9,1... | collective-permute-start | bytes 24584 | tf_op jit(solution)/shard_map/ppermute | solution.py:32
  57.2 5.4 %collective-permute-start.24 = (f32[16,128]{1,0:T(8,128)S(1)}, f32[16,128]{1,0:T(8,128)S(1)}, u32[]{:S(2)}, u32[]{:S(2)}) collective-permute-start(f32[16,128]{1,0:T(8,128)S(1)} %add.3.refs_0_), channel_id=1, source_target_pairs={{0,3},{1,2},{2,1},{3,0},{4,7},{5,6},{6,5},{7,4},{8,11},{9,10},{10,... | collective-permute-start | bytes 24584 | tf_op jit(solution)/shard_map/ppermute | solution.py:48
  59.5 4.5 %collective-permute-start.23 = (f32[16,128]{1,0:T(8,128)S(1)}, f32[16,128]{1,0:T(8,128)S(1)}, u32[]{:S(2)}, u32[]{:S(2)}) collective-permute-start(f32[16,128]{1,0:T(8,128)S(1)} %add.3.refs_0_), channel_id=1, source_target_pairs={{0,2},{1,3},{2,0},{3,1},{4,6},{5,7},{6,4},{7,5},{8,10},{9,11},{10,... | collective-permute-start | bytes 24584 | tf_op jit(solution)/shard_map/ppermute | solution.py:48
  59.5 4.5 %collective-permute-start.22 = (f32[16,128]{1,0:T(8,128)S(1)}, f32[16,128]{1,0:T(8,128)S(1)}, u32[]{:S(2)}, u32[]{:S(2)}) collective-permute-start(f32[16,128]{1,0:T(8,128)S(1)} %add.3.refs_0_), channel_id=1, source_target_pairs={{0,1},{1,0},{2,3},{3,2},{4,5},{5,4},{6,7},{7,6},{8,9},{9,8},{10,11... | collective-permute-start | bytes 24584 | tf_op jit(solution)/shard_map/ppermute | solution.py:48

commit v3 on v2

--- a/solution.py
+++ b/solution.py
@@ -20,36 +20,79 @@
 bf16 = jnp.bfloat16
 
 
-def pairs_a(n):
-    return [(i, i ^ 1) for i in range(n)]
-
-
-def pairs_b(n):
-    return [(i, (i + 1) % n if i % 2 else (i - 1) % n) for i in range(n)]
-
-
-def swap_a(value, axis):
-    return lax.ppermute(value, axis, pairs_a(lax.axis_size(axis)))
-
-
-def swap_b(value, axis):
-    return lax.ppermute(value, axis, pairs_b(lax.axis_size(axis)))
-
-
-def both(value_a, value_b, axis):
-    got_a = swap_a(value_a, axis)
-    if lax.axis_size(axis) == 2:
-        return got_a, got_a
-    return got_a, swap_b(value_b, axis)
-
-
-def by_xor(value, axis):
-    n = lax.axis_size(axis)
-    return [lax.ppermute(value, axis, [(i, i ^ k) for i in range(n)]) for k in range(1, n)]
-
-
-def call(body, name, outs, *args, scratch=()):
+ALL = ("grp", "gx", "gy")
+
+
+def permuted(value, target):
+    sizes = [lax.axis_size(a) for a in ALL]
+    flat = lambda g, x, y: (g * sizes[1] + x) * sizes[2] + y
+    pairs = []
+    for g in range(sizes[0]):
+        for x in range(sizes[1]):
+            for y in range(sizes[2]):
+                pairs.append((flat(g, x, y), flat(*target(g, x, y))))
+    return lax.ppermute(value, ALL, pairs)
+
+
+def idle(g, x, y):
+    return g, x ^ 1, y
+
+
+def x_swap(value):
+    return permuted(value, idle)
+
+
+def exchange_x(value):
+    n = lax.axis_size("gx")
+    got = x_swap(value)
+    if n == 2:
+        return got, got
+    return got, permuted(value, lambda g, x, y: (g, ((x + 1) if x % 2 else (x - 1)) % n, y))
+
+
+def up_or_down(i, n, kind):
+    j = i + 1 if i % 2 == kind else i - 1
+    return j if 0 <= j < n else None
+
+
+def pair_y(kind):
+    n = lax.axis_size("gy")
+
+    def target(g, x, y):
+        j = up_or_down(y, n, kind)
+        return idle(g, x, y) if j is None else (g, x, j)
+
+    return target
+
+
+def pair_first(kind):
+    last = lax.axis_size("grp") - 1
+    along_y = pair_y(kind)
+
+    def target(g, x, y):
+        if g == last:
+            return along_y(g, x, y)
+        j = up_or_down(g, last, kind)
+        return idle(g, x, y) if j is None else (j, x, y)
+
+    return target
+
+
+def star(value):
+    n = lax.axis_size("grp")
+
+    def meet(k):
+        def target(g, x, y):
+            return (g ^ k, x, y) if n - 1 in (g, g ^ k) else idle(g, x, y)
+
+        return target
+
+    return [permuted(value, meet(k)) for k in range(1, n)]
+
+
+def call(body, name, outs, *args, scratch=(), space=pltpu.VMEM):
     vmem = pl.BlockSpec(memory_space=pltpu.VMEM)
+    source = pl.BlockSpec(memory_space=space)
     unique, spots = [], []
     for arg in args:
         found = [i for i, other in enumerate(unique) if other is arg]
@@ -64,7 +107,7 @@
         expanded,
         name=name,
         out_shape=[o if hasattr(o, "dtype") else jax.ShapeDtypeStruct(o, f32) for o in outs],
-        in_specs=[vmem] * len(unique),
+        in_specs=[source] * len(unique),
         out_specs=[vmem] * len(outs),
         scratch_shapes=list(scratch),
         compiler_params=pltpu.CompilerParams(vmem_limit_bytes=GRANT),
@@ -204,14 +247,15 @@
         out[...] = jnp.where(keep, wide, 0.0).astype(bf16)
 
 
-def add_apply(nodes, weight, out, k_high, k_low, first, last):
+def add_apply(nodes, weight, out, k_high, k_low, first, last, own=None):
     rows = nodes.shape[2]
     tiles = rows // 8
     for m in range(3):
         out[m, first] = jnp.zeros((rows, 128), f32)
 
-    def plane(x, carry):
-        v = stiff(k_high, k_low, stack_tiles(corners(nodes, x), range(tiles)))
+    def plane(x, energy):
+        u = stack_tiles(corners(nodes, x), range(tiles))
+        v = stiff(k_high, k_low, u)
         w = weight[x]
 
         def entry(j):
@@ -230,16 +274,31 @@
                     out[m, x] = out[m, x] + total
                 else:
                     out[m, x + 1] = total
-        return carry
-
-    lax.fori_loop(first, last, plane, 0)
+        if own is None:
+            return energy
+        planes, spots = own
+        inside = jnp.where((x >= planes[0]) & (x < planes[-1] + 1), 1.0, 0.0)
+        for t in spots:
+            cols = slice(128 * t, 128 * t + 128)
+            energy = energy + inside * w[8 * t : 8 * t + 8] * dots(u[:, cols], v[:, cols])
+        return energy
+
+    return lax.fori_loop(first, last, plane, jnp.zeros((8, 128), f32))
+
+
+def dots(u, v):
+    part = u * v
+    total = part[0:8]
+    for j in range(1, 24):
+        total = total + part[8 * j : 8 * j + 8]
+    return total
 
 
 def total_of(value):
     return jnp.sum(jnp.sum(value, axis=0, keepdims=True), axis=1, keepdims=True)
 
 
-def onehot_sum(rows_of, size_x, size_y, shape, row_fn):
+def onehot_sum(size_x, size_y, shape, row_fn):
     def plane(x, acc):
         lefts, rights = [], []
         for y in range(size_y):
@@ -260,33 +319,66 @@
     return 8 * (field * size_x + x)
 
 
-def pack_body(p, src, sto, well, host, u, body, mod, mask, tile, ya, yb, zmsg):
+def pack_body(p, src, sto, well, host, u, body, mod, mask, tile, ya, yb, *scratch):
     at = Place()
     size_x, size_y = p.shape[0], p.shape[1]
+    refs, sems = scratch[:-1], scratch[-1]
+
+    def fetch(first, sources):
+        copies = [
+            pltpu.make_async_copy(s, refs[first + i], sems.at[first + i])
+            for i, s in enumerate(sources)
+        ]
+        for c in copies:
+            c.start()
+        for c in copies:
+            c.wait()
+        return refs[first : first + len(copies)]
 
     @pl.when(at.mech)
     def _():
-        tile[0:3] = u[...]
-        tile[3:6] = body[...]
-        tile[6] = mod[...] * mask[...].astype(f32)
+        u_in, body_in, mod_in, mask_in = fetch(0, (u, body, mod, mask))
+        tile[0:3] = u_in[...]
+        tile[3:6] = body_in[...]
+        tile[6] = mod_in[...] * mask_in[...].astype(f32)
         pack_rows(at, tile, ya, yb, 7, size_x, size_y)
 
     @pl.when(~at.mech)
     def _():
+        p_in, src_in, sto_in, well_in, host_in = fetch(4, (p, src, sto, well, host))
         where = lane((size_y, 128))
         msg = jnp.zeros((size_y, 128), f32)
         for x in range(size_x):
-            diag = 6.0 + sto[x] + well_index * well[x].astype(f32)
-            for f, v in enumerate((p[x], relaxation / diag, src[x], host[x].astype(f32))):
+            diag = 6.0 + sto_in[x] + well_index * well_in[x].astype(f32)
+            fields = (p_in[x], relaxation / diag, src_in[x], host_in[x].astype(f32))
+            for f, v in enumerate(fields):
                 s = z_slot(f, x, size_x)
                 msg = jnp.where((where >= s) & (where < s + 6), roll(v, s + 3, 1), msg)
-        zmsg[...] = msg
-
-
-def strain_body(tile, xa, xb, ya, yb, xyaa, xyab, xyba, xybb, mask, host, zmsg, out, ue):
+        ya[0:size_y] = msg
+        yb[0:size_y] = msg
+
+
+def count_body(host, out):
+    at = Place()
+    size_x, size_y = host.shape[0], host.shape[1]
+    rows = size_x * size_y
+
+    @pl.when(~at.mech)
+    def _():
+        high_id, low_id = sub((rows, 128)), sub((128, 128))
+
+        def row(x, y):
+            h = host[x, y : y + 1, :]
+            left = jnp.where(high_id == (h >> 7), 1.0, 0.0).astype(bf16)
+            right = jnp.where(low_id == (h & 127), 1.0, 0.0).astype(bf16)
+            return left, right
+
+        out[...] = onehot_sum(size_x, size_y, (rows, 128), row)
+
+
+def strain_body(tile, xa, xb, ya, yb, xyaa, xyab, xyba, xybb, mask, counts, out, ue):
     at = Place()
     size_x, size_y = mask.shape[0], mask.shape[1]
-    rows = size_x * size_y
 
     @pl.when(at.mech)
     def _():
@@ -325,16 +417,7 @@
 
     @pl.when(~at.mech)
     def _():
-        high_id, low_id = sub((rows, 128)), sub((128, 128))
-
-        def row(x, y):
-            h = host[x, y : y + 1, :]
-            left = jnp.where(high_id == (h >> 7), 1.0, 0.0).astype(bf16)
-            right = jnp.where(low_id == (h & 127), 1.0, 0.0).astype(bf16)
-            return left, right
-
-        out[0:rows, :] = onehot_sum(None, size_x, size_y, (rows, 128), row)
-        out[rows : rows + size_y, :] = zmsg[...]
+        out[...] = counts[...]
 
 
 def gather_body(*refs):
@@ -355,10 +438,11 @@
 
     @pl.when(~at.mech)
     def _():
-        table[...] = pick(at.groups - 1, (slice(0, rows), slice(None)))
-        zrows = (slice(rows, rows + size_y), slice(None))
-        before = jnp.where(at.g > 0, pick(at.g - 1, zrows), 0.0)
-        after = jnp.where(at.g < at.groups - 2, pick(at.g + 1, zrows), 0.0)
+        table[...] = pick(at.groups - 1, slice(None))
+        godd = lax.rem(at.g, 2) == 1
+        msg_a, msg_b = ya[0:size_y], yb[0:size_y]
+        before = jnp.where(at.g > 0, jnp.where(godd, msg_a, msg_b), 0.0)
+        after = jnp.where(at.g < at.groups - 2, jnp.where(godd, msg_b, msg_a), 0.0)
         spot = lane((size_y, 128))
         zside = jnp.where((spot & 7) < 3, before, after)
         first_host = z_slot(3, 0, size_x)
@@ -409,10 +493,6 @@
     size_x, size_y = sto.shape[0], sto.shape[1]
     rows = size_x * size_y
     nx = size_x + 2 * H
-
-    @pl.when(at.mech)
-    def _():
-        pressure[...] = jnp.zeros_like(pressure)
 
     @pl.when(~at.mech)
     def _():
@@ -451,7 +531,7 @@
             right = jnp.where(block_ids == block[x, y : y + 1, :], 1.0, 0.0).astype(bf16)
             return jnp.concatenate([high, low], axis=0), right
 
-        acc = onehot_sum(None, size_x, size_y, (32, NBLK), coarse_row)
+        acc = onehot_sum(size_x, size_y, (32, NBLK), coarse_row)
         corr[...] = jnp.zeros_like(corr)
         corr[:, 0:NBLK] = (acc[0:8] + acc[16:24]) / (1.0 + (acc[8:16] + acc[24:32]))
         lines = [jnp.broadcast_to(corr[j : j + 1, :], (8, 128)) for j in range(8)]
@@ -479,7 +559,7 @@
             right = jnp.where(low_id == (h & 127), 1.0, 0.0).astype(bf16)
             return jnp.concatenate(left, axis=0), right
 
-        acc = onehot_sum(None, size_x, size_y, (2 * rows, 128), sum_row)
+        acc = onehot_sum(size_x, size_y, (2 * rows, 128), sum_row)
         sums[...] = acc[0:rows] + acc[rows : 2 * rows]
 
 
@@ -537,7 +617,9 @@
                     res[m, x] = jnp.where(inside_x(x), value, 0.0)
             before = (ssz, dsz, sdz)
 
-        add_apply(res, we, acc, k_high, k_low, 2, size_x + 4)
+        tiles = range(TOP // 8, (TOP + size_y) // 8)
+        planes = range(H, H + size_x)
+        e22 = add_apply(res, we, acc, k_high, k_low, 2, size_x + 4, (planes, tiles))
         rr = jnp.zeros((8, 128), f32)
         rq = jnp.zeros((8, 128), f32)
         for m in range(3):
@@ -565,25 +647,16 @@
                         qq = qq + v * v
                         rq = rq + v * res[m, x, t : t + 8, :]
         rq, qq = total_of(rq), total_of(qq)
-        tiles = range(TOP // 8, (TOP + size_y) // 8)
 
         def plane(x, sums):
             uq = stack_tiles(corners(acc, x), tiles)
             ur = stack_tiles(corners(res, x), tiles)
             vq = stiff(k_high, k_low, uq)
-            vr = stiff(k_high, k_low, ur)
             w = jnp.concatenate([we[x, 8 * t : 8 * t + 8, :] for t in tiles], axis=1)
-            out = []
-            for s, u, v in zip(sums, (uq, ur, ur), (vq, vq, vr)):
-                part = u * v
-                t = part[0:8]
-                for j in range(1, 24):
-                    t = t + part[8 * j : 8 * j + 8]
-                out.append(s + w * t)
-            return tuple(out)
+            return tuple(s + w * dots(u, vq) for s, u in zip(sums, (uq, ur)))
 
         zero = jnp.zeros((8, 128 * len(tiles)), f32)
-        e11, e12, e22 = lax.fori_loop(H, H + size_x, plane, (zero, zero, zero))
+        e11, e12 = lax.fori_loop(H, H + size_x, plane, (zero, zero))
         e11 = total_of(e11) + spring_coef * qq
         e12 = total_of(e12) + spring_coef * rq
         e22 = total_of(e22) + spring_coef * rr
@@ -600,14 +673,16 @@
 
 def final_body(*refs):
     at = Place()
-    scals, own, r, q, u, out = refs[:-5], *refs[-5:]
+    scals, own, r, q, u, updated, pressure, out = refs[:-7], *refs[-7:]
 
     @pl.when(~at.mech)
     def _():
         out[...] = jnp.zeros_like(out)
+        pressure[...] = updated[...]
 
     @pl.when(at.mech)
     def _():
+        pressure[...] = jnp.zeros_like(pressure)
         parts = [s[8 * i : 8 * i + 8] for s in scals for i in range(s.shape[0] // 8)]
         get = lambda part, i: part[i : i + 1]
         total = lambda fn: functools.reduce(lambda a, b: a + b, [fn(p) for p in parts])
@@ -634,11 +709,12 @@
         out[...] = u[...] + by_r[None, None] * r[...] + by_q[None, None] * q[...]
 
 
-def neighbours(tile, msg_a, msg_b):
-    xa, xb = both(tile, tile, "gx")
-    ya, yb = both(msg_a, msg_b, "gy")
-    xyaa, xyba = both(ya, ya, "gx")
-    xyab, xybb = both(yb, yb, "gx")
+def neighbours(tile, msg_a, msg_b, pair=pair_y):
+    xa, xb = exchange_x(tile)
+    yb = permuted(msg_b, pair(1))
+    ya = permuted(msg_a, pair(0))
+    xyab, xybb = exchange_x(yb)
+    xyaa, xyba = exchange_x(ya)
     return (xa, xb, ya, yb, xyaa, xyab, xyba, xybb)
 
 
@@ -666,21 +742,26 @@
     kron = jax.ShapeDtypeStruct((8 * stiffness.shape[0],) * 2, bf16)
 
     msg = (7 * size_x * H, size_z)
-    tile, ya, yb, zmsg = call(
+    inputs = (displacement[0], body_force[0], modulus[0], mask, p, src, sto, well, host)
+    tile, ya, yb = call(
         pack_body,
         "pack",
-        [(7, size_x, size_y, size_z), msg, msg, (size_y, size_z)],
+        [(7, size_x, size_y, size_z), msg, msg],
         p, src, sto, well, host, u, body, modulus[0], mask,
+        scratch=[pltpu.VMEM(v.shape, v.dtype) for v in inputs]
+        + [pltpu.SemaphoreType.DMA((len(inputs),))],
+        space=pltpu.HBM,
     )
-    near = neighbours(tile, ya, yb)
+    near = neighbours(tile, ya, yb, pair_first)
+    (counts,) = call(count_body, "count", [(rows, size_z)], host)
     (line,) = call(
         strain_body,
         "strain",
-        [(rows + size_y, size_z)],
-        tile, *near, mask, host, zmsg,
+        [(rows, size_z)],
+        tile, *near, mask, counts,
         scratch=[pltpu.VMEM((3, size_x + 1, size_y + 8, size_z), f32)],
     )
-    got = by_xor(line, "grp")
+    got = star(line)
     msg = (3 * size_x * H, 2 * size_z)
     cells, ya, yb, g0, we, k_high, k_low = call(
         gather_body,
@@ -705,7 +786,7 @@
             pltpu.VMEM((8, size_z), f32),
         ],
     )
-    summed = by_xor(sums, "grp")
+    summed = star(sums)
     msg = (size_x * H, size_z)
     elem, ya, yb = call(
         element_body,
@@ -728,12 +809,15 @@
         ],
     )
     if duo:
-        pair = scal + swap_a(scal, "gx")
-        scals = [pair] + by_xor(pair, "gy")
+        pair = scal + x_swap(scal)
+        n = lax.axis_size("gy")
+        scals = [pair] + [permuted(pair, lambda g, x, y: (g, x, y ^ k)) for k in range(1, n)]
     else:
         scals = [lax.all_gather(scal, ("gx", "gy"), tiled=True)]
-    (moved,) = call(final_body, "final", [own], *scals, scal, r, q, u)
-    return (updated[None], moved[None])
+    pressure_out, moved = call(
+        final_body, "final", [p.shape, own], *scals, scal, r, q, u, updated
+    )
+    return (pressure_out[None], moved[None])
 
 
 def solution(mesh):

time: 65.4 us -> 56.2 us (0.86)
  starting transfers between devices: 22.2 us -> 17.8 us
  waiting for transfers between devices: 23.8 us -> 19.6 us
    ppermute x25, starting transfers between devices: 22.2 us -> 17.8 us  [permuted(): return lax.ppermute(value, ALL, pairs)]
    ppermute x25, waiting for transfers between devices: 23.8 us -> 19.6 us  [permuted(): return lax.ppermute(value, ALL, pairs)]
    pallas_call x7 -> x8, Pallas kernels: 10.9 us -> 10.3 us  [call(): pl.pallas_call(expanded, name=name, out_shape=[o if hasattr(o, 'dtype') e...]
  transfers between devices with their start and end apart: 25 -> 25, of which waited for: 17 -> 18; matrix products, arithmetic and copies ran while one was open for 0% -> 0% of each run, Pallas kernels for 0% -> 0%
where the time goes in v3:
time: 56.2 us; the launch traced here: 55.6 us
  waiting for transfers between devices  19.6 us (35%)
  starting transfers between devices  17.8 us (32%)
  Pallas kernels  10.3 us (18%)
  local copies, waits for them, and re-layouts  7.12 us (13%)
  between operations  0.79 us (1%)
    ppermute x25, waiting for transfers between devices, permuted(): return lax.ppermute(value, ALL, pairs)  19.6 us
    ppermute x25, starting transfers between devices, permuted(): return lax.ppermute(value, ALL, pairs)  17.8 us
    pallas_call x8, Pallas kernels, call(): pl.pallas_call(expanded, name=name, out_shape=[o if hasattr(o, 'dtype') e...  10.3 us
    unnamed x32, local copies, waits for them, and re-layouts  7.12 us
  transfers between devices with their start and end apart: 25, of which 18 were waited for; matrix products, arithmetic and copies ran while one was open for 0% of the time, Pallas kernels for 0%

profile of v3, /device:TPU:6, one launch (start us, length us, event | category | flops | bytes accessed | tf_op | source)
XLA Modules:
  0.0 55.6 jit_solution(888863611469882965)
XLA Ops:
  0.6 0.7 %copy-done = s32[1,4,16,128]{3,2,1,0:T(8,128)S(1)} copy-done((s32[1,4,16,128]{3,2,1,0:T(8,128)S(1)}, s32[1,4,16,128]{3,2,1,0:T(8,128)}, u32[]{:S(2)}) %copy-start) | copy-done | bytes 32792
  1.4 0.9 %copy-done.2 = f32[1,3,4,16,128]{4,3,2,1,0:T(8,128)S(1)} copy-done((f32[1,3,4,16,128]{4,3,2,1,0:T(8,128)S(1)}, f32[1,3,4,16,128]{4,3,2,1,0:T(8,128)}, u32[]{:S(2)}) %copy-start.2) | copy-done | bytes 98328
  2.3 0.8 %copy-done.4 = s32[1,4,16,128]{3,2,1,0:T(8,128)S(1)} copy-done((s32[1,4,16,128]{3,2,1,0:T(8,128)S(1)}, s32[1,4,16,128]{3,2,1,0:T(8,128)}, u32[]{:S(2)}) %copy-start.4) | copy-done | bytes 32792
  3.0 0.8 %copy-done.6 = f32[1,4,16,128]{3,2,1,0:T(8,128)S(1)} copy-done((f32[1,4,16,128]{3,2,1,0:T(8,128)S(1)}, f32[1,4,16,128]{3,2,1,0:T(8,128)}, u32[]{:S(2)}) %copy-start.6) | copy-done | bytes 32792
  3.8 0.8 %copy-done.7 = s32[1,4,16,128]{3,2,1,0:T(8,128)S(1)} copy-done((s32[1,4,16,128]{3,2,1,0:T(8,128)S(1)}, s32[1,4,16,128]{3,2,1,0:T(8,128)}, u32[]{:S(2)}) %copy-start.7) | copy-done | bytes 32792
  4.6 0.8 %copy-done.10 = f32[1,4,16,128]{3,2,1,0:T(8,128)S(1)} copy-done((f32[1,4,16,128]{3,2,1,0:T(8,128)S(1)}, f32[1,4,16,128]{3,2,1,0:T(8,128)}, u32[]{:S(2)}) %copy-start.10) | copy-done | bytes 32792
  5.3 0.8 %copy-done.11 = f32[1,4,16,128]{3,2,1,0:T(8,128)S(1)} copy-done((f32[1,4,16,128]{3,2,1,0:T(8,128)S(1)}, f32[1,4,16,128]{3,2,1,0:T(8,128)}, u32[]{:S(2)}) %copy-start.11) | copy-done | bytes 32792
  6.1 0.9 %copy-done.12 = f32[1,3,4,16,128]{4,3,2,1,0:T(8,128)S(1)} copy-done((f32[1,3,4,16,128]{4,3,2,1,0:T(8,128)S(1)}, f32[1,3,4,16,128]{4,3,2,1,0:T(8,128)}, u32[]{:S(2)}) %copy-start.12) | copy-done | bytes 98328
  7.0 0.8 %copy-done.13 = f32[1,4,16,128]{3,2,1,0:T(8,128)S(1)} copy-done((f32[1,4,16,128]{3,2,1,0:T(8,128)S(1)}, f32[1,4,16,128]{3,2,1,0:T(8,128)}, u32[]{:S(2)}) %copy-start.13) | copy-done | bytes 32792
  7.7 0.4 pack.1
  8.2 1.6 %collective-permute-start.1 = (f32[84,128]{1,0:T(8,128)S(1)}, f32[84,128]{1,0:T(8,128)S(1)}, u32[]{:S(2)}, u32[]{:S(2)}) collective-permute-start(f32[84,128]{1,0:T(8,128)S(1)} %get-tuple-element.23), channel_id=1, source_target_pairs={{0,8},{1,9},{2,10},{3,11},{4,12},{5,13},{6,14},{7,15},{8,0},{9,1},... | collective-permute-start | bytes 129032 | tf_op jit(solution)/shard_map/ppermute | solution.py:34
  9.9 0.2 collective-permute-start.2
  10.0 2.3 %collective-permute-done.1.refs_2_.refs_10_ = f32[84,128]{1,0:T(8,128)S(1)} collective-permute-done((f32[84,128]{1,0:T(8,128)S(1)}, f32[84,128]{1,0:T(8,128)S(1)}, u32[]{:S(2)}, u32[]{:S(2)}) %collective-permute-start.1) | collective-permute-done | bytes 43040 | tf_op jit(solution)/shard_map/ppermute | solution.py:34
  12.4 0.5 collective-permute-start.4
  12.9 0.7 %collective-permute-done.3.refs_4_.refs_12_ = f32[84,128]{1,0:T(8,128)S(1)} collective-permute-done((f32[84,128]{1,0:T(8,128)S(1)}, f32[84,128]{1,0:T(8,128)S(1)}, u32[]{:S(2)}, u32[]{:S(2)}) %collective-permute-start.3) | collective-permute-done | bytes 43040 | tf_op jit(solution)/shard_map/ppermute | solution.py:34
  13.6 0.2 collective-permute-done.4.refs_5_.refs_13_
  13.9 0.5 collective-permute-start.7
  14.4 1.3 %collective-permute-start.6 = (f32[64,128]{1,0:T(8,128)S(1)}, f32[64,128]{1,0:T(8,128)S(1)}, u32[]{:S(2)}, u32[]{:S(2)}) collective-permute-start(f32[64,128]{1,0:T(8,128)S(1)} %strain.1), channel_id=1, source_target_pairs={{0,4},{1,5},{2,6},{3,7},{4,0},{5,1},{6,2},{7,3},{8,24},{9,25},{10,... | collective-permute-start | bytes 98312 | tf_op jit(solution)/shard_map/ppermute | solution.py:34
  15.7 0.5 collective-permute-start.5
  16.2 2.6 %collective-permute-done.7.refs_2_.refs_5_ = f32[64,128]{1,0:T(8,128)S(1)} collective-permute-done((f32[64,128]{1,0:T(8,128)S(1)}, f32[64,128]{1,0:T(8,128)S(1)}, u32[]{:S(2)}, u32[]{:S(2)}) %collective-permute-start.7) | collective-permute-done | bytes 32800 | tf_op jit(solution)/shard_map/ppermute | solution.py:34
  18.9 0.7 %collective-permute-done.5.refs_0_.refs_3_ = f32[64,128]{1,0:T(8,128)S(1)} collective-permute-done((f32[64,128]{1,0:T(8,128)S(1)}, f32[64,128]{1,0:T(8,128)S(1)}, u32[]{:S(2)}, u32[]{:S(2)}) %collective-permute-start.5) | collective-permute-done | bytes 32800 | tf_op jit(solution)/shard_map/ppermute | solution.py:34
  19.6 4.3 %gather.1 = (f32[3,4,16,256]{3,2,1,0:T(8,128)S(1)}, f32[36,256]{1,0:T(8,128)S(1)}, f32[36,256]{1,0:T(8,128)S(1)}, f32[3,10,32,128]{3,2,1,0:T(8,128)S(1)}, f32[10...) custom-call(f32[64,128]{1,0:T(8,128)S(1)} %collective-permute-done.5.refs_0_.refs_3_, ...), custom_call_target="tpu_custom_call" | custom-call | tf_op jit(solution)/shard_map/gather/pallas_call | solution.py:106
  24.0 2.1 %collective-permute-start.9 = (f32[36,256]{1,0:T(8,128)S(1)}, f32[36,256]{1,0:T(8,128)S(1)}, u32[]{:S(2)}, u32[]{:S(2)}) collective-permute-start(f32[36,256]{1,0:T(8,128)S(1)} %get-tuple-element.26), channel_id=1, source_target_pairs={{0,1},{1,0},{2,3},{3,2},{4,5},{5,4},{6,7},{7,6},{8,9},{9,8},{10,11... | collective-permute-start | bytes 110600 | tf_op jit(solution)/shard_map/ppermute | solution.py:34
  26.1 0.2 collective-permute-start.10
  26.3 2.0 %collective-permute-done.9.refs_2_ = f32[36,256]{1,0:T(8,128)S(1)} collective-permute-done((f32[36,256]{1,0:T(8,128)S(1)}, f32[36,256]{1,0:T(8,128)S(1)}, u32[]{:S(2)}, u32[]{:S(2)}) %collective-permute-start.9) | collective-permute-done | bytes 36896 | tf_op jit(solution)/shard_map/ppermute | solution.py:34
  28.3 0.5 collective-permute-start.12
  28.8 0.7 %collective-permute-done.11.refs_4_ = f32[36,256]{1,0:T(8,128)S(1)} collective-permute-done((f32[36,256]{1,0:T(8,128)S(1)}, f32[36,256]{1,0:T(8,128)S(1)}, u32[]{:S(2)}, u32[]{:S(2)}) %collective-permute-start.11) | collective-permute-done | bytes 36896 | tf_op jit(solution)/shard_map/ppermute | solution.py:34
  29.5 0.2 collective-permute-done.12.refs_5_
  29.7 1.2 %collective-permute-start.15 = (f32[64,128]{1,0:T(8,128)S(1)}, f32[64,128]{1,0:T(8,128)S(1)}, u32[]{:S(2)}, u32[]{:S(2)}) collective-permute-start(f32[64,128]{1,0:T(8,128)S(1)} %get-tuple-element.28), channel_id=1, source_target_pairs={{0,24},{1,25},{2,26},{3,27},{4,28},{5,29},{6,30},{7,31},{8,12},{9,... | collective-permute-start | bytes 98312 | tf_op jit(solution)/shard_map/ppermute | solution.py:34
  30.9 0.6 %collective-permute-start.14 = (f32[64,128]{1,0:T(8,128)S(1)}, f32[64,128]{1,0:T(8,128)S(1)}, u32[]{:S(2)}, u32[]{:S(2)}) collective-permute-start(f32[64,128]{1,0:T(8,128)S(1)} %get-tuple-element.28), channel_id=1, source_target_pairs={{0,4},{1,5},{2,6},{3,7},{4,0},{5,1},{6,2},{7,3},{8,24},{9,25},{10,... | collective-permute-start | bytes 98312 | tf_op jit(solution)/shard_map/ppermute | solution.py:34
  31.5 0.4 collective-permute-start.13
  32.0 2.7 %collective-permute-done.15.refs_2_ = f32[64,128]{1,0:T(8,128)S(1)} collective-permute-done((f32[64,128]{1,0:T(8,128)S(1)}, f32[64,128]{1,0:T(8,128)S(1)}, u32[]{:S(2)}, u32[]{:S(2)}) %collective-permute-start.15) | collective-permute-done | bytes 32800 | tf_op jit(solution)/shard_map/ppermute | solution.py:34
  34.6 0.4 collective-permute-done.14.refs_1_
  35.0 0.5 collective-permute-done.13.refs_0_
  35.6 2.7 %collective-permute-start.17 = (f32[12,128]{1,0:T(8,128)S(1)}, f32[12,128]{1,0:T(8,128)S(1)}, u32[]{:S(2)}, u32[]{:S(2)}) collective-permute-start(f32[12,128]{1,0:T(8,128)S(1)} %get-tuple-element.30), channel_id=1, source_target_pairs={{0,1},{1,0},{2,3},{3,2},{4,5},{5,4},{6,7},{7,6},{8,9},{9,8},{10,11... | collective-permute-start | bytes 18440 | tf_op jit(solution)/shard_map/ppermute | solution.py:34
  38.4 1.5 %collective-permute-done.17.refs_2_ = f32[12,128]{1,0:T(8,128)S(1)} collective-permute-done((f32[12,128]{1,0:T(8,128)S(1)}, f32[12,128]{1,0:T(8,128)S(1)}, u32[]{:S(2)}, u32[]{:S(2)}) %collective-permute-start.17) | collective-permute-done | bytes 6176 | tf_op jit(solution)/shard_map/ppermute | solution.py:34
  39.9 0.5 collective-permute-start.20
  40.4 0.7 %collective-permute-done.19.refs_4_ = f32[12,128]{1,0:T(8,128)S(1)} collective-permute-done((f32[12,128]{1,0:T(8,128)S(1)}, f32[12,128]{1,0:T(8,128)S(1)}, u32[]{:S(2)}, u32[]{:S(2)}) %collective-permute-start.19) | collective-permute-done | bytes 6176 | tf_op jit(solution)/shard_map/ppermute | solution.py:34
  41.0 0.2 collective-permute-done.20.refs_5_
  41.2 4.6 %krylov.1 = (f32[3,4,16,128]{3,2,1,0:T(8,128)S(1)}, f32[3,4,16,128]{3,2,1,0:T(8,128)S(1)}, f32[16,128]{1,0:T(8,128)S(1)}) custom-call(f32[1,4,16,128]{3,2,1,0:T(8,128)S(1)} %get-tuple-element.29.refs_0_, f32[1,4,16,128]{3,2,1,0:T(8,128)S(1)} %collective-permute-done.16.refs_1_, f32[12,128]{1,0:T(8,128)S(1)} %collective-permute-done.17.refs_2_, ...), custom_call_target="tpu_custom_call" | custom-call | tf_op jit(solution)/shard_map/krylov/pallas_call | solution.py:106
  45.9 0.3 collective-permute-start.21
  46.2 0.8 %collective-permute-done.21 = f32[16,128]{1,0:T(8,128)S(1)} collective-permute-done((f32[16,128]{1,0:T(8,128)S(1)}, f32[16,128]{1,0:T(8,128)S(1)}, u32[]{:S(2)}, u32[]{:S(2)}) %collective-permute-start.21) | collective-permute-done | bytes 8224 | tf_op jit(solution)/shard_map/ppermute | solution.py:34
  47.0 3.3 %collective-permute-start.24 = (f32[16,128]{1,0:T(8,128)S(1)}, f32[16,128]{1,0:T(8,128)S(1)}, u32[]{:S(2)}, u32[]{:S(2)}) collective-permute-start(f32[16,128]{1,0:T(8,128)S(1)} %add.3.refs_0_), channel_id=1, source_target_pairs={{0,3},{1,2},{2,1},{3,0},{4,7},{5,6},{6,5},{7,4},{8,11},{9,10},{10,... | collective-permute-start | bytes 24584 | tf_op jit(solution)/shard_map/ppermute | solution.py:34
  50.3 0.4 collective-permute-start.23
  50.7 0.7 %collective-permute-start.22 = (f32[16,128]{1,0:T(8,128)S(1)}, f32[16,128]{1,0:T(8,128)S(1)}, u32[]{:S(2)}, u32[]{:S(2)}) collective-permute-start(f32[16,128]{1,0:T(8,128)S(1)} %add.3.refs_0_), channel_id=1, source_target_pairs={{0,1},{1,0},{2,3},{3,2},{4,5},{5,4},{6,7},{7,6},{8,9},{9,8},{10,11... | collective-permute-start | bytes 24584 | tf_op jit(solution)/shard_map/ppermute | solution.py:34
  51.4 1.1 %collective-permute-done.24.refs_3_ = f32[16,128]{1,0:T(8,128)S(1)} collective-permute-done((f32[16,128]{1,0:T(8,128)S(1)}, f32[16,128]{1,0:T(8,128)S(1)}, u32[]{:S(2)}, u32[]{:S(2)}) %collective-permute-start.24) | collective-permute-done | bytes 8224 | tf_op jit(solution)/shard_map/ppermute | solution.py:34
  52.5 2.4 %collective-permute-done.23.refs_2_ = f32[16,128]{1,0:T(8,128)S(1)} collective-permute-done((f32[16,128]{1,0:T(8,128)S(1)}, f32[16,128]{1,0:T(8,128)S(1)}, u32[]{:S(2)}, u32[]{:S(2)}) %collective-permute-start.23) | collective-permute-done | bytes 8224 | tf_op jit(solution)/shard_map/ppermute | solution.py:34
  54.9 0.7 %final.1 = (f32[4,16,128]{2,1,0:T(8,128)}, f32[3,4,16,128]{3,2,1,0:T(8,128)}) custom-call(f32[16,128]{1,0:T(8,128)S(1)} %add.3.refs_0_, f32[16,128]{1,0:T(8,128)S(1)} %collective-permute-done.22.refs_1_, f32[16,128]{1,0:T(8,128)S(1)} %collective-permute-done.23.refs_2_, f32[16,128]{1,0:T(8,128)S(1)} %collective-permute-done.24.refs_3_, ...), custom_call_target="tpu_custom_call" | custom-call | tf_op jit(solution)/shard_map/final/pallas_call | solution.py:106
  (43 shorter events, 0.7 us)
Async XLA Ops:
  0.6 0.8 %copy-start = (s32[1,4,16,128]{3,2,1,0:T(8,128)S(1)}, s32[1,4,16,128]{3,2,1,0:T(8,128)}, u32[]{:S(2)}) copy-start(s32[1,4,16,128]{3,2,1,0:T(8,128)} %param.18) | copy-start | bytes 98308
  1.4 0.9 %copy-start.2 = (f32[1,3,4,16,128]{4,3,2,1,0:T(8,128)S(1)}, f32[1,3,4,16,128]{4,3,2,1,0:T(8,128)}, u32[]{:S(2)}) copy-start(f32[1,3,4,16,128]{4,3,2,1,0:T(8,128)} %param.19) | copy-start | bytes 294916
  2.3 0.8 %copy-start.4 = (s32[1,4,16,128]{3,2,1,0:T(8,128)S(1)}, s32[1,4,16,128]{3,2,1,0:T(8,128)}, u32[]{:S(2)}) copy-start(s32[1,4,16,128]{3,2,1,0:T(8,128)} %param.22) | copy-start | bytes 98308
  3.0 0.8 %copy-start.6 = (f32[1,4,16,128]{3,2,1,0:T(8,128)S(1)}, f32[1,4,16,128]{3,2,1,0:T(8,128)}, u32[]{:S(2)}) copy-start(f32[1,4,16,128]{3,2,1,0:T(8,128)} %param.14) | copy-start | bytes 98308
  3.8 0.8 %copy-start.7 = (s32[1,4,16,128]{3,2,1,0:T(8,128)S(1)}, s32[1,4,16,128]{3,2,1,0:T(8,128)}, u32[]{:S(2)}) copy-start(s32[1,4,16,128]{3,2,1,0:T(8,128)} %param.15) | copy-start | bytes 98308
  4.6 0.8 %copy-start.10 = (f32[1,4,16,128]{3,2,1,0:T(8,128)S(1)}, f32[1,4,16,128]{3,2,1,0:T(8,128)}, u32[]{:S(2)}) copy-start(f32[1,4,16,128]{3,2,1,0:T(8,128)} %param.12) | copy-start | bytes 98308
  5.3 0.8 %copy-start.11 = (f32[1,4,16,128]{3,2,1,0:T(8,128)S(1)}, f32[1,4,16,128]{3,2,1,0:T(8,128)}, u32[]{:S(2)}) copy-start(f32[1,4,16,128]{3,2,1,0:T(8,128)} %param.13) | copy-start | bytes 98308
  6.1 0.9 %copy-start.12 = (f32[1,3,4,16,128]{4,3,2,1,0:T(8,128)S(1)}, f32[1,3,4,16,128]{4,3,2,1,0:T(8,128)}, u32[]{:S(2)}) copy-start(f32[1,3,4,16,128]{4,3,2,1,0:T(8,128)} %param.20) | copy-start | bytes 294916
  7.0 0.8 %copy-start.13 = (f32[1,4,16,128]{3,2,1,0:T(8,128)S(1)}, f32[1,4,16,128]{3,2,1,0:T(8,128)}, u32[]{:S(2)}) copy-start(f32[1,4,16,128]{3,2,1,0:T(8,128)} %param.21) | copy-start | bytes 98308
  8.2 5.6 %collective-permute-start = (f32[7,4,16,128]{3,2,1,0:T(8,128)S(1)}, f32[7,4,16,128]{3,2,1,0:T(8,128)S(1)}, u32[]{:S(2)}, u32[]{:S(2)}) collective-permute-start(f32[7,4,16,128]{3,2,1,0:T(8,128)S(1)} %get-tuple-element.22.refs_0_.refs_8_), channel_id=1, source_target_pairs={{0,4},{1,5},{2,6},{3,7},{4,0},{5,1},{6,2},{7,3},{8,12},{9,13},{10,... | collective-permute-start | bytes 688136 | tf_op jit(solution)/shard_map/ppermute | solution.py:34
  8.2 4.1 %collective-permute-start.1 = (f32[84,128]{1,0:T(8,128)S(1)}, f32[84,128]{1,0:T(8,128)S(1)}, u32[]{:S(2)}, u32[]{:S(2)}) collective-permute-start(f32[84,128]{1,0:T(8,128)S(1)} %get-tuple-element.23), channel_id=1, source_target_pairs={{0,8},{1,9},{2,10},{3,11},{4,12},{5,13},{6,14},{7,15},{8,0},{9,1},... | collective-permute-start | bytes 129032 | tf_op jit(solution)/shard_map/ppermute | solution.py:34
  9.9 2.5 %collective-permute-start.2 = (f32[84,128]{1,0:T(8,128)S(1)}, f32[84,128]{1,0:T(8,128)S(1)}, u32[]{:S(2)}, u32[]{:S(2)}) collective-permute-start(f32[84,128]{1,0:T(8,128)S(1)} %get-tuple-element.24), channel_id=1, source_target_pairs={{0,4},{1,5},{2,6},{3,7},{4,0},{5,1},{6,2},{7,3},{8,16},{9,17},{10,... | collective-permute-start | bytes 129032 | tf_op jit(solution)/shard_map/ppermute | solution.py:34
  12.4 1.2 %collective-permute-start.3 = (f32[84,128]{1,0:T(8,128)S(1)}, f32[84,128]{1,0:T(8,128)S(1)}, u32[]{:S(2)}, u32[]{:S(2)}) collective-permute-start(f32[84,128]{1,0:T(8,128)S(1)} %collective-permute-done.1.refs_2_.refs_10_), channel_id=1, source_target_pairs={{0,4},{1,5},{2,6},{3,7},{4,0},{5,1},{6,2},{7,3},{8,12},{9,13},{10,... | collective-permute-start | bytes 129032 | tf_op jit(solution)/shard_map/ppermute | solution.py:34
  12.4 1.4 %collective-permute-start.4 = (f32[84,128]{1,0:T(8,128)S(1)}, f32[84,128]{1,0:T(8,128)S(1)}, u32[]{:S(2)}, u32[]{:S(2)}) collective-permute-start(f32[84,128]{1,0:T(8,128)S(1)} %collective-permute-done.2.refs_3_.refs_11_), channel_id=1, source_target_pairs={{0,4},{1,5},{2,6},{3,7},{4,0},{5,1},{6,2},{7,3},{8,12},{9,13},{10,... | collective-permute-start | bytes 129032 | tf_op jit(solution)/shard_map/ppermute | solution.py:34
  12.9 6.8 %copy-start.15 = (f32[24,24]{1,0:T(8,128)S(1)}, f32[24,24]{1,0:T(8,128)}, u32[]{:S(2)}) copy-start(f32[24,24]{1,0:T(8,128)} %refs_14_.1) | copy-start | bytes 6916
  13.9 15.8 %copy-start.1 = (s32[1,4,16,128]{3,2,1,0:T(8,128)S(1)}, s32[1,4,16,128]{3,2,1,0:T(8,128)}, u32[]{:S(2)}) copy-start(s32[1,4,16,128]{3,2,1,0:T(8,128)} %param.18) | copy-start | bytes 98308
  13.9 15.8 %copy-start.8 = (s32[1,4,16,128]{3,2,1,0:T(8,128)S(1)}, s32[1,4,16,128]{3,2,1,0:T(8,128)}, u32[]{:S(2)}) copy-start(s32[1,4,16,128]{3,2,1,0:T(8,128)} %param.15) | copy-start | bytes 98308
  13.9 15.8 %copy-start.9 = (f32[1,8,4,16,128]{4,3,2,1,0:T(8,128)S(1)}, f32[1,8,4,16,128]{4,3,2,1,0:T(8,128)}, u32[]{:S(2)}) copy-start(f32[1,8,4,16,128]{4,3,2,1,0:T(8,128)} %param.17) | copy-start | bytes 786436
  13.9 15.8 %copy-start.14 = (s32[1,4,16,128]{3,2,1,0:T(8,128)S(1)}, s32[1,4,16,128]{3,2,1,0:T(8,128)}, u32[]{:S(2)}) copy-start(s32[1,4,16,128]{3,2,1,0:T(8,128)} %param.16) | copy-start | bytes 98308
  13.9 4.9 %collective-permute-start.7 = (f32[64,128]{1,0:T(8,128)S(1)}, f32[64,128]{1,0:T(8,128)S(1)}, u32[]{:S(2)}, u32[]{:S(2)}) collective-permute-start(f32[64,128]{1,0:T(8,128)S(1)} %strain.1), channel_id=1, source_target_pairs={{0,24},{1,25},{2,26},{3,27},{4,28},{5,29},{6,30},{7,31},{8,12},{9,... | collective-permute-start | bytes 98312 | tf_op jit(solution)/shard_map/ppermute | solution.py:34
  14.4 4.5 %collective-permute-start.6 = (f32[64,128]{1,0:T(8,128)S(1)}, f32[64,128]{1,0:T(8,128)S(1)}, u32[]{:S(2)}, u32[]{:S(2)}) collective-permute-start(f32[64,128]{1,0:T(8,128)S(1)} %strain.1), channel_id=1, source_target_pairs={{0,4},{1,5},{2,6},{3,7},{4,0},{5,1},{6,2},{7,3},{8,24},{9,25},{10,... | collective-permute-start | bytes 98312 | tf_op jit(solution)/shard_map/ppermute | solution.py:34
  15.7 3.9 %collective-permute-start.5 = (f32[64,128]{1,0:T(8,128)S(1)}, f32[64,128]{1,0:T(8,128)S(1)}, u32[]{:S(2)}, u32[]{:S(2)}) collective-permute-start(f32[64,128]{1,0:T(8,128)S(1)} %strain.1), channel_id=1, source_target_pairs={{0,4},{1,5},{2,6},{3,7},{4,0},{5,1},{6,2},{7,3},{8,12},{9,13},{10,... | collective-permute-start | bytes 98312 | tf_op jit(solution)/shard_map/ppermute | solution.py:34
  24.0 5.7 %collective-permute-start.8 = (f32[3,4,16,256]{3,2,1,0:T(8,128)S(1)}, f32[3,4,16,256]{3,2,1,0:T(8,128)S(1)}, u32[]{:S(2)}, u32[]{:S(2)}) collective-permute-start(f32[3,4,16,256]{3,2,1,0:T(8,128)S(1)} %get-tuple-element.25.refs_0_), channel_id=1, source_target_pairs={{0,4},{1,5},{2,6},{3,7},{4,0},{5,1},{6,2},{7,3},{8,12},{9,13},{10,... | collective-permute-start | bytes 589832 | tf_op jit(solution)/shard_map/ppermute | solution.py:34
  24.0 4.3 %collective-permute-start.9 = (f32[36,256]{1,0:T(8,128)S(1)}, f32[36,256]{1,0:T(8,128)S(1)}, u32[]{:S(2)}, u32[]{:S(2)}) collective-permute-start(f32[36,256]{1,0:T(8,128)S(1)} %get-tuple-element.26), channel_id=1, source_target_pairs={{0,1},{1,0},{2,3},{3,2},{4,5},{5,4},{6,7},{7,6},{8,9},{9,8},{10,11... | collective-permute-start | bytes 110600 | tf_op jit(solution)/shard_map/ppermute | solution.py:34
  26.1 2.2 %collective-permute-start.10 = (f32[36,256]{1,0:T(8,128)S(1)}, f32[36,256]{1,0:T(8,128)S(1)}, u32[]{:S(2)}, u32[]{:S(2)}) collective-permute-start(f32[36,256]{1,0:T(8,128)S(1)} %get-tuple-element.27), channel_id=1, source_target_pairs={{0,4},{1,2},{2,1},{3,7},{4,0},{5,6},{6,5},{7,3},{8,12},{9,10},{10,... | collective-permute-start | bytes 110600 | tf_op jit(solution)/shard_map/ppermute | solution.py:34
  28.3 1.2 %collective-permute-start.11 = (f32[36,256]{1,0:T(8,128)S(1)}, f32[36,256]{1,0:T(8,128)S(1)}, u32[]{:S(2)}, u32[]{:S(2)}) collective-permute-start(f32[36,256]{1,0:T(8,128)S(1)} %collective-permute-done.9.refs_2_), channel_id=1, source_target_pairs={{0,4},{1,5},{2,6},{3,7},{4,0},{5,1},{6,2},{7,3},{8,12},{9,13},{10,... | collective-permute-start | bytes 110600 | tf_op jit(solution)/shard_map/ppermute | solution.py:34
  28.3 1.4 %collective-permute-start.12 = (f32[36,256]{1,0:T(8,128)S(1)}, f32[36,256]{1,0:T(8,128)S(1)}, u32[]{:S(2)}, u32[]{:S(2)}) collective-permute-start(f32[36,256]{1,0:T(8,128)S(1)} %collective-permute-done.10.refs_3_), channel_id=1, source_target_pairs={{0,4},{1,5},{2,6},{3,7},{4,0},{5,1},{6,2},{7,3},{8,12},{9,13},{10,... | collective-permute-start | bytes 110600 | tf_op jit(solution)/shard_map/ppermute | solution.py:34
  29.7 5.7 %copy-start.5 = (s32[1,4,16,128]{3,2,1,0:T(8,128)S(1)}, s32[1,4,16,128]{3,2,1,0:T(8,128)}, u32[]{:S(2)}) copy-start(s32[1,4,16,128]{3,2,1,0:T(8,128)} %param.22) | copy-start | bytes 98308
  29.7 4.9 %collective-permute-start.15 = (f32[64,128]{1,0:T(8,128)S(1)}, f32[64,128]{1,0:T(8,128)S(1)}, u32[]{:S(2)}, u32[]{:S(2)}) collective-permute-start(f32[64,128]{1,0:T(8,128)S(1)} %get-tuple-element.28), channel_id=1, source_target_pairs={{0,24},{1,25},{2,26},{3,27},{4,28},{5,29},{6,30},{7,31},{8,12},{9,... | collective-permute-start | bytes 98312 | tf_op jit(solution)/shard_map/ppermute | solution.py:34
  30.9 4.1 %collective-permute-start.14 = (f32[64,128]{1,0:T(8,128)S(1)}, f32[64,128]{1,0:T(8,128)S(1)}, u32[]{:S(2)}, u32[]{:S(2)}) collective-permute-start(f32[64,128]{1,0:T(8,128)S(1)} %get-tuple-element.28), channel_id=1, source_target_pairs={{0,4},{1,5},{2,6},{3,7},{4,0},{5,1},{6,2},{7,3},{8,24},{9,25},{10,... | collective-permute-start | bytes 98312 | tf_op jit(solution)/shard_map/ppermute | solution.py:34
  31.5 3.9 %collective-permute-start.13 = (f32[64,128]{1,0:T(8,128)S(1)}, f32[64,128]{1,0:T(8,128)S(1)}, u32[]{:S(2)}, u32[]{:S(2)}) collective-permute-start(f32[64,128]{1,0:T(8,128)S(1)} %get-tuple-element.28), channel_id=1, source_target_pairs={{0,4},{1,5},{2,6},{3,7},{4,0},{5,1},{6,2},{7,3},{8,12},{9,13},{10,... | collective-permute-start | bytes 98312 | tf_op jit(solution)/shard_map/ppermute | solution.py:34
  35.5 5.7 %collective-permute-start.16 = (f32[1,4,16,128]{3,2,1,0:T(8,128)S(1)}, f32[1,4,16,128]{3,2,1,0:T(8,128)S(1)}, u32[]{:S(2)}, u32[]{:S(2)}) collective-permute-start(f32[1,4,16,128]{3,2,1,0:T(8,128)S(1)} %get-tuple-element.29.refs_0_), channel_id=1, source_target_pairs={{0,4},{1,5},{2,6},{3,7},{4,0},{5,1},{6,2},{7,3},{8,12},{9,13},{10,... | collective-permute-start | bytes 98312 | tf_op jit(solution)/shard_map/ppermute | solution.py:34
  35.6 4.3 %collective-permute-start.17 = (f32[12,128]{1,0:T(8,128)S(1)}, f32[12,128]{1,0:T(8,128)S(1)}, u32[]{:S(2)}, u32[]{:S(2)}) collective-permute-start(f32[12,128]{1,0:T(8,128)S(1)} %get-tuple-element.30), channel_id=1, source_target_pairs={{0,1},{1,0},{2,3},{3,2},{4,5},{5,4},{6,7},{7,6},{8,9},{9,8},{10,11... | collective-permute-start | bytes 18440 | tf_op jit(solution)/shard_map/ppermute | solution.py:34
  38.2 1.6 %collective-permute-start.18 = (f32[12,128]{1,0:T(8,128)S(1)}, f32[12,128]{1,0:T(8,128)S(1)}, u32[]{:S(2)}, u32[]{:S(2)}) collective-permute-start(f32[12,128]{1,0:T(8,128)S(1)} %get-tuple-element.31), channel_id=1, source_target_pairs={{0,4},{1,2},{2,1},{3,7},{4,0},{5,6},{6,5},{7,3},{8,12},{9,10},{10,... | collective-permute-start | bytes 18440 | tf_op jit(solution)/shard_map/ppermute | solution.py:34
  39.9 1.2 %collective-permute-start.19 = (f32[12,128]{1,0:T(8,128)S(1)}, f32[12,128]{1,0:T(8,128)S(1)}, u32[]{:S(2)}, u32[]{:S(2)}) collective-permute-start(f32[12,128]{1,0:T(8,128)S(1)} %collective-permute-done.17.refs_2_), channel_id=1, source_target_pairs={{0,4},{1,5},{2,6},{3,7},{4,0},{5,1},{6,2},{7,3},{8,12},{9,13},{10,... | collective-permute-start | bytes 18440 | tf_op jit(solution)/shard_map/ppermute | solution.py:34
  39.9 1.3 %collective-permute-start.20 = (f32[12,128]{1,0:T(8,128)S(1)}, f32[12,128]{1,0:T(8,128)S(1)}, u32[]{:S(2)}, u32[]{:S(2)}) collective-permute-start(f32[12,128]{1,0:T(8,128)S(1)} %collective-permute-done.18.refs_3_), channel_id=1, source_target_pairs={{0,4},{1,5},{2,6},{3,7},{4,0},{5,1},{6,2},{7,3},{8,12},{9,13},{10,... | collective-permute-start | bytes 18440 | tf_op jit(solution)/shard_map/ppermute | solution.py:34
  41.2 13.7 %copy-start.3 = (f32[1,3,4,16,128]{4,3,2,1,0:T(8,128)S(1)}, f32[1,3,4,16,128]{4,3,2,1,0:T(8,128)}, u32[]{:S(2)}) copy-start(f32[1,3,4,16,128]{4,3,2,1,0:T(8,128)} %param.19) | copy-start | bytes 294916
  45.9 1.2 %collective-permute-start.21 = (f32[16,128]{1,0:T(8,128)S(1)}, f32[16,128]{1,0:T(8,128)S(1)}, u32[]{:S(2)}, u32[]{:S(2)}) collective-permute-start(f32[16,128]{1,0:T(8,128)S(1)} %get-tuple-element.36.refs_4_), channel_id=1, source_target_pairs={{0,4},{1,5},{2,6},{3,7},{4,0},{5,1},{6,2},{7,3},{8,12},{9,13},{10,... | collective-permute-start | bytes 24584 | tf_op jit(solution)/shard_map/ppermute | solution.py:34
  47.0 5.4 %collective-permute-start.24 = (f32[16,128]{1,0:T(8,128)S(1)}, f32[16,128]{1,0:T(8,128)S(1)}, u32[]{:S(2)}, u32[]{:S(2)}) collective-permute-start(f32[16,128]{1,0:T(8,128)S(1)} %add.3.refs_0_), channel_id=1, source_target_pairs={{0,3},{1,2},{2,1},{3,0},{4,7},{5,6},{6,5},{7,4},{8,11},{9,10},{10,... | collective-permute-start | bytes 24584 | tf_op jit(solution)/shard_map/ppermute | solution.py:34
  50.3 4.5 %collective-permute-start.23 = (f32[16,128]{1,0:T(8,128)S(1)}, f32[16,128]{1,0:T(8,128)S(1)}, u32[]{:S(2)}, u32[]{:S(2)}) collective-permute-start(f32[16,128]{1,0:T(8,128)S(1)} %add.3.refs_0_), channel_id=1, source_target_pairs={{0,2},{1,3},{2,0},{3,1},{4,6},{5,7},{6,4},{7,5},{8,10},{9,11},{10,... | collective-permute-start | bytes 24584 | tf_op jit(solution)/shard_map/ppermute | solution.py:34
  50.7 4.2 %collective-permute-start.22 = (f32[16,128]{1,0:T(8,128)S(1)}, f32[16,128]{1,0:T(8,128)S(1)}, u32[]{:S(2)}, u32[]{:S(2)}) collective-permute-start(f32[16,128]{1,0:T(8,128)S(1)} %add.3.refs_0_), channel_id=1, source_target_pairs={{0,1},{1,0},{2,3},{3,2},{4,5},{5,4},{6,7},{7,6},{8,9},{9,8},{10,11... | collective-permute-start | bytes 24584 | tf_op jit(solution)/shard_map/ppermute | solution.py:34

commit v4 on v3

--- a/solution.py
+++ b/solution.py
@@ -103,6 +103,8 @@
     def expanded(*refs):
         return body(*[refs[i] for i in spots], *refs[len(unique) :])
 
+    if space is pltpu.HBM:
+        unique = [pltpu.with_memory_space_constraint(v, space) for v in unique]
     return pl.pallas_call(
         expanded,
         name=name,

time: 56.2 us -> 49.4 us (0.88)
  local copies, waits for them, and re-layouts: 7.12 us -> 0.05 us
  Pallas kernels: 10.3 us -> 11 us
    unnamed x32 -> x20, local copies, waits for them, and re-layouts: 7.12 us -> 0.05 us
    pallas_call x8, Pallas kernels: 10.3 us -> 11 us  [call(): pl.pallas_call(expanded, name=name, out_shape=[o if hasattr(o, 'dtype') e...]
where the time goes in v4:
time: 49.4 us; the launch traced here: 49.2 us
  waiting for transfers between devices  19.6 us (40%)
  starting transfers between devices  17.9 us (36%)
  Pallas kernels  11 us (22%)
  between operations  0.78 us (2%)
    ppermute x25, waiting for transfers between devices, permuted(): return lax.ppermute(value, ALL, pairs)  19.6 us
    ppermute x25, starting transfers between devices, permuted(): return lax.ppermute(value, ALL, pairs)  17.9 us
    pallas_call x8, Pallas kernels, call(): pl.pallas_call(expanded, name=name, out_shape=[o if hasattr(o, 'dtype') e...  11 us
  transfers between devices with their start and end apart: 25, of which 18 were waited for; matrix products, arithmetic and copies ran while one was open for 0% of the time, Pallas kernels for 0%

profile of v4, /device:TPU:6, one launch (start us, length us, event | category | flops | bytes accessed | tf_op | source)
XLA Modules:
  0.0 49.2 jit_solution(8196984824621875571)
XLA Ops:
  0.6 1.1 %pack.1 = (f32[7,4,16,128]{3,2,1,0:T(8,128)S(1)}, f32[84,128]{1,0:T(8,128)S(1)}, f32[84,128]{1,0:T(8,128)S(1)}) custom-call(f32[4,16,128]{2,1,0:T(8,128)} %bitcast.29, f32[4,16,128]{2,1,0:T(8,128)} %bitcast.31, f32[4,16,128]{2,1,0:T(8,128)} %bitcast.22, s32[4,16,128]{2,1,0:T(8,128)} %bitcast.25, s32[4,16,128]{2,1,0:T(8,128)} %bitcast.13, ...), custom_call_target="tpu_custom_call" | custom-call | tf_op jit(solution)/shard_map/pack/pallas_call | solution.py:108
  1.7 0.1 collective-permute-start
  1.8 1.6 %collective-permute-start.1 = (f32[84,128]{1,0:T(8,128)S(1)}, f32[84,128]{1,0:T(8,128)S(1)}, u32[]{:S(2)}, u32[]{:S(2)}) collective-permute-start(f32[84,128]{1,0:T(8,128)S(1)} %get-tuple-element.23), channel_id=1, source_target_pairs={{0,8},{1,9},{2,10},{3,11},{4,12},{5,13},{6,14},{7,15},{8,0},{9,1},... | collective-permute-start | bytes 129032 | tf_op jit(solution)/shard_map/ppermute | solution.py:34
  3.4 0.2 collective-permute-start.2
  3.6 2.3 %collective-permute-done.1.refs_2_.refs_10_ = f32[84,128]{1,0:T(8,128)S(1)} collective-permute-done((f32[84,128]{1,0:T(8,128)S(1)}, f32[84,128]{1,0:T(8,128)S(1)}, u32[]{:S(2)}, u32[]{:S(2)}) %collective-permute-start.1) | collective-permute-done | bytes 43040 | tf_op jit(solution)/shard_map/ppermute | solution.py:34
  5.9 0.5 %collective-permute-start.4 = (f32[84,128]{1,0:T(8,128)S(1)}, f32[84,128]{1,0:T(8,128)S(1)}, u32[]{:S(2)}, u32[]{:S(2)}) collective-permute-start(f32[84,128]{1,0:T(8,128)S(1)} %collective-permute-done.2.refs_3_.refs_11_), channel_id=1, source_target_pairs={{0,4},{1,5},{2,6},{3,7},{4,0},{5,1},{6,2},{7,3},{8,12},{9,13},{10,... | collective-permute-start | bytes 129032 | tf_op jit(solution)/shard_map/ppermute | solution.py:34
  6.5 0.0 copy-start.9
  6.5 0.7 %collective-permute-done.3.refs_4_.refs_12_ = f32[84,128]{1,0:T(8,128)S(1)} collective-permute-done((f32[84,128]{1,0:T(8,128)S(1)}, f32[84,128]{1,0:T(8,128)S(1)}, u32[]{:S(2)}, u32[]{:S(2)}) %collective-permute-start.3) | collective-permute-done | bytes 43040 | tf_op jit(solution)/shard_map/ppermute | solution.py:34
  7.1 0.2 collective-permute-done.4.refs_5_.refs_13_
  7.3 0.1 strain.1
  7.5 0.0 copy-start.5
  7.5 0.0 copy-start.8
  7.5 0.5 %collective-permute-start.7 = (f32[64,128]{1,0:T(8,128)S(1)}, f32[64,128]{1,0:T(8,128)S(1)}, u32[]{:S(2)}, u32[]{:S(2)}) collective-permute-start(f32[64,128]{1,0:T(8,128)S(1)} %strain.1), channel_id=1, source_target_pairs={{0,24},{1,25},{2,26},{3,27},{4,28},{5,29},{6,30},{7,31},{8,12},{9,... | collective-permute-start | bytes 98312 | tf_op jit(solution)/shard_map/ppermute | solution.py:34
  8.0 1.3 %collective-permute-start.6 = (f32[64,128]{1,0:T(8,128)S(1)}, f32[64,128]{1,0:T(8,128)S(1)}, u32[]{:S(2)}, u32[]{:S(2)}) collective-permute-start(f32[64,128]{1,0:T(8,128)S(1)} %strain.1), channel_id=1, source_target_pairs={{0,4},{1,5},{2,6},{3,7},{4,0},{5,1},{6,2},{7,3},{8,24},{9,25},{10,... | collective-permute-start | bytes 98312 | tf_op jit(solution)/shard_map/ppermute | solution.py:34
  9.3 0.5 collective-permute-start.5
  9.8 2.6 %collective-permute-done.7.refs_2_.refs_5_ = f32[64,128]{1,0:T(8,128)S(1)} collective-permute-done((f32[64,128]{1,0:T(8,128)S(1)}, f32[64,128]{1,0:T(8,128)S(1)}, u32[]{:S(2)}, u32[]{:S(2)}) %collective-permute-start.7) | collective-permute-done | bytes 32800 | tf_op jit(solution)/shard_map/ppermute | solution.py:34
  12.4 0.1 collective-permute-done.6.refs_1_.refs_4_
  12.4 0.8 %collective-permute-done.5.refs_0_.refs_3_ = f32[64,128]{1,0:T(8,128)S(1)} collective-permute-done((f32[64,128]{1,0:T(8,128)S(1)}, f32[64,128]{1,0:T(8,128)S(1)}, u32[]{:S(2)}, u32[]{:S(2)}) %collective-permute-start.5) | collective-permute-done | bytes 32800 | tf_op jit(solution)/shard_map/ppermute | solution.py:34
  13.3 4.3 %gather.1 = (f32[3,4,16,256]{3,2,1,0:T(8,128)S(1)}, f32[36,256]{1,0:T(8,128)S(1)}, f32[36,256]{1,0:T(8,128)S(1)}, f32[3,10,32,128]{3,2,1,0:T(8,128)S(1)}, f32[10...) custom-call(f32[64,128]{1,0:T(8,128)S(1)} %collective-permute-done.5.refs_0_.refs_3_, ...), custom_call_target="tpu_custom_call" | custom-call | tf_op jit(solution)/shard_map/gather/pallas_call | solution.py:108
  17.6 0.1 collective-permute-start.8
  17.7 2.1 %collective-permute-start.9 = (f32[36,256]{1,0:T(8,128)S(1)}, f32[36,256]{1,0:T(8,128)S(1)}, u32[]{:S(2)}, u32[]{:S(2)}) collective-permute-start(f32[36,256]{1,0:T(8,128)S(1)} %get-tuple-element.26), channel_id=1, source_target_pairs={{0,1},{1,0},{2,3},{3,2},{4,5},{5,4},{6,7},{7,6},{8,9},{9,8},{10,11... | collective-permute-start | bytes 110600 | tf_op jit(solution)/shard_map/ppermute | solution.py:34
  19.8 0.2 collective-permute-start.10
  19.9 2.0 %collective-permute-done.9.refs_2_ = f32[36,256]{1,0:T(8,128)S(1)} collective-permute-done((f32[36,256]{1,0:T(8,128)S(1)}, f32[36,256]{1,0:T(8,128)S(1)}, u32[]{:S(2)}, u32[]{:S(2)}) %collective-permute-start.9) | collective-permute-done | bytes 36896 | tf_op jit(solution)/shard_map/ppermute | solution.py:34
  22.0 0.5 %collective-permute-start.12 = (f32[36,256]{1,0:T(8,128)S(1)}, f32[36,256]{1,0:T(8,128)S(1)}, u32[]{:S(2)}, u32[]{:S(2)}) collective-permute-start(f32[36,256]{1,0:T(8,128)S(1)} %collective-permute-done.10.refs_3_), channel_id=1, source_target_pairs={{0,4},{1,5},{2,6},{3,7},{4,0},{5,1},{6,2},{7,3},{8,12},{9,13},{10,... | collective-permute-start | bytes 110600 | tf_op jit(solution)/shard_map/ppermute | solution.py:34
  22.5 0.7 %collective-permute-done.11.refs_4_ = f32[36,256]{1,0:T(8,128)S(1)} collective-permute-done((f32[36,256]{1,0:T(8,128)S(1)}, f32[36,256]{1,0:T(8,128)S(1)}, u32[]{:S(2)}, u32[]{:S(2)}) %collective-permute-start.11) | collective-permute-done | bytes 36896 | tf_op jit(solution)/shard_map/ppermute | solution.py:34
  23.2 0.2 collective-permute-done.12.refs_5_
  23.4 1.1 %collective-permute-start.15 = (f32[64,128]{1,0:T(8,128)S(1)}, f32[64,128]{1,0:T(8,128)S(1)}, u32[]{:S(2)}, u32[]{:S(2)}) collective-permute-start(f32[64,128]{1,0:T(8,128)S(1)} %get-tuple-element.28), channel_id=1, source_target_pairs={{0,24},{1,25},{2,26},{3,27},{4,28},{5,29},{6,30},{7,31},{8,12},{9,... | collective-permute-start | bytes 98312 | tf_op jit(solution)/shard_map/ppermute | solution.py:34
  24.5 0.7 %collective-permute-start.14 = (f32[64,128]{1,0:T(8,128)S(1)}, f32[64,128]{1,0:T(8,128)S(1)}, u32[]{:S(2)}, u32[]{:S(2)}) collective-permute-start(f32[64,128]{1,0:T(8,128)S(1)} %get-tuple-element.28), channel_id=1, source_target_pairs={{0,4},{1,5},{2,6},{3,7},{4,0},{5,1},{6,2},{7,3},{8,24},{9,25},{10,... | collective-permute-start | bytes 98312 | tf_op jit(solution)/shard_map/ppermute | solution.py:34
  25.2 0.4 collective-permute-start.13
  25.6 2.7 %collective-permute-done.15.refs_2_ = f32[64,128]{1,0:T(8,128)S(1)} collective-permute-done((f32[64,128]{1,0:T(8,128)S(1)}, f32[64,128]{1,0:T(8,128)S(1)}, u32[]{:S(2)}, u32[]{:S(2)}) %collective-permute-start.15) | collective-permute-done | bytes 32800 | tf_op jit(solution)/shard_map/ppermute | solution.py:34
  28.3 0.4 collective-permute-done.14.refs_1_
  28.6 0.5 collective-permute-done.13.refs_0_
  29.1 0.1 collective-permute-start.16
  29.2 2.7 %collective-permute-start.17 = (f32[12,128]{1,0:T(8,128)S(1)}, f32[12,128]{1,0:T(8,128)S(1)}, u32[]{:S(2)}, u32[]{:S(2)}) collective-permute-start(f32[12,128]{1,0:T(8,128)S(1)} %get-tuple-element.30), channel_id=1, source_target_pairs={{0,1},{1,0},{2,3},{3,2},{4,5},{5,4},{6,7},{7,6},{8,9},{9,8},{10,11... | collective-permute-start | bytes 18440 | tf_op jit(solution)/shard_map/ppermute | solution.py:34
  31.9 0.2 collective-permute-start.18
  32.0 1.5 %collective-permute-done.17.refs_2_ = f32[12,128]{1,0:T(8,128)S(1)} collective-permute-done((f32[12,128]{1,0:T(8,128)S(1)}, f32[12,128]{1,0:T(8,128)S(1)}, u32[]{:S(2)}, u32[]{:S(2)}) %collective-permute-start.17) | collective-permute-done | bytes 6176 | tf_op jit(solution)/shard_map/ppermute | solution.py:34
  33.5 0.5 %collective-permute-start.20 = (f32[12,128]{1,0:T(8,128)S(1)}, f32[12,128]{1,0:T(8,128)S(1)}, u32[]{:S(2)}, u32[]{:S(2)}) collective-permute-start(f32[12,128]{1,0:T(8,128)S(1)} %collective-permute-done.18.refs_3_), channel_id=1, source_target_pairs={{0,4},{1,5},{2,6},{3,7},{4,0},{5,1},{6,2},{7,3},{8,12},{9,13},{10,... | collective-permute-start | bytes 18440 | tf_op jit(solution)/shard_map/ppermute | solution.py:34
  34.0 0.7 %collective-permute-done.19.refs_4_ = f32[12,128]{1,0:T(8,128)S(1)} collective-permute-done((f32[12,128]{1,0:T(8,128)S(1)}, f32[12,128]{1,0:T(8,128)S(1)}, u32[]{:S(2)}, u32[]{:S(2)}) %collective-permute-start.19) | collective-permute-done | bytes 6176 | tf_op jit(solution)/shard_map/ppermute | solution.py:34
  34.7 0.2 collective-permute-done.20.refs_5_
  34.9 4.6 %krylov.1 = (f32[3,4,16,128]{3,2,1,0:T(8,128)S(1)}, f32[3,4,16,128]{3,2,1,0:T(8,128)S(1)}, f32[16,128]{1,0:T(8,128)S(1)}) custom-call(f32[1,4,16,128]{3,2,1,0:T(8,128)S(1)} %get-tuple-element.29.refs_0_, f32[1,4,16,128]{3,2,1,0:T(8,128)S(1)} %collective-permute-done.16.refs_1_, f32[12,128]{1,0:T(8,128)S(1)} %collective-permute-done.17.refs_2_, ...), custom_call_target="tpu_custom_call" | custom-call | tf_op jit(solution)/shard_map/krylov/pallas_call | solution.py:108
  39.5 0.3 collective-permute-start.21
  39.8 0.8 %collective-permute-done.21 = f32[16,128]{1,0:T(8,128)S(1)} collective-permute-done((f32[16,128]{1,0:T(8,128)S(1)}, f32[16,128]{1,0:T(8,128)S(1)}, u32[]{:S(2)}, u32[]{:S(2)}) %collective-permute-start.21) | collective-permute-done | bytes 8224 | tf_op jit(solution)/shard_map/ppermute | solution.py:34
  40.7 3.3 %collective-permute-start.24 = (f32[16,128]{1,0:T(8,128)S(1)}, f32[16,128]{1,0:T(8,128)S(1)}, u32[]{:S(2)}, u32[]{:S(2)}) collective-permute-start(f32[16,128]{1,0:T(8,128)S(1)} %add.3.refs_0_), channel_id=1, source_target_pairs={{0,3},{1,2},{2,1},{3,0},{4,7},{5,6},{6,5},{7,4},{8,11},{9,10},{10,... | collective-permute-start | bytes 24584 | tf_op jit(solution)/shard_map/ppermute | solution.py:34
  43.9 0.4 collective-permute-start.23
  44.3 0.7 %collective-permute-start.22 = (f32[16,128]{1,0:T(8,128)S(1)}, f32[16,128]{1,0:T(8,128)S(1)}, u32[]{:S(2)}, u32[]{:S(2)}) collective-permute-start(f32[16,128]{1,0:T(8,128)S(1)} %add.3.refs_0_), channel_id=1, source_target_pairs={{0,1},{1,0},{2,3},{3,2},{4,5},{5,4},{6,7},{7,6},{8,9},{9,8},{10,11... | collective-permute-start | bytes 24584 | tf_op jit(solution)/shard_map/ppermute | solution.py:34
  45.1 1.1 %collective-permute-done.24.refs_3_ = f32[16,128]{1,0:T(8,128)S(1)} collective-permute-done((f32[16,128]{1,0:T(8,128)S(1)}, f32[16,128]{1,0:T(8,128)S(1)}, u32[]{:S(2)}, u32[]{:S(2)}) %collective-permute-start.24) | collective-permute-done | bytes 8224 | tf_op jit(solution)/shard_map/ppermute | solution.py:34
  46.1 2.4 %collective-permute-done.23.refs_2_ = f32[16,128]{1,0:T(8,128)S(1)} collective-permute-done((f32[16,128]{1,0:T(8,128)S(1)}, f32[16,128]{1,0:T(8,128)S(1)}, u32[]{:S(2)}, u32[]{:S(2)}) %collective-permute-start.23) | collective-permute-done | bytes 8224 | tf_op jit(solution)/shard_map/ppermute | solution.py:34
  48.5 0.7 %final.1 = (f32[4,16,128]{2,1,0:T(8,128)}, f32[3,4,16,128]{3,2,1,0:T(8,128)}) custom-call(f32[16,128]{1,0:T(8,128)S(1)} %add.3.refs_0_, f32[16,128]{1,0:T(8,128)S(1)} %collective-permute-done.22.refs_1_, f32[16,128]{1,0:T(8,128)S(1)} %collective-permute-done.23.refs_2_, f32[16,128]{1,0:T(8,128)S(1)} %collective-permute-done.24.refs_3_, ...), custom_call_target="tpu_custom_call" | custom-call | tf_op jit(solution)/shard_map/final/pallas_call | solution.py:108
  (31 shorter events, 0.1 us)
Async XLA Ops:
  0.6 5.8 %copy-start = (s32[1,4,16,128]{3,2,1,0:T(8,128)S(1)}, s32[1,4,16,128]{3,2,1,0:T(8,128)}, u32[]{:S(2)}) copy-start(s32[1,4,16,128]{3,2,1,0:T(8,128)} %param.18) | copy-start | bytes 98308
  1.7 5.6 %collective-permute-start = (f32[7,4,16,128]{3,2,1,0:T(8,128)S(1)}, f32[7,4,16,128]{3,2,1,0:T(8,128)S(1)}, u32[]{:S(2)}, u32[]{:S(2)}) collective-permute-start(f32[7,4,16,128]{3,2,1,0:T(8,128)S(1)} %get-tuple-element.22.refs_0_.refs_8_), channel_id=1, source_target_pairs={{0,4},{1,5},{2,6},{3,7},{4,0},{5,1},{6,2},{7,3},{8,12},{9,13},{10,... | collective-permute-start | bytes 688136 | tf_op jit(solution)/shard_map/ppermute | solution.py:34
  1.8 4.1 %collective-permute-start.1 = (f32[84,128]{1,0:T(8,128)S(1)}, f32[84,128]{1,0:T(8,128)S(1)}, u32[]{:S(2)}, u32[]{:S(2)}) collective-permute-start(f32[84,128]{1,0:T(8,128)S(1)} %get-tuple-element.23), channel_id=1, source_target_pairs={{0,8},{1,9},{2,10},{3,11},{4,12},{5,13},{6,14},{7,15},{8,0},{9,1},... | collective-permute-start | bytes 129032 | tf_op jit(solution)/shard_map/ppermute | solution.py:34
  3.4 3.9 %copy-start.2 = (s32[1,4,16,128]{3,2,1,0:T(8,128)S(1)}, s32[1,4,16,128]{3,2,1,0:T(8,128)}, u32[]{:S(2)}) copy-start(s32[1,4,16,128]{3,2,1,0:T(8,128)} %param.22) | copy-start | bytes 98308
  3.4 2.5 %collective-permute-start.2 = (f32[84,128]{1,0:T(8,128)S(1)}, f32[84,128]{1,0:T(8,128)S(1)}, u32[]{:S(2)}, u32[]{:S(2)}) collective-permute-start(f32[84,128]{1,0:T(8,128)S(1)} %get-tuple-element.24), channel_id=1, source_target_pairs={{0,4},{1,5},{2,6},{3,7},{4,0},{5,1},{6,2},{7,3},{8,16},{9,17},{10,... | collective-permute-start | bytes 129032 | tf_op jit(solution)/shard_map/ppermute | solution.py:34
  5.9 1.2 %collective-permute-start.3 = (f32[84,128]{1,0:T(8,128)S(1)}, f32[84,128]{1,0:T(8,128)S(1)}, u32[]{:S(2)}, u32[]{:S(2)}) collective-permute-start(f32[84,128]{1,0:T(8,128)S(1)} %collective-permute-done.1.refs_2_.refs_10_), channel_id=1, source_target_pairs={{0,4},{1,5},{2,6},{3,7},{4,0},{5,1},{6,2},{7,3},{8,12},{9,13},{10,... | collective-permute-start | bytes 129032 | tf_op jit(solution)/shard_map/ppermute | solution.py:34
  5.9 1.4 %collective-permute-start.4 = (f32[84,128]{1,0:T(8,128)S(1)}, f32[84,128]{1,0:T(8,128)S(1)}, u32[]{:S(2)}, u32[]{:S(2)}) collective-permute-start(f32[84,128]{1,0:T(8,128)S(1)} %collective-permute-done.2.refs_3_.refs_11_), channel_id=1, source_target_pairs={{0,4},{1,5},{2,6},{3,7},{4,0},{5,1},{6,2},{7,3},{8,12},{9,13},{10,... | collective-permute-start | bytes 129032 | tf_op jit(solution)/shard_map/ppermute | solution.py:34
  6.4 6.8 %copy-start.3 = (f32[1,4,16,128]{3,2,1,0:T(8,128)S(1)}, f32[1,4,16,128]{3,2,1,0:T(8,128)}, u32[]{:S(2)}) copy-start(f32[1,4,16,128]{3,2,1,0:T(8,128)} %param.14) | copy-start | bytes 98308
  6.4 6.8 %copy-start.4 = (s32[1,4,16,128]{3,2,1,0:T(8,128)S(1)}, s32[1,4,16,128]{3,2,1,0:T(8,128)}, u32[]{:S(2)}) copy-start(s32[1,4,16,128]{3,2,1,0:T(8,128)} %param.15) | copy-start | bytes 98308
  6.4 6.8 %copy-start.6 = (f32[1,4,16,128]{3,2,1,0:T(8,128)S(1)}, f32[1,4,16,128]{3,2,1,0:T(8,128)}, u32[]{:S(2)}) copy-start(f32[1,4,16,128]{3,2,1,0:T(8,128)} %param.12) | copy-start | bytes 98308
  6.4 6.8 %copy-start.7 = (f32[1,4,16,128]{3,2,1,0:T(8,128)S(1)}, f32[1,4,16,128]{3,2,1,0:T(8,128)}, u32[]{:S(2)}) copy-start(f32[1,4,16,128]{3,2,1,0:T(8,128)} %param.13) | copy-start | bytes 98308
  6.5 6.8 %copy-start.9 = (f32[24,24]{1,0:T(8,128)S(1)}, f32[24,24]{1,0:T(8,128)}, u32[]{:S(2)}) copy-start(f32[24,24]{1,0:T(8,128)} %refs_14_.1) | copy-start | bytes 6916
  7.5 15.9 %copy-start.5 = (f32[1,8,4,16,128]{4,3,2,1,0:T(8,128)S(1)}, f32[1,8,4,16,128]{4,3,2,1,0:T(8,128)}, u32[]{:S(2)}) copy-start(f32[1,8,4,16,128]{4,3,2,1,0:T(8,128)} %param.17) | copy-start | bytes 786436
  7.5 15.9 %copy-start.8 = (s32[1,4,16,128]{3,2,1,0:T(8,128)S(1)}, s32[1,4,16,128]{3,2,1,0:T(8,128)}, u32[]{:S(2)}) copy-start(s32[1,4,16,128]{3,2,1,0:T(8,128)} %param.16) | copy-start | bytes 98308
  7.5 4.9 %collective-permute-start.7 = (f32[64,128]{1,0:T(8,128)S(1)}, f32[64,128]{1,0:T(8,128)S(1)}, u32[]{:S(2)}, u32[]{:S(2)}) collective-permute-start(f32[64,128]{1,0:T(8,128)S(1)} %strain.1), channel_id=1, source_target_pairs={{0,24},{1,25},{2,26},{3,27},{4,28},{5,29},{6,30},{7,31},{8,12},{9,... | collective-permute-start | bytes 98312 | tf_op jit(solution)/shard_map/ppermute | solution.py:34
  8.0 4.4 %collective-permute-start.6 = (f32[64,128]{1,0:T(8,128)S(1)}, f32[64,128]{1,0:T(8,128)S(1)}, u32[]{:S(2)}, u32[]{:S(2)}) collective-permute-start(f32[64,128]{1,0:T(8,128)S(1)} %strain.1), channel_id=1, source_target_pairs={{0,4},{1,5},{2,6},{3,7},{4,0},{5,1},{6,2},{7,3},{8,24},{9,25},{10,... | collective-permute-start | bytes 98312 | tf_op jit(solution)/shard_map/ppermute | solution.py:34
  9.3 3.9 %collective-permute-start.5 = (f32[64,128]{1,0:T(8,128)S(1)}, f32[64,128]{1,0:T(8,128)S(1)}, u32[]{:S(2)}, u32[]{:S(2)}) collective-permute-start(f32[64,128]{1,0:T(8,128)S(1)} %strain.1), channel_id=1, source_target_pairs={{0,4},{1,5},{2,6},{3,7},{4,0},{5,1},{6,2},{7,3},{8,12},{9,13},{10,... | collective-permute-start | bytes 98312 | tf_op jit(solution)/shard_map/ppermute | solution.py:34
  17.6 5.7 %collective-permute-start.8 = (f32[3,4,16,256]{3,2,1,0:T(8,128)S(1)}, f32[3,4,16,256]{3,2,1,0:T(8,128)S(1)}, u32[]{:S(2)}, u32[]{:S(2)}) collective-permute-start(f32[3,4,16,256]{3,2,1,0:T(8,128)S(1)} %get-tuple-element.25.refs_0_), channel_id=1, source_target_pairs={{0,4},{1,5},{2,6},{3,7},{4,0},{5,1},{6,2},{7,3},{8,12},{9,13},{10,... | collective-permute-start | bytes 589832 | tf_op jit(solution)/shard_map/ppermute | solution.py:34
  17.7 4.2 %collective-permute-start.9 = (f32[36,256]{1,0:T(8,128)S(1)}, f32[36,256]{1,0:T(8,128)S(1)}, u32[]{:S(2)}, u32[]{:S(2)}) collective-permute-start(f32[36,256]{1,0:T(8,128)S(1)} %get-tuple-element.26), channel_id=1, source_target_pairs={{0,1},{1,0},{2,3},{3,2},{4,5},{5,4},{6,7},{7,6},{8,9},{9,8},{10,11... | collective-permute-start | bytes 110600 | tf_op jit(solution)/shard_map/ppermute | solution.py:34
  19.8 2.2 %collective-permute-start.10 = (f32[36,256]{1,0:T(8,128)S(1)}, f32[36,256]{1,0:T(8,128)S(1)}, u32[]{:S(2)}, u32[]{:S(2)}) collective-permute-start(f32[36,256]{1,0:T(8,128)S(1)} %get-tuple-element.27), channel_id=1, source_target_pairs={{0,4},{1,2},{2,1},{3,7},{4,0},{5,6},{6,5},{7,3},{8,12},{9,10},{10,... | collective-permute-start | bytes 110600 | tf_op jit(solution)/shard_map/ppermute | solution.py:34
  22.0 1.2 %collective-permute-start.11 = (f32[36,256]{1,0:T(8,128)S(1)}, f32[36,256]{1,0:T(8,128)S(1)}, u32[]{:S(2)}, u32[]{:S(2)}) collective-permute-start(f32[36,256]{1,0:T(8,128)S(1)} %collective-permute-done.9.refs_2_), channel_id=1, source_target_pairs={{0,4},{1,5},{2,6},{3,7},{4,0},{5,1},{6,2},{7,3},{8,12},{9,13},{10,... | collective-permute-start | bytes 110600 | tf_op jit(solution)/shard_map/ppermute | solution.py:34
  22.0 1.4 %collective-permute-start.12 = (f32[36,256]{1,0:T(8,128)S(1)}, f32[36,256]{1,0:T(8,128)S(1)}, u32[]{:S(2)}, u32[]{:S(2)}) collective-permute-start(f32[36,256]{1,0:T(8,128)S(1)} %collective-permute-done.10.refs_3_), channel_id=1, source_target_pairs={{0,4},{1,5},{2,6},{3,7},{4,0},{5,1},{6,2},{7,3},{8,12},{9,13},{10,... | collective-permute-start | bytes 110600 | tf_op jit(solution)/shard_map/ppermute | solution.py:34
  23.4 4.9 %collective-permute-start.15 = (f32[64,128]{1,0:T(8,128)S(1)}, f32[64,128]{1,0:T(8,128)S(1)}, u32[]{:S(2)}, u32[]{:S(2)}) collective-permute-start(f32[64,128]{1,0:T(8,128)S(1)} %get-tuple-element.28), channel_id=1, source_target_pairs={{0,24},{1,25},{2,26},{3,27},{4,28},{5,29},{6,30},{7,31},{8,12},{9,... | collective-permute-start | bytes 98312 | tf_op jit(solution)/shard_map/ppermute | solution.py:34
  24.5 4.1 %collective-permute-start.14 = (f32[64,128]{1,0:T(8,128)S(1)}, f32[64,128]{1,0:T(8,128)S(1)}, u32[]{:S(2)}, u32[]{:S(2)}) collective-permute-start(f32[64,128]{1,0:T(8,128)S(1)} %get-tuple-element.28), channel_id=1, source_target_pairs={{0,4},{1,5},{2,6},{3,7},{4,0},{5,1},{6,2},{7,3},{8,24},{9,25},{10,... | collective-permute-start | bytes 98312 | tf_op jit(solution)/shard_map/ppermute | solution.py:34
  25.2 3.9 %collective-permute-start.13 = (f32[64,128]{1,0:T(8,128)S(1)}, f32[64,128]{1,0:T(8,128)S(1)}, u32[]{:S(2)}, u32[]{:S(2)}) collective-permute-start(f32[64,128]{1,0:T(8,128)S(1)} %get-tuple-element.28), channel_id=1, source_target_pairs={{0,4},{1,5},{2,6},{3,7},{4,0},{5,1},{6,2},{7,3},{8,12},{9,13},{10,... | collective-permute-start | bytes 98312 | tf_op jit(solution)/shard_map/ppermute | solution.py:34
  29.1 5.7 %collective-permute-start.16 = (f32[1,4,16,128]{3,2,1,0:T(8,128)S(1)}, f32[1,4,16,128]{3,2,1,0:T(8,128)S(1)}, u32[]{:S(2)}, u32[]{:S(2)}) collective-permute-start(f32[1,4,16,128]{3,2,1,0:T(8,128)S(1)} %get-tuple-element.29.refs_0_), channel_id=1, source_target_pairs={{0,4},{1,5},{2,6},{3,7},{4,0},{5,1},{6,2},{7,3},{8,12},{9,13},{10,... | collective-permute-start | bytes 98312 | tf_op jit(solution)/shard_map/ppermute | solution.py:34
  29.2 4.3 %collective-permute-start.17 = (f32[12,128]{1,0:T(8,128)S(1)}, f32[12,128]{1,0:T(8,128)S(1)}, u32[]{:S(2)}, u32[]{:S(2)}) collective-permute-start(f32[12,128]{1,0:T(8,128)S(1)} %get-tuple-element.30), channel_id=1, source_target_pairs={{0,1},{1,0},{2,3},{3,2},{4,5},{5,4},{6,7},{7,6},{8,9},{9,8},{10,11... | collective-permute-start | bytes 18440 | tf_op jit(solution)/shard_map/ppermute | solution.py:34
  31.9 1.6 %collective-permute-start.18 = (f32[12,128]{1,0:T(8,128)S(1)}, f32[12,128]{1,0:T(8,128)S(1)}, u32[]{:S(2)}, u32[]{:S(2)}) collective-permute-start(f32[12,128]{1,0:T(8,128)S(1)} %get-tuple-element.31), channel_id=1, source_target_pairs={{0,4},{1,2},{2,1},{3,7},{4,0},{5,6},{6,5},{7,3},{8,12},{9,10},{10,... | collective-permute-start | bytes 18440 | tf_op jit(solution)/shard_map/ppermute | solution.py:34
  33.5 1.2 %collective-permute-start.19 = (f32[12,128]{1,0:T(8,128)S(1)}, f32[12,128]{1,0:T(8,128)S(1)}, u32[]{:S(2)}, u32[]{:S(2)}) collective-permute-start(f32[12,128]{1,0:T(8,128)S(1)} %collective-permute-done.17.refs_2_), channel_id=1, source_target_pairs={{0,4},{1,5},{2,6},{3,7},{4,0},{5,1},{6,2},{7,3},{8,12},{9,13},{10,... | collective-permute-start | bytes 18440 | tf_op jit(solution)/shard_map/ppermute | solution.py:34
  33.5 1.3 %collective-permute-start.20 = (f32[12,128]{1,0:T(8,128)S(1)}, f32[12,128]{1,0:T(8,128)S(1)}, u32[]{:S(2)}, u32[]{:S(2)}) collective-permute-start(f32[12,128]{1,0:T(8,128)S(1)} %collective-permute-done.18.refs_3_), channel_id=1, source_target_pairs={{0,4},{1,5},{2,6},{3,7},{4,0},{5,1},{6,2},{7,3},{8,12},{9,13},{10,... | collective-permute-start | bytes 18440 | tf_op jit(solution)/shard_map/ppermute | solution.py:34
  34.8 13.7 %copy-start.1 = (f32[1,3,4,16,128]{4,3,2,1,0:T(8,128)S(1)}, f32[1,3,4,16,128]{4,3,2,1,0:T(8,128)}, u32[]{:S(2)}) copy-start(f32[1,3,4,16,128]{4,3,2,1,0:T(8,128)} %param.19) | copy-start | bytes 294916
  39.5 1.2 %collective-permute-start.21 = (f32[16,128]{1,0:T(8,128)S(1)}, f32[16,128]{1,0:T(8,128)S(1)}, u32[]{:S(2)}, u32[]{:S(2)}) collective-permute-start(f32[16,128]{1,0:T(8,128)S(1)} %get-tuple-element.36.refs_4_), channel_id=1, source_target_pairs={{0,4},{1,5},{2,6},{3,7},{4,0},{5,1},{6,2},{7,3},{8,12},{9,13},{10,... | collective-permute-start | bytes 24584 | tf_op jit(solution)/shard_map/ppermute | solution.py:34
  40.7 5.4 %collective-permute-start.24 = (f32[16,128]{1,0:T(8,128)S(1)}, f32[16,128]{1,0:T(8,128)S(1)}, u32[]{:S(2)}, u32[]{:S(2)}) collective-permute-start(f32[16,128]{1,0:T(8,128)S(1)} %add.3.refs_0_), channel_id=1, source_target_pairs={{0,3},{1,2},{2,1},{3,0},{4,7},{5,6},{6,5},{7,4},{8,11},{9,10},{10,... | collective-permute-start | bytes 24584 | tf_op jit(solution)/shard_map/ppermute | solution.py:34
  43.9 4.5 %collective-permute-start.23 = (f32[16,128]{1,0:T(8,128)S(1)}, f32[16,128]{1,0:T(8,128)S(1)}, u32[]{:S(2)}, u32[]{:S(2)}) collective-permute-start(f32[16,128]{1,0:T(8,128)S(1)} %add.3.refs_0_), channel_id=1, source_target_pairs={{0,2},{1,3},{2,0},{3,1},{4,6},{5,7},{6,4},{7,5},{8,10},{9,11},{10,... | collective-permute-start | bytes 24584 | tf_op jit(solution)/shard_map/ppermute | solution.py:34
  44.3 4.2 %collective-permute-start.22 = (f32[16,128]{1,0:T(8,128)S(1)}, f32[16,128]{1,0:T(8,128)S(1)}, u32[]{:S(2)}, u32[]{:S(2)}) collective-permute-start(f32[16,128]{1,0:T(8,128)S(1)} %add.3.refs_0_), channel_id=1, source_target_pairs={{0,1},{1,0},{2,3},{3,2},{4,5},{5,4},{6,7},{7,6},{8,9},{9,8},{10,11... | collective-permute-start | bytes 24584 | tf_op jit(solution)/shard_map/ppermute | solution.py:34

commit v5 on v4

v5 whole, which is shorter than its diff:
```python
import functools
import jax
import jax.numpy as jnp
from jax import lax
from jax.experimental import pallas as pl
from jax.experimental.pallas import tpu as pltpu
from jax.sharding import PartitionSpec as P

NBLK = 64

biot_coef = 1.5
relaxation = 0.8
spring_coef = 0.5
well_index = 4.0

H = 3
TOP = 8
GRANT = 16 * 1024 * 1024
f32 = jnp.float32
bf16 = jnp.bfloat16


ALL = ("grp", "gx", "gy")


def permuted(value, target):
    sizes = [lax.axis_size(a) for a in ALL]
    flat = lambda g, x, y: (g * sizes[1] + x) * sizes[2] + y
    pairs = []
    for g in range(sizes[0]):
        for x in range(sizes[1]):
            for y in range(sizes[2]):
                pairs.append((flat(g, x, y), flat(*target(g, x, y))))
    return lax.ppermute(value, ALL, pairs)


def idle(g, x, y):
    return g, x ^ 1, y


def x_swap(value):
    return permuted(value, idle)


def exchange_x(value):
    n = lax.axis_size("gx")
    got = x_swap(value)
    if n == 2:
        return got, got
    return got, permuted(value, lambda g, x, y: (g, ((x + 1) if x % 2 else (x - 1)) % n, y))


def up_or_down(i, n, kind):
    j = i + 1 if i % 2 == kind else i - 1
    return j if 0 <= j < n else None


def pair_y(kind):
    n = lax.axis_size("gy")

    def target(g, x, y):
        j = up_or_down(y, n, kind)
        return idle(g, x, y) if j is None else (g, x, j)

    return target


def pair_first(kind):
    last = lax.axis_size("grp") - 1
    along_y = pair_y(kind)

    def target(g, x, y):
        if g == last:
            return along_y(g, x, y)
        j = up_or_down(g, last, kind)
        return idle(g, x, y) if j is None else (j, x, y)

    return target


def star(value):
    n = lax.axis_size("grp")

    def meet(k):
        def target(g, x, y):
            return (g ^ k, x, y) if n - 1 in (g, g ^ k) else idle(g, x, y)

        return target

    return [permuted(value, meet(k)) for k in range(1, n)]


def call(body, name, outs, *args, scratch=(), space=pltpu.VMEM):
    vmem = pl.BlockSpec(memory_space=pltpu.VMEM)
    source = pl.BlockSpec(memory_space=space)
    unique, spots = [], []
    for arg in args:
        found = [i for i, other in enumerate(unique) if other is arg]
        if not found:
            unique.append(arg)
        spots.append(found[0] if found else len(unique) - 1)

    def expanded(*refs):
        return body(*[refs[i] for i in spots], *refs[len(unique) :])

    if space is pltpu.HBM:
        unique = [pltpu.with_memory_space_constraint(v, space) for v in unique]
    return pl.pallas_call(
        expanded,
        name=name,
        out_shape=[o if hasattr(o, "dtype") else jax.ShapeDtypeStruct(o, f32) for o in outs],
        in_specs=[source] * len(unique),
        out_specs=[vmem] * len(outs),
        scratch_shapes=list(scratch),
        compiler_params=pltpu.CompilerParams(vmem_limit_bytes=GRANT),
    )(*unique)


class Place:
    def __init__(self):
        self.groups = lax.axis_size("grp")
        self.g = lax.axis_index("grp")
        self.mech = self.g == self.groups - 1
        for name in ("x", "y"):
            n, i = lax.axis_size("g" + name), lax.axis_index("g" + name)
            setattr(self, name + "odd", lax.rem(i, 2) == 1)
            setattr(self, name + "prev", i > 0)
            setattr(self, name + "next", i < n - 1)


def lane(shape):
    return lax.broadcasted_iota(jnp.int32, shape, len(shape) - 1)


def sub(shape):
    return lax.broadcasted_iota(jnp.int32, shape, len(shape) - 2)


def roll(value, shift, axis):
    return pltpu.roll(value, shift % value.shape[axis], axis)


def z_up(value):
    n = value.shape[-1]
    return jnp.where(lane(value.shape) < n - 1, roll(value, -1, value.ndim - 1), 0.0)


def z_down(value):
    return jnp.where(lane(value.shape) > 0, roll(value, 1, value.ndim - 1), 0.0)


def y_up(value):
    return roll(value, -1, value.ndim - 2)


def y_down(value):
    return roll(value, 1, value.ndim - 2)


def send_rows(at, out_a, out_b, first, low, high):
    rows = slice(first, first + low.shape[0])
    out_a[rows, :] = jnp.where(at.yodd, low, high)
    out_b[rows, :] = jnp.where(at.yodd, high, low)


class Near:
    def __init__(self, at, xa, xb, ya, yb, xyaa, xyab, xyba, xybb):
        self.at, self.tiles = at, (xa, xb)
        self.rows_of = {0: (ya, yb), "a": (xyaa, xyab), "b": (xyba, xybb)}
        self.one = lax.axis_size("gx") == 2

    def x_side(self, dx):
        at = self.at
        return (at.xodd, at.xprev) if dx < 0 else (~at.xodd, at.xnext)

    def plane(self, dx, f, x):
        of_a, valid = self.x_side(dx)
        value = self.tiles[0][f, x]
        if not self.one:
            value = jnp.where(of_a, value, self.tiles[1][f, x])
        return jnp.where(valid, value, 0.0)

    def rows(self, dx, dy, first, count):
        at = self.at
        y_of_a, valid = (at.yodd, at.yprev) if dy < 0 else (~at.yodd, at.ynext)

        def of(kind):
            a, b = self.rows_of[kind]
            rows = slice(first, first + count)
            return jnp.where(y_of_a, a[rows, :], b[rows, :])

        if dx == 0:
            return jnp.where(valid, of(0), 0.0)
        x_of_a, x_valid = self.x_side(dx)
        value = of("a")
        if not self.one:
            value = jnp.where(x_of_a, value, of("b"))
        return jnp.where(valid & x_valid, value, 0.0)


def source_plane(x, size_x):
    if x < 0:
        return -1, x + size_x
    return (1, x - size_x) if x >= size_x else (0, x)


def extend(near, ext, tile, fields, size_x, size_y, wide, high):
    rows = ext.shape[2]
    end = TOP + size_y
    for f in range(fields):
        for x in range(-wide, size_x + wide):
            dx, xs = source_plane(x, size_x)
            xe = x + wide
            first = (f * size_x + xs) * high
            ext[f, xe, 0:TOP, :] = jnp.zeros((TOP, 128), f32)
            ext[f, xe, end:rows, :] = jnp.zeros((rows - end, 128), f32)
            ext[f, xe, TOP:end, :] = tile[f, xs] if dx == 0 else near.plane(dx, f, xs)
            ext[f, xe, TOP - high : TOP, :] = near.rows(dx, -1, first, high)
            ext[f, xe, end : end + high, :] = near.rows(dx, 1, first, high)


def merged(value):
    first, last = value[0:8], value[value.shape[0] - 8 :]
    return jnp.where(sub((8, 128)) == 7, first, last)


def middle(value):
    return [value[t : t + 8] for t in range(TOP, value.shape[0] - 8, 8)]


def variants(here):
    up = z_up(here)
    return {(0, 0): here, (0, 1): up, (1, 0): y_up(here), (1, 1): y_up(up)}


class Corners:
    def __init__(self, nodes):
        self.nodes, self.seen = nodes, {}

    def __call__(self, x):
        for k in (x, x + 1):
            if k not in self.seen:
                self.seen[k] = [variants(self.nodes[m, k]) for m in range(3)]
        return [
            self.seen[x + a][m][b, e]
            for a in range(2) for b in range(2) for e in range(2) for m in range(3)
        ]


def stack_tiles(values, with_ends):
    tiles = [([merged(v)] if with_ends else []) + middle(v) for v in values]
    cols = [jnp.concatenate([t[i] for t in tiles], axis=0) for i in range(len(tiles[0]))]
    return jnp.concatenate(cols, axis=1)


def split(value):
    high = value.astype(bf16)
    return high, (value - high.astype(f32)).astype(bf16)


def stiff(k_both, stacked):
    high, low = split(stacked)
    dot = functools.partial(jnp.dot, preferred_element_type=f32)
    n = stacked.shape[0]
    wide = dot(k_both[...], high)
    return (wide[0:n] + wide[n:]) + dot(k_both[0:n, :], low)


def spread_stiffness(stiffness, k_both):
    n = 8 * stiffness.shape[0]
    pick = jnp.where(sub((n, n // 8)) // 8 == lane((n, n // 8)), 1.0, 0.0).astype(bf16)
    keep = (sub((n, n)) & 7) == (lane((n, n)) & 7)
    for i, term in enumerate(split(stiffness[...])):
        tall = jnp.dot(pick, term, preferred_element_type=f32).astype(bf16)
        wide = lax.dot_general(tall, pick, (((1,), (1,)), ((), ())), preferred_element_type=f32)
        k_both[i * n : i * n + n, :] = jnp.where(keep, wide, 0.0).astype(bf16)


def dots(u, v):
    part = u * v
    total = part[0:8]
    for j in range(1, 24):
        total = total + part[8 * j : 8 * j + 8]
    return total


def apply(nodes, weight, k_both, planes, own=()):
    corners = Corners(nodes)
    out = {}
    energy = jnp.zeros((8, 128), f32)
    planes = list(planes)
    for i in range(0, len(planes), 2):
        group = planes[i : i + 2]
        stacks = [stack_tiles(corners(x), True) for x in group]
        width = stacks[0].shape[1]
        v_all = stiff(k_both, jnp.concatenate(stacks, axis=1))
        for k, x in enumerate(group):
            v = v_all[:, k * width : (k + 1) * width]
            w_plane = weight[x]
            w = [merged(w_plane)] + middle(w_plane)

            def entry(j):
                return [w[t] * v[8 * j : 8 * j + 8, 128 * t : 128 * t + 128] for t in range(len(w))]

            def joined(c, m):
                tiles = [p + z_down(q) for p, q in zip(entry(3 * c + m), entry(3 * (c + 1) + m))]
                return jnp.concatenate(tiles + tiles[:1], axis=0)

            for a in range(2):
                for m in range(3):
                    total = joined(4 * a, m) + y_down(joined(4 * a + 2, m))
                    key = (m, x + a)
                    out[key] = out[key] + total if key in out else total
            if x in own:
                for t in range(1, len(w)):
                    cols = slice(128 * t, 128 * t + 128)
                    energy = energy + w[t] * dots(stacks[k][:, cols], v[:, cols])
    return out, energy


def total_of(value):
    return jnp.sum(jnp.sum(value, axis=0, keepdims=True), axis=1, keepdims=True)


def onehot_sum(size_x, size_y, row_fn):
    acc = None
    for x in range(size_x):
        rows = [row_fn(x, y) for y in range(size_y)]
        part = lax.dot_general(
            jnp.concatenate([r[0] for r in rows], axis=1),
            jnp.concatenate([r[1] for r in rows], axis=1),
            (((1,), (1,)), ((), ())),
            preferred_element_type=f32,
        )
        acc = part if acc is None else acc + part
    return acc


def spread_row(row, count):
    return jnp.broadcast_to(row, (16, 128)).astype(bf16) if count == 16 else jnp.concatenate(
        [spread_row(row, 16)] * (count // 16), axis=0
    )


def hits(row, count):
    ids = sub((count, 128)).astype(f32).astype(bf16)
    return ids == spread_row(row.astype(f32), count)


def host_row(host, x, y, size, values):
    h = host[x, y : y + 1, :]
    hit = hits(h >> 7, size)
    zero = jnp.zeros((size, 128), bf16)
    left = [jnp.where(hit, v, zero) for v in values]
    right = jnp.where(hits(h & 127, 128), jnp.ones((128, 128), bf16), jnp.zeros((128, 128), bf16))
    return jnp.concatenate(left, axis=0), right


def z_slot(field, x, size_x):
    return 8 * (field * size_x + x)


def pack_body(p, src, sto, well, host, u, mod, mask, tile, ya, yb, *scratch):
    at = Place()
    size_x, size_y = p.shape[0], p.shape[1]
    refs, sems = scratch[:-1], scratch[-1]

    def fetch(first, sources):
        copies = [
            pltpu.make_async_copy(s, refs[first + i], sems.at[first + i])
            for i, s in enumerate(sources)
        ]
        for c in copies:
            c.start()
        for c in copies:
            c.wait()
        return refs[first : first + len(copies)]

    @pl.when(at.mech)
    def _():
        u_in, mod_in, mask_in = fetch(0, (u, mod, mask))
        tile[0:3] = u_in[...]
        tile[3] = mod_in[...] * mask_in[...].astype(f32)
        for f in range(4):
            for x in range(size_x):
                low, high = tile[f, x, 0:1, :], tile[f, x, size_y - 1 : size_y, :]
                send_rows(at, ya, yb, f * size_x + x, low, high)

    @pl.when(~at.mech)
    def _():
        p_in, src_in, sto_in, well_in, host_in = fetch(3, (p, src, sto, well, host))
        where = lane((size_y, 128))
        msg = jnp.zeros((size_y, 128), f32)
        for x in range(size_x):
            diag = 6.0 + sto_in[x] + well_index * well_in[x].astype(f32)
            fields = (p_in[x], relaxation / diag, src_in[x], host_in[x].astype(f32))
            for f, v in enumerate(fields):
                s = z_slot(f, x, size_x)
                msg = jnp.where((where >= s) & (where < s + 6), roll(v, s + 3, 1), msg)
        ya[0:size_y] = msg
        yb[0:size_y] = msg


def count_body(host, out):
    at = Place()
    size_x, size_y = host.shape[0], host.shape[1]
    rows = size_x * size_y

    @pl.when(~at.mech)
    def _():
        one = [jnp.ones((rows, 128), bf16)]
        out[...] = onehot_sum(size_x, size_y, lambda x, y: host_row(host, x, y, rows, one))


def strain_body(tile, *refs):
    at = Place()
    near, (mask, counts, out, ue) = Near(at, *refs[:8]), refs[8:]
    size_x, size_y = mask.shape[0], mask.shape[1]

    @pl.when(at.mech)
    def _():
        for m in range(3):
            for x in range(size_x + 1):
                dx, xs = source_plane(x, size_x)
                ue[m, x, 0:size_y, :] = tile[m, xs] if dx == 0 else near.plane(dx, m, xs)
                ue[m, x, size_y : size_y + 8, :] = jnp.zeros((8, 128), f32)
                ue[m, x, size_y : size_y + 1, :] = near.rows(dx, 1, m * size_x + xs, 1)
        before = None
        for x in range(size_x + 1):
            v = ue[0, x]
            s = v + z_up(v)
            q0 = s + y_up(s)
            v = ue[1, x]
            s = v + z_up(v)
            q1 = y_up(s) - s
            v = ue[2, x]
            s = z_up(v) - v
            q2 = s + y_up(s)
            if x:
                value = (q0 - before[0]) + (q1 + before[1]) + (q2 + before[2])
                r = (x - 1) * size_y
                out[r : r + size_y, :] = 0.25 * mask[x - 1].astype(f32) * value[0:size_y]
            before = (q0, q1, q2)

    @pl.when(~at.mech)
    def _():
        out[...] = counts[...]


def z_fold(values, size_x):
    spot = lane(values[0].shape)
    out = jnp.zeros(values[0].shape, f32)
    for i, v in enumerate(values):
        out = jnp.where((spot >= 8 * i) & (spot < 8 * i + 6), roll(v, 8 * i + 3, 1), out)
    return out


def z_unfold(value, i, depth):
    spot = lane(value.shape)
    return jnp.where((spot < depth) | (spot >= 128 - depth), roll(value, -(8 * i + 3), 1), 0.0)


def gather_body(*refs):
    at = Place()
    k = at.groups - 1
    got, refs = refs[:k], refs[k:]
    p, src, sto, well, host, body, stiffness, tile = refs[:8]
    near, ya, yb = Near(at, *refs[8:16]), refs[10], refs[11]
    out, out_a, out_b, k_both, shift, ext, table, cells = refs[16:]
    size_x, size_y = p.shape[0], p.shape[1]
    rows = size_x * size_y

    @pl.when(~at.mech)
    def _():
        value = got[0][...]
        for i in range(1, k):
            value = jnp.where((at.g ^ k) == i + 1, got[i][...], value)
        table[...] = value
        godd = lax.rem(at.g, 2) == 1
        msg_a, msg_b = ya[0:size_y], yb[0:size_y]
        before = jnp.where(at.g > 0, jnp.where(godd, msg_a, msg_b), 0.0)
        after = jnp.where(at.g < at.groups - 2, jnp.where(godd, msg_b, msg_a), 0.0)
        spot = lane((size_y, 128))
        zside = jnp.where((spot & 7) < 3, before, after)
        first_host = 8 * (3 * size_x)
        for x in range(size_x):
            cells[x * size_y : (x + 1) * size_y] = host[x]
        cells[rows : rows + size_y] = jnp.where(spot >= first_host, zside, 0.0).astype(jnp.int32)

        def step(i, carry):
            here = pl.ds(pl.multiple_of(8 * i, 8), 8)
            index = cells[here, :]
            high, low = index >> 7, index & 127
            parts = [jnp.zeros((8, 128), f32) for _ in range(4)]
            for h in range(rows):
                line = jnp.broadcast_to(table[h : h + 1, :], (8, 128))
                found = jnp.take_along_axis(line, low, axis=1, mode="promise_in_bounds")
                parts[h % 4] = jnp.where(high == h, found, parts[h % 4])
            ext[0, 0, here, :] = (parts[0] + parts[1]) + (parts[2] + parts[3])
            return carry

        lax.fori_loop(0, (rows + size_y) // 8, step, 0)
        zstrain = ext[0, 0, rows : rows + size_y, :]
        for x in range(size_x):
            diag = 6.0 + sto[x] + well_index * well[x].astype(f32)
            strain = ext[0, 0, x * size_y : (x + 1) * size_y, :]
            out[0, x] = p[x]
            out[1, x] = relaxation / diag
            out[2, x] = src[x] - biot_coef * strain
            out[3, x] = z_unfold(zside, x, 3)
            out[4, x] = z_unfold(zside, size_x + x, 2)
            zforce = z_unfold(zside, 2 * size_x + x, 2)
            out[5, x] = zforce - biot_coef * z_unfold(zstrain, 3 * size_x + x, 2)
        low, high = slice(0, H), slice(size_y - H, size_y)
        for f in range(3):
            for x in range(size_x):
                send_rows(at, out_a, out_b, (f * size_x + x) * H, out[f, x, low, :], out[f, x, high, :])
        fold = [
            z_fold([out[3 + f, x, side, :] for f in range(3) for x in range(size_x)], size_x)
            for side in (low, high)
        ]
        send_rows(at, out_a, out_b, 3 * size_x * H, *fold)

    @pl.when(at.mech)
    def _():
        spread_stiffness(stiffness, k_both)
        nodes = ext.at[:, 0 : size_x + 2, 0 : size_y + 2 * TOP]
        extend(near, nodes, tile, 4, size_x, size_y, 1, 1)
        image, _ = apply(nodes, nodes.at[3], k_both, range(size_x + 1))
        own = slice(TOP, TOP + size_y)
        weight = jnp.zeros((8, 128), f32)
        for x in range(size_x):
            for m in range(3):
                u = tile[m, x]
                out[m, x] = body[m, x] - image[m, x + 1][own] - spring_coef * u
            out[3, x] = tile[3, x]
            for t in range(0, size_y, 8):
                weight = weight + tile[3, x, t : t + 8, :]
        n = stiffness.shape[0]
        trace = total_of(jnp.where(sub((n, n)) == lane((n, n)), stiffness[...], 0.0))
        mean = total_of(weight) * trace / (3.0 * rows * 128.0)
        shift[...] = jnp.broadcast_to(mean + spring_coef, (8, 128))
        for f in range(4):
            for x in range(size_x):
                low, high = out[f, x, 0:2, :], out[f, x, size_y - 2 : size_y, :]
                send_rows(at, out_a, out_b, (f * size_x + x) * 2, low, high)


def flow_body(tile, *refs):
    at = Place()
    near, refs = Near(at, *refs[:8]), refs[8:]
    sto, well, block, basis, host, pressure, sums, mech, ext, work, corr = refs
    size_x, size_y = sto.shape[0], sto.shape[1]
    rows = size_x * size_y
    nx = size_x + 2 * H

    @pl.when(at.mech)
    def _():
        extend(near, mech, tile, 4, size_x, size_y, 2, 2)

    @pl.when(~at.mech)
    def _():
        main = ext.at[:, :, :, 0:128]
        extend(near, main, tile, 3, size_x, size_y, H, H)
        first = 3 * size_x * H
        end = TOP + size_y
        for x in range(-H, size_x + H):
            dx, xs = source_plane(x, size_x)
            below, above = near.rows(dx, -1, first, H), near.rows(dx, 1, first, H)
            for f in range(3):
                i = f * size_x + xs
                xe = x + H
                ext[f, xe, 0:TOP, 128:256] = jnp.zeros((TOP, 128), f32)
                ext[f, xe, end : end + TOP, 128:256] = jnp.zeros((TOP, 128), f32)
                own = tile[3 + f, xs] if dx == 0 else near.plane(dx, 3 + f, xs)
                ext[f, xe, TOP:end, 128:256] = own
                ext[f, xe, TOP - H : TOP, 128:256] = z_unfold(below, i, H)
                ext[f, xe, end : end + H, 128:256] = z_unfold(above, i, H)

        def around(field, x):
            v = field[x]
            total = field[x + 1] + field[x - 1]
            total = total + y_up(v) + y_down(v)
            return total + roll(v, 1, 1) + roll(v, -1, 1)

        p0 = [ext[0, x] for x in range(nx)]
        p1 = [None] * nx
        for x in range(1, nx - 1):
            p1[x] = (1.0 - relaxation) * p0[x] + ext[1, x] * (ext[2, x] + around(p0, x))
        p2 = [None] * nx
        for x in range(2, nx - 2):
            p2[x] = (1.0 - relaxation) * p1[x] + ext[1, x] * (ext[2, x] + around(p1, x))
        own = slice(TOP, TOP + size_y)
        for x in range(size_x):
            r = slice(x * size_y, (x + 1) * size_y)
            diag = 6.0 + sto[x] + well_index * well[x].astype(f32)
            here = p2[x + H]
            res = (ext[2, x + H] + around(p2, x + H))[own, 0:128] - diag * here[own, 0:128]
            work[0, r, :] = here[own, 0:128]
            work[1, r, :] = res
            work[2, r, :] = diag
        one, zero = jnp.ones((NBLK, 128), bf16), jnp.zeros((NBLK, 128), bf16)

        def coarse_row(x, y):
            r = x * size_y + y
            w = basis[pl.ds(r, 8, stride=rows), :]
            res, diag = work[1, r : r + 1, :], work[2, r : r + 1, :]
            high, low = split(jnp.concatenate([w * res, w * w * diag], axis=0))
            right = jnp.where(hits(block[x, y : y + 1, :], NBLK), one, zero)
            return jnp.concatenate([high, low], axis=0), right

        acc = onehot_sum(size_x, size_y, coarse_row)
        corr[...] = jnp.zeros_like(corr)
        corr[:, 0:NBLK] = (acc[0:8] + acc[16:24]) / (1.0 + (acc[8:16] + acc[24:32]))
        lines = [jnp.broadcast_to(corr[j : j + 1, :], (8, 128)) for j in range(8)]
        for x in range(size_x):
            for t in range(size_y // 8):
                ids = block[x, 8 * t : 8 * t + 8, :]
                r = x * size_y + 8 * t
                delta = jnp.zeros((8, 128), f32)
                for j in range(8):
                    got = jnp.take_along_axis(lines[j], ids, axis=1, mode="promise_in_bounds")
                    delta = delta + basis[j * rows + r : j * rows + r + 8, :] * got
                updated = work[0, r : r + 8, :] + delta
                pressure[x, 8 * t : 8 * t + 8, :] = updated
                change = updated - tile[0, x, 8 * t : 8 * t + 8, :]
                high = change.astype(bf16).astype(f32)
                work[0, r : r + 8, :] = high
                work[1, r : r + 8, :] = change - high

        def sum_row(x, y):
            r = x * size_y + y
            values = [spread_row(work[i, r : r + 1, :], rows) for i in range(2)]
            return host_row(host, x, y, rows, values)

        acc = onehot_sum(size_x, size_y, sum_row)
        sums[...] = acc[0:rows] + acc[rows : 2 * rows]


def element_body(*refs):
    at = Place()
    k = at.groups - 1
    sums, counts, refs = refs[:k], refs[k : 2 * k], refs[2 * k :]
    mask, out, out_a, out_b = refs
    size_x, size_y = mask.shape[0], mask.shape[1]

    @pl.when(at.mech)
    def _():
        for x in range(size_x):
            r = slice(x * size_y, (x + 1) * size_y)
            total = sums[0][r, :]
            count = counts[0][r, :]
            for i in range(1, k):
                total = total + sums[i][r, :]
                count = count + counts[i][r, :]
            out[0, x] = mask[x].astype(f32) * (total / jnp.maximum(count, 1.0))
        for x in range(size_x):
            send_rows(at, out_a, out_b, 2 * x, out[0, x, 0:2, :], out[0, x, size_y - 2 : size_y, :])


def krylov_body(tile, *refs):
    at = Place()
    near, (mech, k_both, shift, r_out, q_out, scal, ext, res, acc) = Near(at, *refs[:8]), refs[8:]
    size_x, size_y = tile.shape[1], tile.shape[2]
    rows = ext.shape[2]
    own = slice(TOP, TOP + size_y)

    @pl.when(at.mech)
    def _():
        extend(near, ext, tile, 1, size_x, size_y, 2, 2)
        line = sub((rows, 128))
        inside = ((line >= TOP) | at.yprev) & ((line < TOP + size_y) | at.ynext)

        def inside_x(x):
            if x < 2:
                return inside & at.xprev
            return inside & at.xnext if x >= 2 + size_x else inside

        before = None
        for x in range(size_x + 4):
            e = ext[0, x]
            sz = e + z_down(e)
            szd = y_down(sz)
            dz = z_down(e) - e
            now = (szd + sz, szd - sz, dz + y_down(dz))
            if before is not None:
                f = (before[0] - now[0], before[1] + now[1], before[2] + now[2])
                for m in range(3):
                    value = mech[m, x] + (0.25 * biot_coef) * f[m]
                    res[m, x] = jnp.where(inside_x(x), value, 0.0)
            before = now

        weight = mech.at[3]
        planes = range(2, 2 + size_x)
        image, e22 = apply(res, weight, k_both, range(1, size_x + 3), planes)
        gap = spring_coef - shift[0:1, :]
        rr = jnp.zeros((8, 128), f32)
        rq, qq = rr, rr
        for m in range(3):
            for x in range(2, size_x + 3):
                r = res[m, x]
                q = jnp.where(inside_x(x), image[m, x] + gap * r, 0.0)
                acc[m, x] = q
                if x in planes:
                    q_out[m, x - 2] = q[own]
                    r_out[m, x - 2] = r[own]
                    for t in range(TOP, TOP + size_y, 8):
                        rt, qt = r[t : t + 8], q[t : t + 8]
                        rr = rr + rt * rt
                        rq = rq + rt * qt
                        qq = qq + qt * qt
        of_q, of_r = Corners(acc), Corners(res)
        e11 = jnp.zeros((8, 128), f32)
        e12 = e11
        for x in planes:
            uq = stack_tiles(of_q(x), False)
            ur = stack_tiles(of_r(x), False)
            vq = stiff(k_both, uq)
            for t, w in enumerate(middle(weight[x])):
                cols = slice(128 * t, 128 * t + 128)
                e11 = e11 + w * dots(uq[:, cols], vq[:, cols])
                e12 = e12 + w * dots(ur[:, cols], vq[:, cols])
        e11 = e11 + spring_coef * qq
        e12 = e12 + spring_coef * rq
        e22 = e22 + spring_coef * rr
        line = sub((8, 128))
        value = jnp.where(line == 1, shift[...], 0.0)
        for i, v in ((0, rr), (2, rq), (3, qq), (4, e11), (5, e12), (6, e22)):
            value = jnp.where(line == i, total_of(v), value)
        if scal.shape[0] == 8:
            scal[...] = value
        else:
            scal[0:8] = jnp.where(at.xodd, 0.0, value)
            scal[8:16] = jnp.where(at.xodd, value, 0.0)


def final_body(*refs):
    at = Place()
    scals, own, r, q, u, updated, pressure, out = refs[:-7], *refs[-7:]

    @pl.when(~at.mech)
    def _():
        out[...] = jnp.zeros_like(out)
        pressure[...] = updated[...]

    @pl.when(at.mech)
    def _():
        pressure[...] = jnp.zeros_like(pressure)
        parts = [s[8 * i : 8 * i + 8] for s in scals for i in range(s.shape[0] // 8)]
        get = lambda part, i: part[i : i + 1]
        total = lambda fn: functools.reduce(lambda a, b: a + b, [fn(p) for p in parts])
        rr = total(lambda p: get(p, 0))
        mean = total(lambda p: get(p, 2) + get(p, 1) * get(p, 0)) / rr

        def shifted(low, mid, high):
            def one(p):
                gap = get(p, 1) - mean
                return get(p, high) + gap * (2.0 * get(p, mid) + gap * get(p, low))

            return total(one)

        qq = shifted(0, 2, 3)
        energy = shifted(6, 5, 4)
        ratio = qq / (mean * mean * rr)
        curve = energy / (mean * mean) - ratio * ratio * mean * rr
        second = ratio * rr / curve
        shift = own[1:2]
        if own.shape[0] == 16:
            shift = jnp.where(at.xodd, own[9:10], shift)
        by_r = 1.0 / mean + second * (ratio - (shift - mean) / mean)
        by_q = -second / mean
        out[...] = u[...] + by_r[None, None] * r[...] + by_q[None, None] * q[...]


def neighbours(tile, msg_a, msg_b, pair=pair_y):
    xa, xb = exchange_x(tile)
    yb = permuted(msg_b, pair(1))
    ya = permuted(msg_a, pair(0))
    xyab, xybb = exchange_x(yb)
    xyaa, xyba = exchange_x(ya)
    return (xa, xb, ya, yb, xyaa, xyab, xyba, xybb)


def local(
    pressure,
    source,
    storage,
    well_mask,
    block_id,
    basis_weight,
    host_elem,
    displacement,
    body_force,
    modulus,
    elem_mask,
    stiffness,
):
    p, src, sto, well = pressure[0], source[0], storage[0], well_mask[0]
    host, block, mask = host_elem[0], block_id[0], elem_mask[0]
    size_x, size_y, size_z = p.shape
    rows = size_x * size_y
    basis = basis_weight[0].reshape(8 * rows, size_z)
    u, body = displacement[0], body_force[0]
    nx, ny = size_x + 2 * H, size_y + 2 * TOP
    cell = (size_x, size_y, size_z)

    msg = (max(4 * size_x, size_y), size_z)
    inputs = (displacement[0], modulus[0], mask, p, src, sto, well, host)
    tile, ya, yb = call(
        pack_body,
        "pack",
        [(4, *cell), msg, msg],
        p, src, sto, well, host, u, modulus[0], mask,
        scratch=[pltpu.VMEM(v.shape, v.dtype) for v in inputs]
        + [pltpu.SemaphoreType.DMA((len(inputs),))],
        space=pltpu.HBM,
    )
    near = neighbours(tile, ya, yb, pair_first)
    (counts,) = call(count_body, "count", [(rows, size_z)], host)
    (line,) = call(
        strain_body,
        "strain",
        [(rows, size_z)],
        tile, *near, mask, counts,
        scratch=[pltpu.VMEM((3, size_x + 1, size_y + 8, size_z), f32)],
    )
    got = star(line)
    msg = (3 * size_x * H + 4, size_z)
    n = 8 * stiffness.shape[0]
    k_shape = jax.ShapeDtypeStruct((2 * n, n), bf16)
    cells, ya, yb, k_both, shift = call(
        gather_body,
        "gather",
        [(6, *cell), msg, msg, k_shape, (8, size_z)],
        *got, p, src, sto, well, host, body, stiffness, tile, *near,
        scratch=[
            pltpu.VMEM((4, size_x + 2, max(ny, rows + size_y), size_z), f32),
            pltpu.VMEM((rows, size_z), f32),
            pltpu.VMEM((rows + size_y, size_z), jnp.int32),
        ],
    )
    near = neighbours(cells, ya, yb)
    updated, sums, mech = call(
        flow_body,
        "flow",
        [cell, (rows, size_z), (4, size_x + 4, ny, size_z)],
        cells, *near, sto, well, block, basis, host,
        scratch=[
            pltpu.VMEM((3, nx, ny, 2 * size_z), f32),
            pltpu.VMEM((3, rows, size_z), f32),
            pltpu.VMEM((8, size_z), f32),
        ],
    )
    summed = star(sums)
    msg = (2 * size_x, size_z)
    elem, ya, yb = call(
        element_body,
        "element",
        [(1, *cell), msg, msg],
        *summed, *got, mask,
    )
    near = neighbours(elem, ya, yb)
    own = (3, *cell)
    duo = lax.axis_size("gx") == 2
    r, q, scal = call(
        krylov_body,
        "krylov",
        [own, own, (16 if duo else 8, size_z)],
        elem, *near, mech, k_both, shift,
        scratch=[
            pltpu.VMEM((1, size_x + 4, ny, size_z), f32),
            pltpu.VMEM((3, size_x + 4, ny, size_z), f32),
            pltpu.VMEM((3, size_x + 4, ny, size_z), f32),
        ],
    )
    if duo:
        pair = scal + x_swap(scal)
        scals = [pair] + [
            permuted(pair, lambda g, x, y: (g, x, y ^ k)) for k in range(1, lax.axis_size("gy"))
        ]
    else:
        scals = [lax.all_gather(scal, ("gx", "gy"), tiled=True)]
    pressure_out, moved = call(
        final_body, "final", [p.shape, own], *scals, scal, r, q, u, updated
    )
    return (pressure_out[None], moved[None])


def solution(mesh):
    cell = P("grp", "gx", "gy", None)
    deep = P("grp", None, "gx", "gy", None)
    placed = (cell, cell, cell, cell, cell, deep, cell, deep, deep, cell, cell, P())
    return jax.shard_map(
        local,
        mesh=mesh,
        in_specs=placed,
        out_specs=(cell, deep),
        check_vma=False,
    )
```

time: 49.4 us -> 43 us (0.87)
  Pallas kernels: 11 us -> 4.77 us
  waiting for transfers between devices: 19.6 us -> 18.2 us
  starting transfers between devices: 17.9 us -> 18.9 us
    pallas_call x8, Pallas kernels: 11 us -> 4.77 us  [call(): pl.pallas_call(expanded, name=name, out_shape=[o if hasattr(o, 'dtype') e...]
    ppermute x25, waiting for transfers between devices: 19.6 us -> 18.2 us  [permuted(): return lax.ppermute(value, ALL, pairs)]
    ppermute x25, starting transfers between devices: 17.9 us -> 18.9 us  [permuted(): return lax.ppermute(value, ALL, pairs)]
  transfers between devices with their start and end apart: 25 -> 25, of which waited for: 18 -> 17; matrix products, arithmetic and copies ran while one was open for 0% -> 0% of each run, Pallas kernels for 0% -> 0%
where the time goes in v5:
time: 43 us; the launch traced here: 42.8 us
  starting transfers between devices  18.9 us (44%)
  waiting for transfers between devices  18.2 us (42%)
  Pallas kernels  4.77 us (11%)
  between operations  0.8 us (2%)
    ppermute x25, starting transfers between devices, permuted(): return lax.ppermute(value, ALL, pairs)  18.9 us
    ppermute x25, waiting for transfers between devices, permuted(): return lax.ppermute(value, ALL, pairs)  18.2 us
    pallas_call x8, Pallas kernels, call(): pl.pallas_call(expanded, name=name, out_shape=[o if hasattr(o, 'dtype') e...  4.77 us
  transfers between devices with their start and end apart: 25, of which 17 were waited for; matrix products, arithmetic and copies ran while one was open for 0% of the time, Pallas kernels for 0%

profile of v5, /device:TPU:6, one launch (start us, length us, event | category | flops | bytes accessed | tf_op | source)
XLA Modules:
  0.0 42.8 jit_solution(2263027703241217799)
XLA Ops:
  0.6 1.0 %pack.1 = (f32[4,4,16,128]{3,2,1,0:T(8,128)S(1)}, f32[16,128]{1,0:T(8,128)S(1)}, f32[16,128]{1,0:T(8,128)S(1)}) custom-call(f32[4,16,128]{2,1,0:T(8,128)} %bitcast.29, f32[4,16,128]{2,1,0:T(8,128)} %bitcast.31, f32[4,16,128]{2,1,0:T(8,128)} %bitcast.22, s32[4,16,128]{2,1,0:T(8,128)} %bitcast.25, s32[4,16,128]{2,1,0:T(8,128)} %bitcast.13, ...), custom_call_target="tpu_custom_call" | custom-call | tf_op jit(solution)/shard_map/pack/pallas_call | solution.py:108
  1.7 0.1 collective-permute-start
  1.7 1.6 %collective-permute-start.1 = (f32[16,128]{1,0:T(8,128)S(1)}, f32[16,128]{1,0:T(8,128)S(1)}, u32[]{:S(2)}, u32[]{:S(2)}) collective-permute-start(f32[16,128]{1,0:T(8,128)S(1)} %get-tuple-element.22), channel_id=1, source_target_pairs={{0,8},{1,9},{2,10},{3,11},{4,12},{5,13},{6,14},{7,15},{8,0},{9,1},... | collective-permute-start | bytes 24584 | tf_op jit(solution)/shard_map/ppermute | solution.py:34
  3.4 0.2 collective-permute-start.2
  3.5 1.9 %collective-permute-done.1.refs_2_.refs_12_ = f32[16,128]{1,0:T(8,128)S(1)} collective-permute-done((f32[16,128]{1,0:T(8,128)S(1)}, f32[16,128]{1,0:T(8,128)S(1)}, u32[]{:S(2)}, u32[]{:S(2)}) %collective-permute-start.1) | collective-permute-done | bytes 8224 | tf_op jit(solution)/shard_map/ppermute | solution.py:34
  5.5 0.5 %collective-permute-start.4 = (f32[16,128]{1,0:T(8,128)S(1)}, f32[16,128]{1,0:T(8,128)S(1)}, u32[]{:S(2)}, u32[]{:S(2)}) collective-permute-start(f32[16,128]{1,0:T(8,128)S(1)} %collective-permute-done.2.refs_3_.refs_13_), channel_id=1, source_target_pairs={{0,4},{1,5},{2,6},{3,7},{4,0},{5,1},{6,2},{7,3},{8,12},{9,13},{10,... | collective-permute-start | bytes 24584 | tf_op jit(solution)/shard_map/ppermute | solution.py:34
  6.0 0.0 copy-start.7
  6.0 0.0 copy-start.8
  6.0 0.6 %collective-permute-done.3.refs_4_.refs_14_ = f32[16,128]{1,0:T(8,128)S(1)} collective-permute-done((f32[16,128]{1,0:T(8,128)S(1)}, f32[16,128]{1,0:T(8,128)S(1)}, u32[]{:S(2)}, u32[]{:S(2)}) %collective-permute-start.3) | collective-permute-done | bytes 8224 | tf_op jit(solution)/shard_map/ppermute | solution.py:34
  6.6 0.2 collective-permute-done.4.refs_5_.refs_15_
  6.8 0.1 strain.1
  6.9 0.1 collective-permute-start.7
  7.0 1.5 %collective-permute-start.6 = (f32[64,128]{1,0:T(8,128)S(1)}, f32[64,128]{1,0:T(8,128)S(1)}, u32[]{:S(2)}, u32[]{:S(2)}) collective-permute-start(f32[64,128]{1,0:T(8,128)S(1)} %strain.1), channel_id=1, source_target_pairs={{0,4},{1,5},{2,6},{3,7},{4,0},{5,1},{6,2},{7,3},{8,24},{9,25},{10,... | collective-permute-start | bytes 98312 | tf_op jit(solution)/shard_map/ppermute | solution.py:34
  8.5 0.6 %collective-permute-start.5 = (f32[64,128]{1,0:T(8,128)S(1)}, f32[64,128]{1,0:T(8,128)S(1)}, u32[]{:S(2)}, u32[]{:S(2)}) collective-permute-start(f32[64,128]{1,0:T(8,128)S(1)} %strain.1), channel_id=1, source_target_pairs={{0,4},{1,5},{2,6},{3,7},{4,0},{5,1},{6,2},{7,3},{8,12},{9,13},{10,... | collective-permute-start | bytes 98312 | tf_op jit(solution)/shard_map/ppermute | solution.py:34
  9.1 2.7 %collective-permute-done.7.refs_2_.refs_5_ = f32[64,128]{1,0:T(8,128)S(1)} collective-permute-done((f32[64,128]{1,0:T(8,128)S(1)}, f32[64,128]{1,0:T(8,128)S(1)}, u32[]{:S(2)}, u32[]{:S(2)}) %collective-permute-start.7) | collective-permute-done | bytes 32800 | tf_op jit(solution)/shard_map/ppermute | solution.py:34
  11.8 0.6 %collective-permute-done.5.refs_0_.refs_3_ = f32[64,128]{1,0:T(8,128)S(1)} collective-permute-done((f32[64,128]{1,0:T(8,128)S(1)}, f32[64,128]{1,0:T(8,128)S(1)}, u32[]{:S(2)}, u32[]{:S(2)}) %collective-permute-start.5) | collective-permute-done | bytes 32800 | tf_op jit(solution)/shard_map/ppermute | solution.py:34
  12.5 0.0 copy-start.5
  12.5 1.1 %gather.1 = (f32[6,4,16,128]{3,2,1,0:T(8,128)S(1)}, f32[40,128]{1,0:T(8,128)S(1)}, f32[40,128]{1,0:T(8,128)S(1)}, bf16[384,192]{1,0:T(8,128)(2,1)S(1)}, f32[8,128]{1,0:T(8,128)S(1)}) custom-call(f32[64,128]{1,0:T(8,128)S(1)} %collective-permute-done.5.refs_0_.refs_3_, f32[64,128]{1,0:T(8,128)S(1)} %collective-permute-done.6.refs_1_.refs_4_, ...), custom_call_target="tpu_custom_call" | custom-call | tf_op jit(solution)/shard_map/gather/pallas_call | solution.py:108
  13.6 0.1 collective-permute-start.8
  13.7 2.1 %collective-permute-start.9 = (f32[40,128]{1,0:T(8,128)S(1)}, f32[40,128]{1,0:T(8,128)S(1)}, u32[]{:S(2)}, u32[]{:S(2)}) collective-permute-start(f32[40,128]{1,0:T(8,128)S(1)} %get-tuple-element.25), channel_id=1, source_target_pairs={{0,1},{1,0},{2,3},{3,2},{4,5},{5,4},{6,7},{7,6},{8,9},{9,8},{10,11... | collective-permute-start | bytes 61448 | tf_op jit(solution)/shard_map/ppermute | solution.py:34
  15.8 0.2 collective-permute-start.10
  16.0 1.6 %collective-permute-done.9.refs_2_ = f32[40,128]{1,0:T(8,128)S(1)} collective-permute-done((f32[40,128]{1,0:T(8,128)S(1)}, f32[40,128]{1,0:T(8,128)S(1)}, u32[]{:S(2)}, u32[]{:S(2)}) %collective-permute-start.9) | collective-permute-done | bytes 20512 | tf_op jit(solution)/shard_map/ppermute | solution.py:34
  17.6 0.5 %collective-permute-start.12 = (f32[40,128]{1,0:T(8,128)S(1)}, f32[40,128]{1,0:T(8,128)S(1)}, u32[]{:S(2)}, u32[]{:S(2)}) collective-permute-start(f32[40,128]{1,0:T(8,128)S(1)} %collective-permute-done.10.refs_3_), channel_id=1, source_target_pairs={{0,4},{1,5},{2,6},{3,7},{4,0},{5,1},{6,2},{7,3},{8,12},{9,13},{10,... | collective-permute-start | bytes 61448 | tf_op jit(solution)/shard_map/ppermute | solution.py:34
  18.1 0.7 %collective-permute-done.11.refs_4_ = f32[40,128]{1,0:T(8,128)S(1)} collective-permute-done((f32[40,128]{1,0:T(8,128)S(1)}, f32[40,128]{1,0:T(8,128)S(1)}, u32[]{:S(2)}, u32[]{:S(2)}) %collective-permute-start.11) | collective-permute-done | bytes 20512 | tf_op jit(solution)/shard_map/ppermute | solution.py:34
  18.8 0.2 collective-permute-done.12.refs_5_
  18.9 0.1 flow.1
  19.0 2.1 %collective-permute-start.15 = (f32[64,128]{1,0:T(8,128)S(1)}, f32[64,128]{1,0:T(8,128)S(1)}, u32[]{:S(2)}, u32[]{:S(2)}) collective-permute-start(f32[64,128]{1,0:T(8,128)S(1)} %get-tuple-element.27), channel_id=1, source_target_pairs={{0,24},{1,25},{2,26},{3,27},{4,28},{5,29},{6,30},{7,31},{8,12},{9,... | collective-permute-start | bytes 98312 | tf_op jit(solution)/shard_map/ppermute | solution.py:34
  21.1 0.5 %collective-permute-start.14 = (f32[64,128]{1,0:T(8,128)S(1)}, f32[64,128]{1,0:T(8,128)S(1)}, u32[]{:S(2)}, u32[]{:S(2)}) collective-permute-start(f32[64,128]{1,0:T(8,128)S(1)} %get-tuple-element.27), channel_id=1, source_target_pairs={{0,4},{1,5},{2,6},{3,7},{4,0},{5,1},{6,2},{7,3},{8,24},{9,25},{10,... | collective-permute-start | bytes 98312 | tf_op jit(solution)/shard_map/ppermute | solution.py:34
  21.6 0.7 %collective-permute-start.13 = (f32[64,128]{1,0:T(8,128)S(1)}, f32[64,128]{1,0:T(8,128)S(1)}, u32[]{:S(2)}, u32[]{:S(2)}) collective-permute-start(f32[64,128]{1,0:T(8,128)S(1)} %get-tuple-element.27), channel_id=1, source_target_pairs={{0,4},{1,5},{2,6},{3,7},{4,0},{5,1},{6,2},{7,3},{8,12},{9,13},{10,... | collective-permute-start | bytes 98312 | tf_op jit(solution)/shard_map/ppermute | solution.py:34
  22.3 1.6 %collective-permute-done.15.refs_2_ = f32[64,128]{1,0:T(8,128)S(1)} collective-permute-done((f32[64,128]{1,0:T(8,128)S(1)}, f32[64,128]{1,0:T(8,128)S(1)}, u32[]{:S(2)}, u32[]{:S(2)}) %collective-permute-start.15) | collective-permute-done | bytes 32800 | tf_op jit(solution)/shard_map/ppermute | solution.py:34
  23.9 1.1 %collective-permute-done.14.refs_1_ = f32[64,128]{1,0:T(8,128)S(1)} collective-permute-done((f32[64,128]{1,0:T(8,128)S(1)}, f32[64,128]{1,0:T(8,128)S(1)}, u32[]{:S(2)}, u32[]{:S(2)}) %collective-permute-start.14) | collective-permute-done | bytes 32800 | tf_op jit(solution)/shard_map/ppermute | solution.py:34
  25.0 0.5 %collective-permute-done.13.refs_0_ = f32[64,128]{1,0:T(8,128)S(1)} collective-permute-done((f32[64,128]{1,0:T(8,128)S(1)}, f32[64,128]{1,0:T(8,128)S(1)}, u32[]{:S(2)}, u32[]{:S(2)}) %collective-permute-start.13) | collective-permute-done | bytes 32800 | tf_op jit(solution)/shard_map/ppermute | solution.py:34
  25.5 0.1 collective-permute-start.16
  25.6 2.9 %collective-permute-start.17 = (f32[8,128]{1,0:T(8,128)S(1)}, f32[8,128]{1,0:T(8,128)S(1)}, u32[]{:S(2)}, u32[]{:S(2)}) collective-permute-start(f32[8,128]{1,0:T(8,128)S(1)} %get-tuple-element.29), channel_id=1, source_target_pairs={{0,1},{1,0},{2,3},{3,2},{4,5},{5,4},{6,7},{7,6},{8,9},{9,8},{10,11... | collective-permute-start | bytes 12296 | tf_op jit(solution)/shard_map/ppermute | solution.py:34
  28.5 0.2 collective-permute-start.18
  28.6 1.4 %collective-permute-done.17.refs_2_ = f32[8,128]{1,0:T(8,128)S(1)} collective-permute-done((f32[8,128]{1,0:T(8,128)S(1)}, f32[8,128]{1,0:T(8,128)S(1)}, u32[]{:S(2)}, u32[]{:S(2)}) %collective-permute-start.17) | collective-permute-done | bytes 4128 | tf_op jit(solution)/shard_map/ppermute | solution.py:34
  30.1 0.5 %collective-permute-start.20 = (f32[8,128]{1,0:T(8,128)S(1)}, f32[8,128]{1,0:T(8,128)S(1)}, u32[]{:S(2)}, u32[]{:S(2)}) collective-permute-start(f32[8,128]{1,0:T(8,128)S(1)} %collective-permute-done.18.refs_3_), channel_id=1, source_target_pairs={{0,4},{1,5},{2,6},{3,7},{4,0},{5,1},{6,2},{7,3},{8,12},{9,13},{10,... | collective-permute-start | bytes 12296 | tf_op jit(solution)/shard_map/ppermute | solution.py:34
  30.6 0.7 %collective-permute-done.19.refs_4_ = f32[8,128]{1,0:T(8,128)S(1)} collective-permute-done((f32[8,128]{1,0:T(8,128)S(1)}, f32[8,128]{1,0:T(8,128)S(1)}, u32[]{:S(2)}, u32[]{:S(2)}) %collective-permute-start.19) | collective-permute-done | bytes 4128 | tf_op jit(solution)/shard_map/ppermute | solution.py:34
  31.2 0.2 collective-permute-done.20.refs_5_
  31.4 1.7 %krylov.1 = (f32[3,4,16,128]{3,2,1,0:T(8,128)S(1)}, f32[3,4,16,128]{3,2,1,0:T(8,128)S(1)}, f32[16,128]{1,0:T(8,128)S(1)}) custom-call(f32[1,4,16,128]{3,2,1,0:T(8,128)S(1)} %get-tuple-element.28.refs_0_, f32[1,4,16,128]{3,2,1,0:T(8,128)S(1)} %collective-permute-done.16.refs_1_, f32[8,128]{1,0:T(8,128)S(1)} %collective-permute-done.17.refs_2_, ...), custom_call_target="tpu_custom_call" | custom-call | tf_op jit(solution)/shard_map/krylov/pallas_call | solution.py:108
  33.1 0.4 collective-permute-start.21
  33.4 0.8 %collective-permute-done.21 = f32[16,128]{1,0:T(8,128)S(1)} collective-permute-done((f32[16,128]{1,0:T(8,128)S(1)}, f32[16,128]{1,0:T(8,128)S(1)}, u32[]{:S(2)}, u32[]{:S(2)}) %collective-permute-start.21) | collective-permute-done | bytes 8224 | tf_op jit(solution)/shard_map/ppermute | solution.py:34
  34.2 3.3 %collective-permute-start.24 = (f32[16,128]{1,0:T(8,128)S(1)}, f32[16,128]{1,0:T(8,128)S(1)}, u32[]{:S(2)}, u32[]{:S(2)}) collective-permute-start(f32[16,128]{1,0:T(8,128)S(1)} %add.3.refs_0_), channel_id=1, source_target_pairs={{0,3},{1,2},{2,1},{3,0},{4,7},{5,6},{6,5},{7,4},{8,11},{9,10},{10,... | collective-permute-start | bytes 24584 | tf_op jit(solution)/shard_map/ppermute | solution.py:34
  37.5 0.4 collective-permute-start.23
  37.9 0.7 %collective-permute-start.22 = (f32[16,128]{1,0:T(8,128)S(1)}, f32[16,128]{1,0:T(8,128)S(1)}, u32[]{:S(2)}, u32[]{:S(2)}) collective-permute-start(f32[16,128]{1,0:T(8,128)S(1)} %add.3.refs_0_), channel_id=1, source_target_pairs={{0,1},{1,0},{2,3},{3,2},{4,5},{5,4},{6,7},{7,6},{8,9},{9,8},{10,11... | collective-permute-start | bytes 24584 | tf_op jit(solution)/shard_map/ppermute | solution.py:34
  38.6 1.1 %collective-permute-done.24.refs_3_ = f32[16,128]{1,0:T(8,128)S(1)} collective-permute-done((f32[16,128]{1,0:T(8,128)S(1)}, f32[16,128]{1,0:T(8,128)S(1)}, u32[]{:S(2)}, u32[]{:S(2)}) %collective-permute-start.24) | collective-permute-done | bytes 8224 | tf_op jit(solution)/shard_map/ppermute | solution.py:34
  39.7 2.4 %collective-permute-done.23.refs_2_ = f32[16,128]{1,0:T(8,128)S(1)} collective-permute-done((f32[16,128]{1,0:T(8,128)S(1)}, f32[16,128]{1,0:T(8,128)S(1)}, u32[]{:S(2)}, u32[]{:S(2)}) %collective-permute-start.23) | collective-permute-done | bytes 8224 | tf_op jit(solution)/shard_map/ppermute | solution.py:34
  42.1 0.7 %final.1 = (f32[4,16,128]{2,1,0:T(8,128)}, f32[3,4,16,128]{3,2,1,0:T(8,128)}) custom-call(f32[16,128]{1,0:T(8,128)S(1)} %add.3.refs_0_, f32[16,128]{1,0:T(8,128)S(1)} %collective-permute-done.22.refs_1_, f32[16,128]{1,0:T(8,128)S(1)} %collective-permute-done.23.refs_2_, f32[16,128]{1,0:T(8,128)S(1)} %collective-permute-done.24.refs_3_, ...), custom_call_target="tpu_custom_call" | custom-call | tf_op jit(solution)/shard_map/final/pallas_call | solution.py:108
  (33 shorter events, 0.1 us)
Async XLA Ops:
  0.6 5.3 %copy-start = (s32[1,4,16,128]{3,2,1,0:T(8,128)S(1)}, s32[1,4,16,128]{3,2,1,0:T(8,128)}, u32[]{:S(2)}) copy-start(s32[1,4,16,128]{3,2,1,0:T(8,128)} %param.18) | copy-start | bytes 98308
  1.7 5.1 %collective-permute-start = (f32[4,4,16,128]{3,2,1,0:T(8,128)S(1)}, f32[4,4,16,128]{3,2,1,0:T(8,128)S(1)}, u32[]{:S(2)}, u32[]{:S(2)}) collective-permute-start(f32[4,4,16,128]{3,2,1,0:T(8,128)S(1)} %get-tuple-element.21.refs_0_.refs_10_), channel_id=1, source_target_pairs={{0,4},{1,5},{2,6},{3,7},{4,0},{5,1},{6,2},{7,3},{8,12},{9,13},{10,... | collective-permute-start | bytes 393224 | tf_op jit(solution)/shard_map/ppermute | solution.py:34
  1.7 3.7 %collective-permute-start.1 = (f32[16,128]{1,0:T(8,128)S(1)}, f32[16,128]{1,0:T(8,128)S(1)}, u32[]{:S(2)}, u32[]{:S(2)}) collective-permute-start(f32[16,128]{1,0:T(8,128)S(1)} %get-tuple-element.22), channel_id=1, source_target_pairs={{0,8},{1,9},{2,10},{3,11},{4,12},{5,13},{6,14},{7,15},{8,0},{9,1},... | collective-permute-start | bytes 24584 | tf_op jit(solution)/shard_map/ppermute | solution.py:34
  3.4 3.4 %copy-start.2 = (s32[1,4,16,128]{3,2,1,0:T(8,128)S(1)}, s32[1,4,16,128]{3,2,1,0:T(8,128)}, u32[]{:S(2)}) copy-start(s32[1,4,16,128]{3,2,1,0:T(8,128)} %param.22) | copy-start | bytes 98308
  3.4 2.1 %collective-permute-start.2 = (f32[16,128]{1,0:T(8,128)S(1)}, f32[16,128]{1,0:T(8,128)S(1)}, u32[]{:S(2)}, u32[]{:S(2)}) collective-permute-start(f32[16,128]{1,0:T(8,128)S(1)} %get-tuple-element.23), channel_id=1, source_target_pairs={{0,4},{1,5},{2,6},{3,7},{4,0},{5,1},{6,2},{7,3},{8,16},{9,17},{10,... | collective-permute-start | bytes 24584 | tf_op jit(solution)/shard_map/ppermute | solution.py:34
  5.4 1.2 %collective-permute-start.3 = (f32[16,128]{1,0:T(8,128)S(1)}, f32[16,128]{1,0:T(8,128)S(1)}, u32[]{:S(2)}, u32[]{:S(2)}) collective-permute-start(f32[16,128]{1,0:T(8,128)S(1)} %collective-permute-done.1.refs_2_.refs_12_), channel_id=1, source_target_pairs={{0,4},{1,5},{2,6},{3,7},{4,0},{5,1},{6,2},{7,3},{8,12},{9,13},{10,... | collective-permute-start | bytes 24584 | tf_op jit(solution)/shard_map/ppermute | solution.py:34
  5.5 1.3 %collective-permute-start.4 = (f32[16,128]{1,0:T(8,128)S(1)}, f32[16,128]{1,0:T(8,128)S(1)}, u32[]{:S(2)}, u32[]{:S(2)}) collective-permute-start(f32[16,128]{1,0:T(8,128)S(1)} %collective-permute-done.2.refs_3_.refs_13_), channel_id=1, source_target_pairs={{0,4},{1,5},{2,6},{3,7},{4,0},{5,1},{6,2},{7,3},{8,12},{9,13},{10,... | collective-permute-start | bytes 24584 | tf_op jit(solution)/shard_map/ppermute | solution.py:34
  6.0 6.5 %copy-start.3 = (f32[1,4,16,128]{3,2,1,0:T(8,128)S(1)}, f32[1,4,16,128]{3,2,1,0:T(8,128)}, u32[]{:S(2)}) copy-start(f32[1,4,16,128]{3,2,1,0:T(8,128)} %param.14) | copy-start | bytes 98308
  6.0 6.5 %copy-start.4 = (s32[1,4,16,128]{3,2,1,0:T(8,128)S(1)}, s32[1,4,16,128]{3,2,1,0:T(8,128)}, u32[]{:S(2)}) copy-start(s32[1,4,16,128]{3,2,1,0:T(8,128)} %param.15) | copy-start | bytes 98308
  6.0 6.5 %copy-start.6 = (f32[1,4,16,128]{3,2,1,0:T(8,128)S(1)}, f32[1,4,16,128]{3,2,1,0:T(8,128)}, u32[]{:S(2)}) copy-start(f32[1,4,16,128]{3,2,1,0:T(8,128)} %param.12) | copy-start | bytes 98308
  6.0 6.5 %copy-start.7 = (f32[1,4,16,128]{3,2,1,0:T(8,128)S(1)}, f32[1,4,16,128]{3,2,1,0:T(8,128)}, u32[]{:S(2)}) copy-start(f32[1,4,16,128]{3,2,1,0:T(8,128)} %param.13) | copy-start | bytes 98308
  6.0 6.5 %copy-start.8 = (f32[1,3,4,16,128]{4,3,2,1,0:T(8,128)S(1)}, f32[1,3,4,16,128]{4,3,2,1,0:T(8,128)}, u32[]{:S(2)}) copy-start(f32[1,3,4,16,128]{4,3,2,1,0:T(8,128)} %param.20) | copy-start | bytes 294916
  6.0 6.5 %copy-start.10 = (f32[24,24]{1,0:T(8,128)S(1)}, f32[24,24]{1,0:T(8,128)}, u32[]{:S(2)}) copy-start(f32[24,24]{1,0:T(8,128)} %refs_9_.1) | copy-start | bytes 6916
  6.9 4.9 %collective-permute-start.7 = (f32[64,128]{1,0:T(8,128)S(1)}, f32[64,128]{1,0:T(8,128)S(1)}, u32[]{:S(2)}, u32[]{:S(2)}) collective-permute-start(f32[64,128]{1,0:T(8,128)S(1)} %strain.1), channel_id=1, source_target_pairs={{0,24},{1,25},{2,26},{3,27},{4,28},{5,29},{6,30},{7,31},{8,12},{9,... | collective-permute-start | bytes 98312 | tf_op jit(solution)/shard_map/ppermute | solution.py:34
  7.0 4.8 %collective-permute-start.6 = (f32[64,128]{1,0:T(8,128)S(1)}, f32[64,128]{1,0:T(8,128)S(1)}, u32[]{:S(2)}, u32[]{:S(2)}) collective-permute-start(f32[64,128]{1,0:T(8,128)S(1)} %strain.1), channel_id=1, source_target_pairs={{0,4},{1,5},{2,6},{3,7},{4,0},{5,1},{6,2},{7,3},{8,24},{9,25},{10,... | collective-permute-start | bytes 98312 | tf_op jit(solution)/shard_map/ppermute | solution.py:34
  8.5 3.9 %collective-permute-start.5 = (f32[64,128]{1,0:T(8,128)S(1)}, f32[64,128]{1,0:T(8,128)S(1)}, u32[]{:S(2)}, u32[]{:S(2)}) collective-permute-start(f32[64,128]{1,0:T(8,128)S(1)} %strain.1), channel_id=1, source_target_pairs={{0,4},{1,5},{2,6},{3,7},{4,0},{5,1},{6,2},{7,3},{8,12},{9,13},{10,... | collective-permute-start | bytes 98312 | tf_op jit(solution)/shard_map/ppermute | solution.py:34
  12.5 6.5 %copy-start.5 = (f32[1,8,4,16,128]{4,3,2,1,0:T(8,128)S(1)}, f32[1,8,4,16,128]{4,3,2,1,0:T(8,128)}, u32[]{:S(2)}) copy-start(f32[1,8,4,16,128]{4,3,2,1,0:T(8,128)} %param.17) | copy-start | bytes 786436
  12.5 6.4 %copy-start.9 = (s32[1,4,16,128]{3,2,1,0:T(8,128)S(1)}, s32[1,4,16,128]{3,2,1,0:T(8,128)}, u32[]{:S(2)}) copy-start(s32[1,4,16,128]{3,2,1,0:T(8,128)} %param.16) | copy-start | bytes 98308
  13.6 5.3 %collective-permute-start.8 = (f32[6,4,16,128]{3,2,1,0:T(8,128)S(1)}, f32[6,4,16,128]{3,2,1,0:T(8,128)S(1)}, u32[]{:S(2)}, u32[]{:S(2)}) collective-permute-start(f32[6,4,16,128]{3,2,1,0:T(8,128)S(1)} %get-tuple-element.24.refs_0_), channel_id=1, source_target_pairs={{0,4},{1,5},{2,6},{3,7},{4,0},{5,1},{6,2},{7,3},{8,12},{9,13},{10,... | collective-permute-start | bytes 589832 | tf_op jit(solution)/shard_map/ppermute | solution.py:34
  13.7 3.8 %collective-permute-start.9 = (f32[40,128]{1,0:T(8,128)S(1)}, f32[40,128]{1,0:T(8,128)S(1)}, u32[]{:S(2)}, u32[]{:S(2)}) collective-permute-start(f32[40,128]{1,0:T(8,128)S(1)} %get-tuple-element.25), channel_id=1, source_target_pairs={{0,1},{1,0},{2,3},{3,2},{4,5},{5,4},{6,7},{7,6},{8,9},{9,8},{10,11... | collective-permute-start | bytes 61448 | tf_op jit(solution)/shard_map/ppermute | solution.py:34
  15.8 1.8 %collective-permute-start.10 = (f32[40,128]{1,0:T(8,128)S(1)}, f32[40,128]{1,0:T(8,128)S(1)}, u32[]{:S(2)}, u32[]{:S(2)}) collective-permute-start(f32[40,128]{1,0:T(8,128)S(1)} %get-tuple-element.26), channel_id=1, source_target_pairs={{0,4},{1,2},{2,1},{3,7},{4,0},{5,6},{6,5},{7,3},{8,12},{9,10},{10,... | collective-permute-start | bytes 61448 | tf_op jit(solution)/shard_map/ppermute | solution.py:34
  17.6 1.2 %collective-permute-start.11 = (f32[40,128]{1,0:T(8,128)S(1)}, f32[40,128]{1,0:T(8,128)S(1)}, u32[]{:S(2)}, u32[]{:S(2)}) collective-permute-start(f32[40,128]{1,0:T(8,128)S(1)} %collective-permute-done.9.refs_2_), channel_id=1, source_target_pairs={{0,4},{1,5},{2,6},{3,7},{4,0},{5,1},{6,2},{7,3},{8,12},{9,13},{10,... | collective-permute-start | bytes 61448 | tf_op jit(solution)/shard_map/ppermute | solution.py:34
  17.6 1.4 %collective-permute-start.12 = (f32[40,128]{1,0:T(8,128)S(1)}, f32[40,128]{1,0:T(8,128)S(1)}, u32[]{:S(2)}, u32[]{:S(2)}) collective-permute-start(f32[40,128]{1,0:T(8,128)S(1)} %collective-permute-done.10.refs_3_), channel_id=1, source_target_pairs={{0,4},{1,5},{2,6},{3,7},{4,0},{5,1},{6,2},{7,3},{8,12},{9,13},{10,... | collective-permute-start | bytes 61448 | tf_op jit(solution)/shard_map/ppermute | solution.py:34
  19.0 4.9 %collective-permute-start.15 = (f32[64,128]{1,0:T(8,128)S(1)}, f32[64,128]{1,0:T(8,128)S(1)}, u32[]{:S(2)}, u32[]{:S(2)}) collective-permute-start(f32[64,128]{1,0:T(8,128)S(1)} %get-tuple-element.27), channel_id=1, source_target_pairs={{0,24},{1,25},{2,26},{3,27},{4,28},{5,29},{6,30},{7,31},{8,12},{9,... | collective-permute-start | bytes 98312 | tf_op jit(solution)/shard_map/ppermute | solution.py:34
  21.1 3.9 %collective-permute-start.14 = (f32[64,128]{1,0:T(8,128)S(1)}, f32[64,128]{1,0:T(8,128)S(1)}, u32[]{:S(2)}, u32[]{:S(2)}) collective-permute-start(f32[64,128]{1,0:T(8,128)S(1)} %get-tuple-element.27), channel_id=1, source_target_pairs={{0,4},{1,5},{2,6},{3,7},{4,0},{5,1},{6,2},{7,3},{8,24},{9,25},{10,... | collective-permute-start | bytes 98312 | tf_op jit(solution)/shard_map/ppermute | solution.py:34
  21.6 3.9 %collective-permute-start.13 = (f32[64,128]{1,0:T(8,128)S(1)}, f32[64,128]{1,0:T(8,128)S(1)}, u32[]{:S(2)}, u32[]{:S(2)}) collective-permute-start(f32[64,128]{1,0:T(8,128)S(1)} %get-tuple-element.27), channel_id=1, source_target_pairs={{0,4},{1,5},{2,6},{3,7},{4,0},{5,1},{6,2},{7,3},{8,12},{9,13},{10,... | collective-permute-start | bytes 98312 | tf_op jit(solution)/shard_map/ppermute | solution.py:34
  25.5 5.9 %collective-permute-start.16 = (f32[1,4,16,128]{3,2,1,0:T(8,128)S(1)}, f32[1,4,16,128]{3,2,1,0:T(8,128)S(1)}, u32[]{:S(2)}, u32[]{:S(2)}) collective-permute-start(f32[1,4,16,128]{3,2,1,0:T(8,128)S(1)} %get-tuple-element.28.refs_0_), channel_id=1, source_target_pairs={{0,4},{1,5},{2,6},{3,7},{4,0},{5,1},{6,2},{7,3},{8,12},{9,13},{10,... | collective-permute-start | bytes 98312 | tf_op jit(solution)/shard_map/ppermute | solution.py:34
  25.6 4.4 %collective-permute-start.17 = (f32[8,128]{1,0:T(8,128)S(1)}, f32[8,128]{1,0:T(8,128)S(1)}, u32[]{:S(2)}, u32[]{:S(2)}) collective-permute-start(f32[8,128]{1,0:T(8,128)S(1)} %get-tuple-element.29), channel_id=1, source_target_pairs={{0,1},{1,0},{2,3},{3,2},{4,5},{5,4},{6,7},{7,6},{8,9},{9,8},{10,11... | collective-permute-start | bytes 12296 | tf_op jit(solution)/shard_map/ppermute | solution.py:34
  28.5 1.6 %collective-permute-start.18 = (f32[8,128]{1,0:T(8,128)S(1)}, f32[8,128]{1,0:T(8,128)S(1)}, u32[]{:S(2)}, u32[]{:S(2)}) collective-permute-start(f32[8,128]{1,0:T(8,128)S(1)} %get-tuple-element.30), channel_id=1, source_target_pairs={{0,4},{1,2},{2,1},{3,7},{4,0},{5,6},{6,5},{7,3},{8,12},{9,10},{10,... | collective-permute-start | bytes 12296 | tf_op jit(solution)/shard_map/ppermute | solution.py:34
  30.1 1.2 %collective-permute-start.19 = (f32[8,128]{1,0:T(8,128)S(1)}, f32[8,128]{1,0:T(8,128)S(1)}, u32[]{:S(2)}, u32[]{:S(2)}) collective-permute-start(f32[8,128]{1,0:T(8,128)S(1)} %collective-permute-done.17.refs_2_), channel_id=1, source_target_pairs={{0,4},{1,5},{2,6},{3,7},{4,0},{5,1},{6,2},{7,3},{8,12},{9,13},{10,... | collective-permute-start | bytes 12296 | tf_op jit(solution)/shard_map/ppermute | solution.py:34
  30.1 1.3 %collective-permute-start.20 = (f32[8,128]{1,0:T(8,128)S(1)}, f32[8,128]{1,0:T(8,128)S(1)}, u32[]{:S(2)}, u32[]{:S(2)}) collective-permute-start(f32[8,128]{1,0:T(8,128)S(1)} %collective-permute-done.18.refs_3_), channel_id=1, source_target_pairs={{0,4},{1,5},{2,6},{3,7},{4,0},{5,1},{6,2},{7,3},{8,12},{9,13},{10,... | collective-permute-start | bytes 12296 | tf_op jit(solution)/shard_map/ppermute | solution.py:34
  31.4 10.7 %copy-start.1 = (f32[1,3,4,16,128]{4,3,2,1,0:T(8,128)S(1)}, f32[1,3,4,16,128]{4,3,2,1,0:T(8,128)}, u32[]{:S(2)}) copy-start(f32[1,3,4,16,128]{4,3,2,1,0:T(8,128)} %param.19) | copy-start | bytes 294916
  33.1 1.2 %collective-permute-start.21 = (f32[16,128]{1,0:T(8,128)S(1)}, f32[16,128]{1,0:T(8,128)S(1)}, u32[]{:S(2)}, u32[]{:S(2)}) collective-permute-start(f32[16,128]{1,0:T(8,128)S(1)} %get-tuple-element.34.refs_4_), channel_id=1, source_target_pairs={{0,4},{1,5},{2,6},{3,7},{4,0},{5,1},{6,2},{7,3},{8,12},{9,13},{10,... | collective-permute-start | bytes 24584 | tf_op jit(solution)/shard_map/ppermute | solution.py:34
  34.2 5.4 %collective-permute-start.24 = (f32[16,128]{1,0:T(8,128)S(1)}, f32[16,128]{1,0:T(8,128)S(1)}, u32[]{:S(2)}, u32[]{:S(2)}) collective-permute-start(f32[16,128]{1,0:T(8,128)S(1)} %add.3.refs_0_), channel_id=1, source_target_pairs={{0,3},{1,2},{2,1},{3,0},{4,7},{5,6},{6,5},{7,4},{8,11},{9,10},{10,... | collective-permute-start | bytes 24584 | tf_op jit(solution)/shard_map/ppermute | solution.py:34
  37.5 4.5 %collective-permute-start.23 = (f32[16,128]{1,0:T(8,128)S(1)}, f32[16,128]{1,0:T(8,128)S(1)}, u32[]{:S(2)}, u32[]{:S(2)}) collective-permute-start(f32[16,128]{1,0:T(8,128)S(1)} %add.3.refs_0_), channel_id=1, source_target_pairs={{0,2},{1,3},{2,0},{3,1},{4,6},{5,7},{6,4},{7,5},{8,10},{9,11},{10,... | collective-permute-start | bytes 24584 | tf_op jit(solution)/shard_map/ppermute | solution.py:34
  37.9 4.2 %collective-permute-start.22 = (f32[16,128]{1,0:T(8,128)S(1)}, f32[16,128]{1,0:T(8,128)S(1)}, u32[]{:S(2)}, u32[]{:S(2)}) collective-permute-start(f32[16,128]{1,0:T(8,128)S(1)} %add.3.refs_0_), channel_id=1, source_target_pairs={{0,1},{1,0},{2,3},{3,2},{4,5},{5,4},{6,7},{7,6},{8,9},{9,8},{10,11... | collective-permute-start | bytes 24584 | tf_op jit(solution)/shard_map/ppermute | solution.py:34
